TPU v7x, 128 devices: a whole 4x4x4 slice. The times are simulated.
128 devices in a mesh: member: 8 (over y, core), dp: 16 (over z, x).
Axes of the slice: x: 4, y: 4, z: 4, core: 2. Of those that a mesh axis runs over, the one named last changes fastest.
Arguments:
- observations: bfloat16 [4096, 1152], P(('member', 'dp')), may hold values from -6 to 6
- rollout: bfloat16 [4096, 384], P(('member', 'dp')), as said below
- done_flags: int32 [4096, 24], P(('member', 'dp')), may hold values 0 or 1
- member_ids: int32 [4096, 1], P(('member', 'dp')), may hold values from 0 to 15; in each aligned block of 32 rows (0 to 31, 32 to 63, ...) at most 6 rows name the same one
- embed_weight: float32 [16, 48, 256], P('member'), may hold values from -0.875 to 0.875
- conv_weight: float32 [16, 3, 2, 256, 256], P('member'), may hold values from -0.25 to 0.25
- trunk_in: float32 [16, 256, 512], P('member'), may hold values from -0.375 to 0.375
- trunk_mid: float32 [16, 512, 512], P('member'), may hold values from -0.25 to 0.25
- head_weight: float32 [16, 512, 13], P('member'), may hold values from -0.15625 to 0.15625
- log_std: float32 [16, 12], P('member'), may hold values from -0.1 to 0.1
Outputs:
- embed_dir: float32 [16, 48, 256], P('member', 'dp')
- conv_dir: float32 [16, 3, 2, 256, 256], P('member', None, None, 'dp')
- in_dir: float32 [16, 256, 512], P('member', 'dp')
- mid_dir: float32 [16, 512, 512], P('member', 'dp')
- head_dir: float32 [16, 512, 13], P('member', 'dp')
- std_dir: float32 [16, 12], P('member')
Inputs may be any that keep to these rules, and one draw needn't show every extreme that they name: `member_ids`: in each shard's 32 rows no member is named more than 6 times, a bound that some block reaches. `rollout`: per step: 12 action values, reward, old value, next value, old log-probability.
All inputs are finite; a program needn't handle non-finite values. No bound on the sum of `done_flags` on one device may be relied on, other than what follows from the above.
Results may differ from a plain program's by a relative error of at most 0.023.
Values may be sent and summed in bfloat16 or wider, within the bound.
No kernel may reach another device: no remote copies, remote signals or barrier semaphores. Data moves between devices by JAX's collectives and lax.ppermute only.
A program may use at most 128 MiB of HBM per device.

v0:
```python
from functools import partial
import math

import jax
import jax.numpy as jnp
from jax import lax
from jax.sharding import PartitionSpec as P

gamma_rate = 0.99
trace_rate = 0.95
penalty_weight = 0.5
value_weight = 0.5
half_log_tau = 0.9189385332046727


def advantages(reward, old_value, next_value, done_mask):
    alive = 1.0 - done_mask
    td_error = reward + gamma_rate * alive * next_value - old_value
    step_count = td_error.shape[1]
    running = td_error[:, step_count - 1]
    columns = [running]
    for step_index in range(step_count - 2, -1, -1):
        running = td_error[:, step_index] + gamma_rate * trace_rate * alive[:, step_index] * running
        columns.append(running)
    advantage = jnp.stack(columns[::-1], axis=1)
    return (advantage, advantage + old_value)


def policy_loss(weights, observations, rollout, done_mask, live_mask):
    embedding, conv_stack, trunk_first, trunk_second, head_mat, log_scale = weights
    row_count, step_count = done_mask.shape
    channels = embedding.shape[1]
    action_count = log_scale.shape[0]
    features = observations.reshape(row_count * step_count, embedding.shape[0])
    hidden = jnp.dot(features, embedding.astype(jnp.bfloat16), preferred_element_type=jnp.float32)
    for conv_layer in range(conv_stack.shape[0]):
        dilation = 2**conv_layer
        current = hidden.astype(jnp.bfloat16)
        shaped = current.reshape(row_count, step_count, channels)
        earlier = jnp.pad(shaped[:, : step_count - dilation], ((0, 0), (dilation, 0), (0, 0)))
        earlier = earlier.reshape(row_count * step_count, channels)
        mixing = jnp.dot(
            current,
            conv_stack[conv_layer, 0].astype(jnp.bfloat16),
            preferred_element_type=jnp.float32,
        )
        mixing = mixing + jnp.dot(
            earlier,
            conv_stack[conv_layer, 1].astype(jnp.bfloat16),
            preferred_element_type=jnp.float32,
        )
        hidden = hidden + jax.nn.elu(mixing)
    trunk_input = hidden.astype(jnp.bfloat16)
    first_units = jax.nn.elu(
        jnp.dot(trunk_input, trunk_first.astype(jnp.bfloat16), preferred_element_type=jnp.float32)
    ).astype(jnp.bfloat16)
    second = jax.nn.elu(
        jnp.dot(first_units, trunk_second.astype(jnp.bfloat16), preferred_element_type=jnp.float32)
    ).astype(jnp.bfloat16)
    head_out = jnp.dot(second, head_mat.astype(jnp.bfloat16), preferred_element_type=jnp.float32)
    action_mean = head_out[:, :action_count]
    value_pred = head_out[:, action_count]
    record = rollout.astype(jnp.float32).reshape(row_count, step_count, -1)
    action = record[:, :, :action_count].reshape(row_count * step_count, action_count)
    advantage, target_value = advantages(
        record[:, :, action_count],
        record[:, :, action_count + 1],
        record[:, :, action_count + 2],
        done_mask,
    )
    old_logp = record[:, :, action_count + 3].reshape(-1)
    scaled = (action - action_mean) * jnp.exp(-log_scale)
    log_prob = jnp.sum(-0.5 * scaled * scaled - log_scale, axis=1) - action_count * half_log_tau
    log_ratio = log_prob - old_logp
    prob_ratio = jnp.exp(log_ratio)
    value_gap = value_pred - target_value.reshape(-1)
    per_step = (
        -prob_ratio * advantage.reshape(-1)
        + penalty_weight * (prob_ratio - 1.0 - log_ratio)
        + 0.5 * value_weight * value_gap * value_gap
    )
    weight = (live_mask[:, None] * jnp.ones((1, step_count), jnp.float32)).reshape(-1)
    return jnp.sum(per_step * weight)


def member_grad(weights, observations, rollout, done_mask, live_mask):
    total_loss, pullback = jax.vjp(
        partial(
            policy_loss,
            observations=observations,
            rollout=rollout,
            done_mask=done_mask,
            live_mask=live_mask,
        ),
        weights,
    )
    return pullback(jnp.ones((), jnp.float32))[0]


def local(
    observations,
    rollout,
    done_flags,
    member_ids,
    embed_weight,
    conv_weight,
    trunk_in,
    trunk_mid,
    head_weight,
    log_std,
):
    groups = lax.axis_size("member")
    per_group = embed_weight.shape[0]
    members = groups * per_group
    local_rows = observations.shape[0]
    capacity = 3 * local_rows // members
    owner_ids = member_ids[:, 0]
    onehot = (owner_ids[:, None] == jnp.arange(members, dtype=jnp.int32)[None, :]).astype(jnp.int32)
    before = jnp.cumsum(onehot, axis=0) - onehot
    ranking = jnp.sum(before * onehot, axis=1)
    target = owner_ids * capacity + ranking
    dispatch = (jnp.arange(members * capacity, dtype=jnp.int32)[:, None] == target[None, :]).astype(
        jnp.bfloat16
    )

    def scatter_rows(values):
        placed = jnp.dot(dispatch, values, preferred_element_type=jnp.float32).astype(jnp.bfloat16)
        return placed.reshape(groups, per_group, capacity, values.shape[1])

    sent_obs = scatter_rows(observations)
    sent_record = scatter_rows(rollout)
    sent_done = scatter_rows(done_flags.astype(jnp.bfloat16))
    sent_live = (
        jnp.sum(dispatch.astype(jnp.float32), axis=1)
        .astype(jnp.bfloat16)
        .reshape(groups, per_group, capacity)
    )
    recv_obs, recv_record, recv_done, recv_live = (
        lax.all_to_all(sent_obs, "member", split_axis=0, concat_axis=2, tiled=True),
        lax.all_to_all(sent_record, "member", split_axis=0, concat_axis=2, tiled=True),
        lax.all_to_all(sent_done, "member", split_axis=0, concat_axis=2, tiled=True),
        lax.all_to_all(sent_live, "member", split_axis=0, concat_axis=2, tiled=True),
    )
    gradients = []
    for member in range(per_group):
        weights = (
            embed_weight[member],
            conv_weight[member],
            trunk_in[member],
            trunk_mid[member],
            head_weight[member],
            log_std[member],
        )
        gradients.append(
            member_grad(
                weights,
                recv_obs[0, member],
                recv_record[0, member],
                recv_done[0, member].astype(jnp.float32),
                recv_live[0, member].astype(jnp.float32),
            )
        )
    grad_embed = jnp.stack([grad_set[0] for grad_set in gradients])
    grad_conv = jnp.stack([grad_set[1] for grad_set in gradients])
    grad_first = jnp.stack([grad_set[2] for grad_set in gradients])
    grad_second = jnp.stack([grad_set[3] for grad_set in gradients])
    grad_head = jnp.stack([grad_set[4] for grad_set in gradients])
    grad_scale = jnp.stack([grad_set[5] for grad_set in gradients])
    entries = sum(
        (
            math.prod(tensor.shape[1:])
            for tensor in (embed_weight, conv_weight, trunk_in, trunk_mid, head_weight, log_std)
        )
    )
    share_dims = (1, 3, 1, 1, 1)
    shards = lax.axis_size("dp")
    shard_index = lax.axis_index("dp")
    summed = (
        lax.psum(grad_embed.astype(jnp.bfloat16), "dp").astype(jnp.float32),
        lax.psum(grad_conv.astype(jnp.bfloat16), "dp").astype(jnp.float32),
        lax.psum(grad_first.astype(jnp.bfloat16), "dp").astype(jnp.float32),
        lax.psum(grad_second.astype(jnp.bfloat16), "dp").astype(jnp.float32),
        lax.psum(grad_head.astype(jnp.bfloat16), "dp").astype(jnp.float32),
        lax.psum(grad_scale.astype(jnp.bfloat16), "dp").astype(jnp.float32),
    )
    squares = sum(
        (
            jnp.sum(grad_part * grad_part, axis=tuple(range(1, grad_part.ndim)))
            for grad_part in summed
        )
    )
    shares = [
        lax.dynamic_slice_in_dim(
            grad_part,
            shard_index * (grad_part.shape[share_dim] // shards),
            grad_part.shape[share_dim] // shards,
            share_dim,
        )
        for grad_part, share_dim in zip(summed[:5], share_dims)
    ]
    std_grad = summed[5]
    root_mean = jnp.sqrt(squares / entries + 1e-06)
    outputs = tuple(
        (grad_part / root_mean.reshape((-1,) + (1,) * (grad_part.ndim - 1)) for grad_part in shares)
    )
    return outputs + (std_grad / root_mean[:, None],)


def solution(mesh):
    placed = (
        P(("member", "dp"), None),
        P(("member", "dp"), None),
        P(("member", "dp"), None),
        P(("member", "dp"), None),
        P("member", None, None),
        P("member", None, None, None, None),
        P("member", None, None),
        P("member", None, None),
        P("member", None, None),
        P("member", None),
    )
    return jax.shard_map(
        local,
        mesh=mesh,
        in_specs=placed,
        out_specs=(
            P("member", "dp", None),
            P("member", None, None, "dp", None),
            P("member", "dp", None),
            P("member", "dp", None),
            P("member", "dp", None),
            P("member", None),
        ),
        check_vma=False,
    )
```

profile of v0, /device:TPU:0, one launch (start us, length us, event | category | flops | bytes accessed | tf_op | source)
XLA Modules:
  0.0 374.6 jit_solution(405467127866470752)
XLA Ops:
  10.3 4.6 %all-to-all-start.3 = ((bf16[8,2,6]{2,1,0:T(2,128)(2,1)}), bf16[8,2,6]{2,1,0:T(2,128)(2,1)S(1)}, u32[]{:S(2)}, u32[]{:S(2)}) async-start(bf16[8,2,6]{2,1,0:T(2,128)(2,1)} %reshape.324), calls=%async_computation.3 | async-start | bytes 8192 | tf_op jit(solution)/shard_map/all_to_all | solution.py:142
  23.4 2.2 slice_bitcast_fusion.1
  27.8 4.8 %all-to-all-start.2 = ((bf16[8,2,144]{2,1,0:T(2,128)(2,1)}), bf16[8,2,144]{2,1,0:T(2,128)(2,1)S(1)}, u32[]{:S(2)}, u32[]{:S(2)}) async-start(bf16[8,2,144]{2,1,0:T(2,128)(2,1)} %reshape.359), calls=%async_computation.2 | async-start | bytes 16384 | tf_op jit(solution)/shard_map/all_to_all | solution.py:141
  36.3 1.6 all-to-all-done.2
  37.9 3.4 all-to-all-start.1
  41.6 5.2 %all-to-all-done.1 = bf16[8,2,6,384]{3,1,2,0:T(2,128)(2,1)S(1)} async-done(((bf16[8,2,6,384]{3,1,2,0:T(2,128)(2,1)}), bf16[8,2,6,384]{3,1,2,0:T(2,128)(2,1)S(1)}, u32[]{:S(2)}, u32[]{:S(2)}) %all-to-all-start.1) | async-done | bytes 73760 | tf_op jit(solution)/shard_map/all_to_all | solution.py:140
  46.8 3.4 all-to-all-start
  63.2 2.2 fusion.77
  68.9 1.7 fusion.234
  73.8 2.5 fusion.49
  85.2 4.5 %fusion.42 = (bf16[1152,256]{1,0:T(8,128)(2,1)S(1)}, f32[1152,256]{1,0:T(8,128)}) fusion(f32[1152,256]{1,0:T(8,128)} %get-tuple-element.135, f32[1152,256]{1,0:T(8,128)S(1)} %get-tuple-element.131, f32[1152,256]{1,0:T(8,128)S(1)} %get-tuple-element.133, f32[1152,256]{1,0:T(8,128)} %fusion.89, bf16[1152,256]{1,0:T(8,128)(2,1)} %bitcast.344, ...), kind=kOutput, calls=%fused_computation.99 | convolution fusion | flops 155123712 | bytes 7208960 | tf_op jit(solution)/shard_map/jvp()/dot_general | solution.py:47
  96.8 2.0 add_reduce_fusion
  100.4 1.6 multiply_reduce_fusion.4
  102.9 3.4 fusion.69
  106.3 2.0 select_add_fusion.1
  108.6 1.6 multiply_reduce_fusion.5
  111.0 2.8 fusion.68
  115.5 2.2 fusion.34
  126.4 2.3 fusion.35
  159.2 3.2 fusion.66
  163.9 2.4 fusion.67
  167.6 2.2 pad_maximum_fusion.1
  174.0 84.9 %all-reduce.33.cloned.1.call-done = (bf16[2,48,256]{2,1,0:T(8,128)(2,1)}, bf16[2,12]{1,0:T(2,128)(2,1)}, bf16[2,512,13]{1,2,0:T(8,128)(2,1)}) async-done(((bf16[2,48,256]{2,1,0:T(8,128)(2,1)}, bf16[2,12]{1,0:T(2,128)(2,1)}, bf16[2,512,13]{1,2,0:T(8,128)(2,1)}), (bf16[2,48,256]{2,1,0:T(8,128)(2,1)}, bf16[2,12]{1,0:T(2,128)(2,1)}, bf16[2,512,13]{1,2,0:T(8,128)(2,1)})) %all-reduce.33.cloned.1.call-update) | async-done | bytes 75840 | tf_op jit(solution)/shard_map/psum | solution.py:179
  262.9 94.8 %all-reduce.35.cloned.1.call-done = (bf16[2,512,512]{2,1,0:T(8,128)(2,1)}, bf16[2,256,512]{2,1,0:T(8,128)(2,1)}, bf16[2,3,2,256,256]{4,3,2,1,0:T(8,128)(2,1)}) async-done(((bf16[2,512,512]{2,1,0:T(8,128)(2,1)}, bf16[2,256,512]{2,1,0:T(8,128)(2,1)}, bf16[2,3,2,256,256]{4,3,2,1,0:T(8,128)(2,1)}), (bf16[2,512,512]{2,1,0:T(8,128)(2,1)}, bf16[2,256,512]{2,1,0:T(8,128)(2,1)}, ...) | async-done | bytes 3145744 | tf_op jit(solution)/shard_map/psum | solution.py:182
  (413 shorter events, 116.0 us)
Async XLA Ops:
  7.2 14.9 %copy-start = (bf16[32,1152]{1,0:T(8,128)(2,1)S(1)}, bf16[32,1152]{1,0:T(8,128)(2,1)}, u32[]{:S(2)}) copy-start(bf16[32,1152]{1,0:T(8,128)(2,1)} %param.10) | copy-start | bytes 221188
  10.3 17.5 %all-to-all-start.3 = ((bf16[8,2,6]{2,1,0:T(2,128)(2,1)}), bf16[8,2,6]{2,1,0:T(2,128)(2,1)S(1)}, u32[]{:S(2)}, u32[]{:S(2)}) async-start(bf16[8,2,6]{2,1,0:T(2,128)(2,1)} %reshape.324), calls=%async_computation.3 | async-start | bytes 8192 | tf_op jit(solution)/shard_map/all_to_all | solution.py:142
  16.2 64.4 %copy-start.94 = (f32[12]{0:T(128)}, f32[12]{0:T(128)S(1)}, u32[]{:S(2)}) copy-start(f32[12]{0:T(128)S(1)} %get-tuple-element.120) | copy-start | bytes 148
  25.6 34.6 %copy-start.25 = (bf16[3,2,256,256]{3,2,1,0:T(8,128)(2,1)}, bf16[3,2,256,256]{3,2,1,0:T(8,128)(2,1)S(1)}, u32[]{:S(2)}) copy-start(bf16[3,2,256,256]{3,2,1,0:T(8,128)(2,1)S(1)} %get-tuple-element.99) | copy-start | bytes 2359300
  25.6 42.8 %copy-start.22 = (bf16[3,2,256,256]{3,2,1,0:T(8,128)(2,1)}, bf16[3,2,256,256]{3,2,1,0:T(8,128)(2,1)S(1)}, u32[]{:S(2)}) copy-start(bf16[3,2,256,256]{3,2,1,0:T(8,128)(2,1)S(1)} %get-tuple-element.98) | copy-start | bytes 2359300
  27.8 10.1 %all-to-all-start.2 = ((bf16[8,2,144]{2,1,0:T(2,128)(2,1)}), bf16[8,2,144]{2,1,0:T(2,128)(2,1)S(1)}, u32[]{:S(2)}, u32[]{:S(2)}) async-start(bf16[8,2,144]{2,1,0:T(2,128)(2,1)} %reshape.359), calls=%async_computation.2 | async-start | bytes 16384 | tf_op jit(solution)/shard_map/all_to_all | solution.py:141
  33.2 8.2 %copy-start.96 = (f32[48]{0:T(128)}, f32[48]{0:T(128)S(1)}, u32[]{:S(2)}) copy-start(f32[48]{0:T(128)S(1)} %get-tuple-element.126) | copy-start | bytes 580
  33.2 8.2 %copy-start.97 = (f32[48]{0:T(128)}, f32[48]{0:T(128)S(1)}, u32[]{:S(2)}) copy-start(f32[48]{0:T(128)S(1)} %get-tuple-element.127) | copy-start | bytes 580
  33.2 8.2 %copy-start.98 = (f32[48]{0:T(128)}, f32[48]{0:T(128)S(1)}, u32[]{:S(2)}) copy-start(f32[48]{0:T(128)S(1)} %get-tuple-element.128) | copy-start | bytes 580
  33.2 8.2 %copy-start.99 = (f32[48]{0:T(128)}, f32[48]{0:T(128)S(1)}, u32[]{:S(2)}) copy-start(f32[48]{0:T(128)S(1)} %get-tuple-element.129) | copy-start | bytes 580
  37.9 8.9 %all-to-all-start.1 = ((bf16[8,2,6,384]{3,1,2,0:T(2,128)(2,1)}), bf16[8,2,6,384]{3,1,2,0:T(2,128)(2,1)S(1)}, u32[]{:S(2)}, u32[]{:S(2)}) async-start(bf16[8,2,6,384]{3,1,2,0:T(2,128)(2,1)} %copy.131), calls=%async_computation.1 | async-start | bytes 147456 | tf_op jit(solution)/shard_map/all_to_all | solution.py:140
  46.8 11.4 %all-to-all-start = ((bf16[8,2,6,1152]{3,1,2,0:T(2,128)(2,1)}), bf16[8,2,6,1152]{3,1,2,0:T(2,128)(2,1)S(1)}, u32[]{:S(2)}, u32[]{:S(2)}) async-start(bf16[8,2,6,1152]{3,1,2,0:T(2,128)(2,1)} %copy.129), calls=%async_computation | async-start | bytes 442368 | tf_op jit(solution)/shard_map/all_to_all | solution.py:139
  50.3 208.6 %all-reduce.33.cloned.1.call-start = ((), (), s32[]{:S(2)}) async-start(), calls=%async_computation.4 | async-start | bytes 164864 | tf_op jit(solution)/shard_map/psum | solution.py:179
  51.3 6.9 %copy-start.77 = (f32[48,24]{0,1:T(8,128)}, f32[48,24]{0,1:T(8,128)S(1)}, u32[]{:S(2)}) copy-start(f32[48,24]{0,1:T(8,128)S(1)} %stack.59) | copy-start | bytes 13828
  53.8 5.4 %copy-start.79 = (f32[48,24,1]{0,2,1:T(1,128)}, f32[48,24,1]{0,2,1:T(1,128)S(1)}, u32[]{:S(2)}) copy-start(f32[48,24,1]{0,2,1:T(1,128)S(1)} %get-tuple-element.104) | copy-start | bytes 13828
  54.0 5.2 %copy-start.81 = (f32[48,24]{0,1:T(8,128)}, f32[48,24]{0,1:T(8,128)S(1)}, u32[]{:S(2)}) copy-start(f32[48,24]{0,1:T(8,128)S(1)} %stack.56) | copy-start | bytes 13828
  59.5 8.3 %copy-start.50 = (bf16[1152,48]{1,0:T(8,128)(2,1)}, bf16[1152,48]{1,0:T(8,128)(2,1)S(1)}, u32[]{:S(2)}) copy-start(bf16[1152,48]{1,0:T(8,128)(2,1)S(1)} %reshape_squeeze.6) | copy-start | bytes 331780
  85.2 4.5 %copy-start.16 = (bf16[2,256,512]{2,1,0:T(8,128)(2,1)S(1)}, bf16[2,256,512]{2,1,0:T(8,128)(2,1)}, u32[]{:S(2)}) copy-start(bf16[2,256,512]{2,1,0:T(8,128)(2,1)} %convert.95) | copy-start | bytes 1572868
  92.5 4.3 %copy-start.78 = (f32[48,24]{0,1:T(8,128)S(1)}, f32[48,24]{0,1:T(8,128)}, u32[]{:S(2)}) copy-start(f32[48,24]{0,1:T(8,128)} %copy-done.77) | copy-start | bytes 13828
  92.5 4.3 %copy-start.80 = (f32[48,24,1]{0,2,1:T(1,128)S(1)}, f32[48,24,1]{0,2,1:T(1,128)}, u32[]{:S(2)}) copy-start(f32[48,24,1]{0,2,1:T(1,128)} %copy-done.79) | copy-start | bytes 13828
  92.6 4.3 %copy-start.82 = (f32[48,24]{0,1:T(8,128)S(1)}, f32[48,24]{0,1:T(8,128)}, u32[]{:S(2)}) copy-start(f32[48,24]{0,1:T(8,128)} %copy-done.81) | copy-start | bytes 13828
  106.3 3.9 %copy-start.92 = (f32[1152,1]{0,1:T(1,128)S(1)}, f32[1152,1]{0,1:T(1,128)}, u32[]{:S(2)}) copy-start(f32[1152,1]{0,1:T(1,128)} %reshape.325) | copy-start | bytes 13828
  173.0 184.7 %all-reduce.35.cloned.1.call-start = ((), (), s32[]{:S(2)}) async-start(), calls=%async_computation.5 | async-start | bytes 6291456 | tf_op jit(solution)/shard_map/psum | solution.py:182
  362.6 4.9 %copy-start.1 = (bf16[32,1152]{1,0:T(8,128)(2,1)S(1)}, bf16[32,1152]{1,0:T(8,128)(2,1)}, u32[]{:S(2)}) copy-start(bf16[32,1152]{1,0:T(8,128)(2,1)} %param.10) | copy-start | bytes 221188
  (95 other events, 168.8 us)
Sparse Core Ops, SparseCore 0:
  173.2 85.6 all-reduce.32
  262.5 95.1 all-reduce.34
where the time goes:
time: 380 us; the launch traced here: 375 us
  waiting for transfers between devices  187 us (49%)
  matrix products  71.3 us (19%)
  local copies, waits for them, and re-layouts  49.7 us (13%)
  other arithmetic  33.2 us (9%)
  between operations  17.2 us (5%)
  starting transfers between devices  16.7 us (4%)
    psum x1, waiting for transfers between devices, local(): lax.psum(grad_second.astype(jnp.bfloat16), 'dp').astype(jnp.float32)  94.8 us
    psum x1, waiting for transfers between devices, local(): lax.psum(grad_embed.astype(jnp.bfloat16), 'dp').astype(jnp.float32)  84.9 us
    dot_general x18, matrix products, policy_loss(): jnp.dot(earlier, conv_stack[conv_layer, 1].astype(jnp.bfloat16), preferre...  25 us
    unnamed x233, local copies, waits for them, and re-layouts  19.8 us
    dot_general x16, matrix products, policy_loss(): jnp.dot(current, conv_stack[conv_layer, 0].astype(jnp.bfloat16), preferre...  12.7 us
    dot_general x6, matrix products, policy_loss(): jnp.dot(second, head_mat.astype(jnp.bfloat16), preferred_element_type=jnp...  11.2 us
    dot_general x6, matrix products, policy_loss(): jnp.dot(first_units, trunk_second.astype(jnp.bfloat16), preferred_element...  9.45 us
  transfers between devices with their start and end apart: 6, of which 4 were waited for; matrix products, arithmetic and copies ran while one was open for 8% of the time, Pallas kernels for 0%

commit v1 on v0

v1 whole, which is shorter than its diff:
```python
import jax
import jax.numpy as jnp
from jax import lax
from jax.experimental import pallas as pl
from jax.experimental.pallas import tpu as pltpu
from jax.sharding import Mesh, PartitionSpec as P

gamma_rate = 0.99
trace_rate = 0.95
half_log_tau = 0.9189385332046727

OBS = 48
STEPS = 24
ACT = 12
CH = 256
UNITS = 512
MEMBERS = 16
CAP = 6
SLOT = 8
REC = 64
WIDTH = STEPS * REC
ENTRIES = 805388
SOURCES = 16
SPANS = SOURCES * CAP
CHUNK_STEPS = 8
CHUNKS = STEPS // CHUNK_STEPS
ROWS = CHUNK_STEPS * SPANS
ALL_ROWS = STEPS * SPANS
PAD = 4 * SPANS
SHARDS = 16
BLOCK = 208
FIRST_LANE = 3
f32 = jnp.float32
bf16 = jnp.bfloat16


def iota(shape, dim):
    return lax.broadcasted_iota(jnp.int32, shape, dim)


def dot(a, b):
    return jnp.dot(a, b, preferred_element_type=f32)


def dot_tn(a, b):
    return lax.dot_general(a, b, (((0,), (0,)), ((), ())), preferred_element_type=f32)


def dot_nt(a, b):
    return lax.dot_general(a, b, (((1,), (1,)), ((), ())), preferred_element_type=f32)


def onehot(cond):
    return jnp.where(cond, 1.0, 0.0).astype(bf16)


def pack_kernel(obs_ref, roll_ref, done_ref, ids_ref, out_ref):
    spans = obs_ref.shape[0]
    row, col = iota((STEPS * 16, 512), 0), iota((STEPS * 16, 512), 1)
    step = col & 127
    pick = onehot((row == 16 * step + 12 + (col >> 7)) & (step < STEPS))
    parts = dot(roll_ref[...], pick)
    reward, old_value = parts[:, 0:128], parts[:, 128:256]
    next_value, old_logp = parts[:, 256:384], parts[:, 384:512]
    widen = onehot(iota((STEPS, 128), 0) == iota((STEPS, 128), 1))
    done = dot(done_ref[...].astype(f32).astype(bf16), widen)
    lane = iota((spans, 128), 1)
    alive = jnp.where(lane < STEPS, 1.0 - done, 0.0)
    advantage = reward + gamma_rate * alive * next_value - old_value
    carry = gamma_rate * trace_rate * alive
    for shift in (1, 2, 4, 8, 16):
        advantage = advantage + carry * pltpu.roll(advantage, 128 - shift, 1)
        carry = carry * pltpu.roll(carry, 128 - shift, 1)
    target = jnp.where(lane < STEPS, advantage + old_value, 0.0)
    advantage = jnp.where(lane < STEPS, advantage, 0.0)
    scalars = jnp.concatenate([target.astype(bf16), advantage.astype(bf16), old_logp.astype(bf16)], axis=1)

    col = iota((384, 512), 1)
    row = iota((384, 512), 0)
    spot, within = col & 63, col >> 6
    place_obs = onehot((row == 48 * within + spot) & (spot < 48))
    place_act = onehot((row == 16 * within + spot - 48) & (spot >= 48) & (spot < 60))[0:128]
    live = jnp.where((iota((spans, 512), 1) & 63) == 63, 1.0, 0.0)
    groups = []
    for g in range(3):
        place_scal = onehot((spot >= 60) & (spot < 63) & (row == (spot - 60) * 128 + 8 * g + within))
        placed = dot(obs_ref[:, 384 * g : 384 * g + 384], place_obs)
        placed = placed + dot(roll_ref[:, 128 * g : 128 * g + 128], place_act)
        placed = placed + dot(scalars, place_scal) + live
        groups.append(placed.astype(bf16))

    ids = ids_ref[...]
    named = (lane == ids).astype(f32)
    lower = onehot(iota((spans, spans), 0) > iota((spans, spans), 1))
    before = dot(lower, named.astype(bf16))
    rank = jnp.sum(before * named, axis=1, keepdims=True)
    slot = ids * SLOT + rank.astype(jnp.int32)
    dispatch = onehot(lane == slot)
    for g in range(3):
        out_ref[:, 512 * g : 512 * g + 512] = dot_tn(dispatch, groups[g]).astype(bf16)


def pack(observations, rollout, done_flags, member_ids):
    return pl.pallas_call(
        pack_kernel,
        out_shape=jax.ShapeDtypeStruct((MEMBERS * SLOT, WIDTH), bf16),
        name="pack",
    )(observations, rollout, done_flags, member_ids)


def weights_kernel(which_ref, embed_ref, conv_ref, in_ref, mid_ref, head_ref, embed_out, conv_out, in_out, mid_out, head_out):
    row, col = iota((128, 256), 0), iota((128, 256), 1)
    embed = embed_ref[0].astype(bf16)
    r, k = iota((128, OBS), 0), iota((128, OBS), 1)
    for half in range(2):
        spread = onehot(r == k + REC * half)
        embed_out[:, 256 * half : 256 * half + 256] = dot(spread, embed).astype(bf16)
    even = (row - 48 == col - FIRST_LANE) & (row >= 48) & (row < 64)
    odd = (row - 112 == col - 128 - FIRST_LANE) & (row >= 112)
    embed_out[:, 512:768] = onehot(even | odd)
    for layer in range(3):
        for tap in range(2):
            conv_out[2 * layer + tap] = conv_ref[0, layer, tap].astype(bf16)
    in_out[...] = in_ref[0].astype(bf16)
    mid_out[...] = mid_ref[0].astype(bf16)
    a, lane = iota((ACT + 1, 128), 0), iota((ACT + 1, 128), 1)
    head_out[...] = dot(head_ref[0].astype(bf16), onehot(a + FIRST_LANE == lane)).astype(bf16)


def prepare(which, embed, conv, trunk_in, trunk_mid, head):
    def one(shape):
        return pl.BlockSpec((1,) + shape, lambda i, w: (w[0],) + (0,) * len(shape))

    def whole(shape):
        return pl.BlockSpec(shape, lambda i, w: (0,) * len(shape))

    outs = ((128, 768), (6, CH, CH), (CH, UNITS), (UNITS, UNITS), (UNITS, 128))
    return pl.pallas_call(
        weights_kernel,
        grid_spec=pltpu.PrefetchScalarGridSpec(
            num_scalar_prefetch=1,
            grid=(1,),
            in_specs=[one(x.shape[1:]) for x in (embed, conv, trunk_in, trunk_mid, head)],
            out_specs=[whole(s) for s in outs],
        ),
        out_shape=[jax.ShapeDtypeStruct(s, bf16) for s in outs],
        cost_estimate=pl.CostEstimate(flops=0, bytes_accessed=5_000_000, transcendentals=0),
        name="weights",
    )(which, embed, conv, trunk_in, trunk_mid, head)


def grad_kernel(
    recv_ref, embed_ref, conv_ref, in_ref, mid_ref, head_ref, scale_ref,
    send_ref, stat_ref,
    xc, hid, rec, c0, c1, c2, c3, g0, g1, g2, first, second, dout, dp2, dp1, dhid, dm0, dm1, dm2, dpair,
    acc_conv, acc_in, acc_mid, acc_head,
):
    cs, gs, dms = (c0, c1, c2), (g0, g1, g2), (dm0, dm1, dm2)
    for ref in cs:
        ref[0:PAD, :] = jnp.zeros((PAD, CH), bf16)
    for ref in dms:
        ref[ALL_ROWS : ALL_ROWS + PAD, :] = jnp.zeros((PAD, CH), bf16)
    acc_conv[...] = jnp.zeros_like(acc_conv)
    acc_in[...] = jnp.zeros_like(acc_in)
    acc_mid[...] = jnp.zeros_like(acc_mid)
    acc_head[...] = jnp.zeros_like(acc_head)
    stat_ref[...] = jnp.zeros_like(stat_ref)

    r, k = iota((SPANS, SOURCES * SLOT), 0), iota((SPANS, SOURCES * SLOT), 1)
    compact = onehot(((k & 7) < CAP) & (r == (k >> 3) * CAP + (k & 7)))
    lane1 = iota((1, 128), 1)
    is_act = (lane1 >= FIRST_LANE) & (lane1 < FIRST_LANE + ACT)
    log_scale = scale_ref[0:1, :]
    inverse = jnp.where(is_act, jnp.exp(-log_scale), 0.0)
    offset = jnp.sum(jnp.where(is_act, log_scale, 0.0), axis=1, keepdims=True) + ACT * half_log_tau

    @pl.loop(0, CHUNKS)
    def _(i):
        base = i * ROWS
        for p in range(CHUNK_STEPS // 2):
            pair = i * (CHUNK_STEPS // 2) + p
            x = recv_ref[:, pl.ds(pl.multiple_of(pair * 128, 128), 128)]
            x = dot(compact, x).astype(bf16)
            xc[pl.ds(pl.multiple_of(pair * SPANS, 16), SPANS), :] = x
            y = dot(x, embed_ref[...])
            for half in range(2):
                at = (2 * p + half) * SPANS
                h = y[:, 256 * half : 256 * half + 256]
                hid[at : at + SPANS, :] = h
                c0[pl.ds(pl.multiple_of(base + PAD + at, 16), SPANS), :] = h.astype(bf16)
                rec[at : at + SPANS, :] = y[:, 512 + 128 * half : 640 + 128 * half]
        for layer in range(3):
            c, g = cs[layer], gs[layer]
            lag = SPANS * 2**layer
            mix = dot(c[pl.ds(pl.multiple_of(base + PAD, 16), ROWS), :], conv_ref[2 * layer])
            mix = mix + dot(c[pl.ds(pl.multiple_of(base + PAD - lag, 16), ROWS), :], conv_ref[2 * layer + 1])
            grown = jnp.exp(jnp.minimum(mix, 0.0))
            h = hid[...] + jnp.where(mix > 0, mix, grown - 1.0)
            g[pl.ds(pl.multiple_of(base, 16), ROWS), :] = grown.astype(bf16)
            if layer < 2:
                hid[...] = h
                cs[layer + 1][pl.ds(pl.multiple_of(base + PAD, 16), ROWS), :] = h.astype(bf16)
            else:
                c3[...] = h.astype(bf16)

        def elu(x):
            return jnp.where(x > 0, x, jnp.exp(jnp.minimum(x, 0.0)) - 1.0).astype(bf16)

        def slope(y):
            return jnp.minimum(y.astype(f32), 0.0) + 1.0

        for n in range(0, UNITS, 256):
            first[:, n : n + 256] = elu(dot(c3[...], in_ref[:, n : n + 256]))
        for n in range(0, UNITS, 256):
            second[:, n : n + 256] = elu(dot(first[...], mid_ref[:, n : n + 256]))
        out = dot(second[...], head_ref[...])
        record = rec[...]
        diff = record - out
        scaled = diff * inverse
        square = scaled * scaled
        advantage = record[:, FIRST_LANE + 13 : FIRST_LANE + 14]
        old_logp = record[:, FIRST_LANE + 14 : FIRST_LANE + 15]
        live = record[:, FIRST_LANE + 15 : FIRST_LANE + 16]
        log_ratio = -0.5 * jnp.sum(square, axis=1, keepdims=True) - offset - old_logp
        ratio = jnp.exp(log_ratio)
        dlog = live * (0.5 * (ratio - 1.0) - ratio * advantage)
        dvalue = -0.5 * live * diff
        d = jnp.where(lane1 == FIRST_LANE + ACT, dvalue, dlog * scaled * inverse)
        dout[...] = d.astype(bf16)
        stat_ref[0:1, :] += jnp.where(is_act, jnp.sum(dlog * (square - 1.0), axis=0, keepdims=True), 0.0)
        for n in range(0, UNITS, 256):
            ds = dot_nt(dout[...], head_ref[n : n + 256, :])
            dp2[:, n : n + 256] = (ds * slope(second[:, n : n + 256])).astype(bf16)
        for n in range(0, UNITS, 256):
            df = dot_nt(dp2[...], mid_ref[n : n + 256, :])
            dp1[:, n : n + 256] = (df * slope(first[:, n : n + 256])).astype(bf16)
        dhid[pl.ds(pl.multiple_of(base, 16), ROWS), :] = dot_nt(dp1[...], in_ref[...])
        acc_head[...] += dot_tn(dout[...], second[...])
        for n in range(0, UNITS, 256):
            acc_mid[n : n + 256, :] += dot_tn(first[:, n : n + 256], dp2[...])
        acc_in[...] += dot_tn(c3[...], dp1[...])

    @pl.loop(0, CHUNKS)
    def _(j):
        i = CHUNKS - 1 - j
        base = i * ROWS
        here = pl.ds(pl.multiple_of(base, 16), ROWS)
        for layer in (2, 1, 0):
            c, g, dm = cs[layer], gs[layer], dms[layer]
            lag = SPANS * 2**layer
            dh = dhid[here, :]
            dm[here, :] = (dh * g[here, :].astype(f32)).astype(bf16)
            dc = dot_nt(dm[here, :], conv_ref[2 * layer])
            dc = dc + dot_nt(dm[pl.ds(pl.multiple_of(base + lag, 16), ROWS), :], conv_ref[2 * layer + 1])
            dh = dh + dc
            if layer > 0:
                dhid[here, :] = dh
            else:
                for s in range(CHUNK_STEPS):
                    at = pl.ds(pl.multiple_of(i * (ROWS // 2) + (s // 2) * SPANS, 16), SPANS)
                    dpair[at, 256 * (s % 2) : 256 * (s % 2) + 256] = dh[s * SPANS : s * SPANS + SPANS].astype(bf16)
            acc_conv[2 * layer] += dot_tn(c[pl.ds(pl.multiple_of(base + PAD, 16), ROWS), :], dm[here, :])
            acc_conv[2 * layer + 1] += dot_tn(c[pl.ds(pl.multiple_of(base + PAD - lag, 16), ROWS), :], dm[here, :])

    dembed = dot_tn(xc[...], dpair[...])
    dembed = (dembed[0:OBS, 0:256] + dembed[REC : REC + OBS, 256:512]).astype(bf16)
    r, k = iota((SHARDS * 16, OBS), 0), iota((SHARDS * 16, OBS), 1)
    spread = onehot(((r & 15) < 3) & (k == (r >> 4) * 3 + (r & 15)))
    extra = dot(spread, dembed).astype(bf16)
    dhead = acc_head[0:16, :]
    for s in range(SHARDS):
        for q in range(6):
            send_ref[s, 16 * q : 16 * q + 16, :] = acc_conv[q, 16 * s : 16 * s + 16, :].astype(bf16)
        for n in range(2):
            send_ref[s, 96 + 16 * n : 112 + 16 * n, :] = acc_in[16 * s : 16 * s + 16, 256 * n : 256 * n + 256].astype(bf16)
            send_ref[s, 128 + 32 * n : 160 + 32 * n, :] = acc_mid[32 * s : 32 * s + 32, 256 * n : 256 * n + 256].astype(bf16)
        send_ref[s, 192:208, :] = extra[16 * s : 16 * s + 16, :]
        moved = jnp.where(iota((16, 32), 0) >= FIRST_LANE, dhead[:, 32 * s : 32 * s + 32].astype(bf16).astype(f32), extra[16 * s : 16 * s + 16, 0:32].astype(f32))
        send_ref[s, 192:208, 0:32] = moved.astype(bf16)


def member_grad(recv, embed, conv, trunk_in, trunk_mid, head, scale):
    v = pltpu.VMEM
    half = ALL_ROWS // 2
    return pl.pallas_call(
        grad_kernel,
        out_shape=(
            jax.ShapeDtypeStruct((SHARDS, BLOCK, 256), bf16),
            jax.ShapeDtypeStruct((8, 128), f32),
        ),
        scratch_shapes=[
            v((half, 128), bf16), v((ROWS, CH), f32), v((ROWS, 128), f32),
            v((PAD + ALL_ROWS, CH), bf16), v((PAD + ALL_ROWS, CH), bf16), v((PAD + ALL_ROWS, CH), bf16),
            v((ROWS, CH), bf16),
            v((ALL_ROWS, CH), bf16), v((ALL_ROWS, CH), bf16), v((ALL_ROWS, CH), bf16),
            v((ROWS, UNITS), bf16), v((ROWS, UNITS), bf16), v((ROWS, 128), bf16),
            v((ROWS, UNITS), bf16), v((ROWS, UNITS), bf16),
            v((ALL_ROWS, CH), f32),
            v((ALL_ROWS + PAD, CH), bf16), v((ALL_ROWS + PAD, CH), bf16), v((ALL_ROWS + PAD, CH), bf16),
            v((half, 512), bf16),
            v((6, CH, CH), f32), v((CH, UNITS), f32), v((UNITS, UNITS), f32), v((128, UNITS), f32),
        ],
        cost_estimate=pl.CostEstimate(flops=11_200_000_000, bytes_accessed=4_000_000, transcendentals=4_000_000),
        compiler_params=pltpu.CompilerParams(vmem_limit_bytes=56 * 1024 * 1024),
        name="grad",
    )(recv, embed, conv, trunk_in, trunk_mid, head, scale)


def reduce_kernel(recv_ref, stat_ref, sum_ref, cast_ref):
    row, lane = iota((16, 256), 0), iota((16, 256), 1)
    ok = (row < FIRST_LANE) | (lane < 32)
    squares = []
    for member in range(2):
        total = recv_ref[member].astype(f32)
        for source in range(member + 2, SHARDS, 2):
            total = total + recv_ref[source].astype(f32)
        sum_ref[member] = total
        square = jnp.sum(total[0:192] * total[0:192]) + jnp.sum(jnp.where(ok, total[192:208] * total[192:208], 0.0))
        squares.append(square)
    lane1 = iota((1, 128), 1)
    line = jnp.where(lane1 == 0, squares[0], jnp.where(lane1 == 1, squares[1], 0.0)) + pltpu.roll(stat_ref[0:1, :], 32, 1)
    for s in range(SHARDS):
        cast_ref[8 * s : 8 * s + 8, :] = jnp.broadcast_to(line, (8, 128))


def reduce_parts(recv, stat):
    return pl.pallas_call(
        reduce_kernel,
        out_shape=(jax.ShapeDtypeStruct((2, BLOCK, 256), f32), jax.ShapeDtypeStruct((SHARDS * 8, 128), f32)),
        name="reduce",
    )(recv, stat)


def finish_kernel(sum_ref, cast_ref, embed_ref, conv_ref, in_ref, mid_ref, head_ref, std_ref):
    lines = [cast_ref[8 * s : 8 * s + 1, :] for s in range(SHARDS)]
    lane1 = iota((1, 128), 1)
    total = sum(lines[1:], lines[0])
    for member in range(2):
        mine = lines[member]
        for s in range(member + 2, SHARDS, 2):
            mine = mine + lines[s]
        lo = 32 + FIRST_LANE
        std = jnp.where((lane1 >= lo) & (lane1 < lo + ACT), mine, 0.0)
        square = jnp.sum(std * std, axis=1, keepdims=True) + total[:, member : member + 1]
        scale = 1.0 / jnp.sqrt(square / ENTRIES + 1e-06)
        std_ref[member : member + 1, :] = (std * scale)[:, lo : lo + ACT]
        part = sum_ref.at[member]
        for q in range(6):
            conv_ref[member, q // 2, q % 2] = part[16 * q : 16 * q + 16, :] * scale
        for n in range(2):
            in_ref[member, :, 256 * n : 256 * n + 256] = part[96 + 16 * n : 112 + 16 * n, :] * scale
            mid_ref[member, :, 256 * n : 256 * n + 256] = part[128 + 32 * n : 160 + 32 * n, :] * scale
        embed_ref[member] = part[192:195, :] * scale
        head = (part[192:208, 0:128] * scale).T
        head_ref[member] = head[0:32, FIRST_LANE:16]


def finish(sums, cast):
    shapes = ((2, 3, 256), (2, 3, 2, 16, 256), (2, 16, 512), (2, 32, 512), (2, 32, 13), (2, 12))
    return pl.pallas_call(
        finish_kernel,
        out_shape=tuple(jax.ShapeDtypeStruct(s, f32) for s in shapes),
        name="finish",
    )(sums, cast)


def local(observations, rollout, done_flags, member_ids, embed_weight, conv_weight, trunk_in, trunk_mid, head_weight, log_std):
    which = lax.axis_index("xl").astype(jnp.int32)
    packed = pack(observations, rollout, done_flags, member_ids)
    recv = lax.all_to_all(packed, ("member", "xl"), split_axis=0, concat_axis=0, tiled=True)
    prepared = prepare(which.reshape(1), embed_weight, conv_weight, trunk_in, trunk_mid, head_weight)
    scale = jnp.pad(lax.dynamic_index_in_dim(log_std, which, 0), ((0, 7), (FIRST_LANE, 128 - ACT - FIRST_LANE)))
    send, stat = member_grad(recv, *prepared, scale)
    parts = lax.all_to_all(send, ("z", "xh", "xl"), split_axis=0, concat_axis=0, tiled=True)
    sums, cast = reduce_parts(parts, stat)
    cast = lax.all_to_all(cast, ("z", "xh", "xl"), split_axis=0, concat_axis=0, tiled=True)
    return finish(sums, cast)


def solution(mesh):
    fine = Mesh(mesh.devices.reshape(8, 4, 2, 2), ("member", "z", "xh", "xl"))
    dp = ("z", "xh", "xl")
    every = ("member",) + dp
    return jax.shard_map(
        local,
        mesh=fine,
        in_specs=(P(every), P(every), P(every), P(every)) + (P("member"),) * 6,
        out_specs=(
            P("member", dp),
            P("member", None, None, dp),
            P("member", dp),
            P("member", dp),
            P("member", dp),
            P("member"),
        ),
        check_vma=False,
    )
```

time: 380 us -> 101 us (0.27); the launches traced: 375 us -> 99.9 us
  waiting for transfers between devices: 187 us -> 2.53 us
  matrix products: 71.3 us -> 0 us
  blocking collectives: 0 us -> 44.1 us
  local copies, waits for them, and re-layouts: 49.7 us -> 8.71 us
  Pallas kernels: 0 us -> 38.3 us
  other arithmetic: 33.2 us -> 0 us
  between operations: 17.2 us -> 0.66 us
  starting transfers between devices: 16.7 us -> 5.6 us
    psum x2 -> x0, waiting for transfers between devices: 180 us -> none  [the longest x1 94.8 us: local(): lax.psum(grad_second.astype(jnp.bfloat16), 'dp').astype(jnp.float32)]
    dot_general x59 -> x0, matrix products: 71.3 us -> none  [the longest x18 25 us: policy_loss(): jnp.dot(earlier, conv_stack[conv_layer, 1].astype(jnp.bfloat16), preferre...]
    all_to_all x0 -> x2, blocking collectives: none -> 44.1 us  [the longest x1 32.3 us: local(): lax.all_to_all(send, ('z', 'xh', 'xl'), split_axis=0, concat_axis=0, tile...]
    pallas_call x0 -> x5, Pallas kernels: none -> 38.3 us  [the longest x1 27.2 us: member_grad(): pl.pallas_call(grad_kernel, out_shape=(jax.ShapeDtypeStruct((SHARDS, BLOC...]
    unnamed x233 -> x7, local copies, waits for them, and re-layouts: 19.8 us -> 5.31 us
    reduce_sum x13 -> x0, other arithmetic: 11.2 us -> none  [the longest x6 4.84 us: local(): jnp.sum(grad_part * grad_part, axis=tuple(range(1, grad_part.ndim)))]
    all_to_all x4 -> x1, starting transfers between devices: 16.1 us -> 5.6 us  [local(): lax.all_to_all(packed, ('member', 'xl'), split_axis=0, concat_axis=0, til...]
    another operation x13 -> x0, other arithmetic: 9.3 us -> none
  transfers between devices with their start and end apart: 6 -> 1, of which waited for: 4 -> 1; matrix products, arithmetic and copies ran while one was open for 8% -> 2% of each run, Pallas kernels for 0% -> 3%
where the time goes in v1:
time: 101 us; the launch traced here: 99.9 us
  blocking collectives  44.1 us (44%)
  Pallas kernels  38.3 us (38%)
  local copies, waits for them, and re-layouts  8.71 us (9%)
  starting transfers between devices  5.6 us (6%)
  waiting for transfers between devices  2.53 us (3%)
    all_to_all x1, blocking collectives, local(): lax.all_to_all(send, ('z', 'xh', 'xl'), split_axis=0, concat_axis=0, tile...  32.3 us
    pallas_call x1, Pallas kernels, member_grad(): pl.pallas_call(grad_kernel, out_shape=(jax.ShapeDtypeStruct((SHARDS, BLOC...  27.2 us
    all_to_all x1, blocking collectives, local(): lax.all_to_all(cast, ('z', 'xh', 'xl'), split_axis=0, concat_axis=0, tile...  11.8 us
    all_to_all x1, starting transfers between devices, local(): lax.all_to_all(packed, ('member', 'xl'), split_axis=0, concat_axis=0, til...  5.6 us
    unnamed x7, local copies, waits for them, and re-layouts  5.31 us
    pallas_call x1, Pallas kernels, prepare(): pl.pallas_call(weights_kernel, grid_spec=pltpu.PrefetchScalarGridSpec(num...  3.35 us
    pallas_call x1, Pallas kernels, pack(): pl.pallas_call(pack_kernel, out_shape=jax.ShapeDtypeStruct((MEMBERS * SLO...  3.23 us
    pallas_call x2, local copies, waits for them, and re-layouts, finish(): pl.pallas_call(finish_kernel, out_shape=tuple((jax.ShapeDtypeStruct(s, f3...  2.73 us
  transfers between devices with their start and end apart: 1, of which 1 were waited for; matrix products, arithmetic and copies ran while one was open for 2% of the time, Pallas kernels for 3%

profile of v1, /device:TPU:0, one launch (start us, length us, event | category | flops | bytes accessed | tf_op | source)
XLA Modules:
  0.0 99.9 jit_solution(13503898439523141980)
XLA Ops:
  0.6 0.0 copy-start
  0.6 1.4 %copy.16.done_ref = s32[32,24]{1,0:T(8,128)} copy(s32[32,24]{0,1:T(8,128)} %param.12) | data formatting | bytes 6144 | tf_op args[2]
  2.0 1.3 %copy.17.ids_ref = s32[32,1]{1,0:T(8,128)} copy(s32[32,1]{0,1:T(1,128)} %param.13) | data formatting | bytes 256 | tf_op args[3]
  3.4 3.2 %pack.1 = bf16[128,1536]{1,0:T(8,128)(2,1)} custom-call(bf16[32,1152]{1,0:T(8,128)(2,1)} %obs_ref.1, bf16[32,384]{1,0:T(8,128)(2,1)} %roll_ref.1, s32[32,24]{1,0:T(8,128)} %copy.16.done_ref, s32[32,1]{1,0:T(8,128)} %copy.17.ids_ref), custom_call_target="tpu_custom_call" | custom-call | tf_op jit(solution)/shard_map/pack/pallas_call | solution.py:104
  6.6 5.6 %all-to-all-start = ((bf16[16,8,1536]{2,1,0:T(8,128)(2,1)}), bf16[16,8,1536]{2,1,0:T(8,128)(2,1)S(1)}, u32[]{:S(2)}, u32[]{:S(2)}) async-start(bf16[16,8,1536]{2,1,0:T(8,128)(2,1)} %bitcast.5), calls=%async_computation | async-start | bytes 786432 | tf_op jit(solution)/shard_map/all_to_all | solution.py:370
  12.2 1.8 %copy.18.head_ref = f32[2,512,13]{2,1,0:T(8,128)} copy(f32[2,512,13]{1,0,2:T(2,128)} %param.18) | data formatting | bytes 106496 | tf_op args[8]
  14.1 0.0 copy-done
  14.1 0.7 pad.4.scale_ref
  14.7 3.4 %weights.1 = (bf16[128,768]{1,0:T(8,128)(2,1)}, bf16[6,256,256]{2,1,0:T(8,128)(2,1)}, bf16[256,512]{1,0:T(8,128)(2,1)}, bf16[512,512]{1,0:T(8,128)(2,1)}, bf16[512,128]{1,0:T(8,128)(2,1)}) custom-call(s32[1]{0:T(128)} %bitcast.2.which_ref, f32[2,48,256]{2,1,0:T(8,128)} %embed_ref.1, f32[2,3,2,256,256]{4,3,2,1,0:T(8,128)} %conv_ref.1, f32[2,256,512]{2,1,0:T(8,128)} %in_ref.1, ...), custom_call_target="tpu_custom_call" | custom-call | bytes 5000000 | tf_op jit(solution)/shard_map/weights/pallas_call | solution.py:138
  18.1 2.5 %all-to-all-done = bf16[16,8,1536]{2,1,0:T(8,128)(2,1)S(1)} async-done(((bf16[16,8,1536]{2,1,0:T(8,128)(2,1)}), bf16[16,8,1536]{2,1,0:T(8,128)(2,1)S(1)}, u32[]{:S(2)}, u32[]{:S(2)}) %all-to-all-start) | async-done | bytes 393248 | tf_op jit(solution)/shard_map/all_to_all | solution.py:370
  20.6 0.0 copy-start.1
  20.6 0.7 copy-done.1
  21.4 27.2 %grad.1 = (bf16[16,208,256]{2,1,0:T(8,128)(2,1)}, f32[8,128]{1,0:T(8,128)}) custom-call(bf16[128,1536]{1,0:T(8,128)(2,1)} %bitcast.6, bf16[128,768]{1,0:T(8,128)(2,1)} %get-tuple-element.15.embed_ref, bf16[6,256,256]{2,1,0:T(8,128)(2,1)} %get-tuple-element.16.conv_ref, bf16[256,512]{1,0:T(8,128)(2,1)} %get-tuple-element.17.in_ref, ...), custom_call_target="tpu_custom_call" | custom-call | flops 11200000000 | bytes 4000000 | tf_op jit(solution)/shard_map/grad/pallas_call | solution.py:285
  48.6 32.3 %all_to_all.27.recv_ref = bf16[16,208,256]{2,1,0:T(8,128)(2,1)} all-to-all(bf16[16,208,256]{2,1,0:T(8,128)(2,1)} %get-tuple-element.20), channel_id=1, replica_groups=mesh['member'=8,'z'=4,'xh'=2,'xl'=2] {'z','xh','xl'}, dimensions={0} | all-to-all | bytes 3407872 | tf_op jit(solution)/shard_map/all_to_all | solution.py:374
  80.9 2.5 %reduce.1 = (f32[2,208,256]{2,1,0:T(8,128)}, f32[128,128]{1,0:T(8,128)}) custom-call(bf16[16,208,256]{2,1,0:T(8,128)(2,1)} %all_to_all.27.recv_ref, f32[8,128]{1,0:T(8,128)} %get-tuple-element.21.stat_ref), custom_call_target="tpu_custom_call" | custom-call | tf_op jit(solution)/shard_map/reduce/pallas_call | solution.py:327
  83.4 11.8 %all_to_all.28 = f32[16,8,128]{2,1,0:T(8,128)} all-to-all(f32[16,8,128]{2,1,0:T(8,128)} %bitcast.8), channel_id=1, replica_groups=mesh['member'=8,'z'=4,'xh'=2,'xl'=2] {'z','xh','xl'}, dimensions={0} | all-to-all | bytes 131072 | tf_op jit(solution)/shard_map/all_to_all | solution.py:376
  95.2 2.0 %finish.1 = (f32[2,3,256]{2,1,0:T(4,128)}, f32[2,3,2,16,256]{4,3,2,1,0:T(8,128)}, f32[2,16,512]{2,1,0:T(8,128)}, f32[2,32,512]{2,1,0:T(8,128)}, f32[2,32,13]{2,1,0:T(8,128)}, /*index=5*/f32[2,12]{1,0:T(2,128)}) custom-call(f32[2,208,256]{2,1,0:T(8,128)} %get-tuple-element.22.sum_ref, f32[128,128]{1,0:T(8,128)} %bitcast.7), custom_call_target="tpu_custom_call" | custom-call | tf_op jit(solution)/shard_map/finish/pallas_call | solution.py:360
  97.2 1.3 %copy.19 = f32[2,3,256]{2,0,1:T(2,128)} copy(f32[2,3,256]{2,1,0:T(4,128)} %get-tuple-element.24) | data formatting | bytes 12288 | tf_op jit(solution)/shard_map/finish/pallas_call | solution.py:360
  98.5 1.4 %copy.20 = f32[2,32,13]{1,0,2:T(2,128)} copy(f32[2,32,13]{2,1,0:T(8,128)} %get-tuple-element.28) | data formatting | bytes 6656 | tf_op jit(solution)/shard_map/finish/pallas_call | solution.py:360
  (1 shorter events, 0.0 us)
Async XLA Ops:
  0.6 13.4 %copy-start = (f32[2,12]{1,0:T(2,128)S(1)}, f32[2,12]{1,0:T(2,128)}, u32[]{:S(2)}) copy-start(f32[2,12]{1,0:T(2,128)} %param.19) | copy-start | bytes 292
  6.6 14.0 %all-to-all-start = ((bf16[16,8,1536]{2,1,0:T(8,128)(2,1)}), bf16[16,8,1536]{2,1,0:T(8,128)(2,1)S(1)}, u32[]{:S(2)}, u32[]{:S(2)}) async-start(bf16[16,8,1536]{2,1,0:T(8,128)(2,1)} %bitcast.5), calls=%async_computation | async-start | bytes 786432 | tf_op jit(solution)/shard_map/all_to_all | solution.py:370
  20.6 0.7 copy-start.1

commit v2 on v1

--- a/solution.py
+++ b/solution.py
@@ -63,7 +63,7 @@
     reward, old_value = parts[:, 0:128], parts[:, 128:256]
     next_value, old_logp = parts[:, 256:384], parts[:, 384:512]
     widen = onehot(iota((STEPS, 128), 0) == iota((STEPS, 128), 1))
-    done = dot(done_ref[...].astype(f32).astype(bf16), widen)
+    done = dot_tn(done_ref[...].astype(f32).astype(bf16), widen)
     lane = iota((spans, 128), 1)
     alive = jnp.where(lane < STEPS, 1.0 - done, 0.0)
     advantage = reward + gamma_rate * alive * next_value - old_value
@@ -89,15 +89,15 @@
         placed = placed + dot(scalars, place_scal) + live
         groups.append(placed.astype(bf16))
 
+    slots = MEMBERS * SLOT
     ids = ids_ref[...]
-    named = (lane == ids).astype(f32)
-    lower = onehot(iota((spans, spans), 0) > iota((spans, spans), 1))
-    before = dot(lower, named.astype(bf16))
-    rank = jnp.sum(before * named, axis=1, keepdims=True)
-    slot = ids * SLOT + rank.astype(jnp.int32)
-    dispatch = onehot(lane == slot)
+    slot, span = iota((slots, spans), 0), iota((slots, spans), 1)
+    named = onehot(iota((MEMBERS, spans), 0) == ids)
+    earlier = onehot(iota((spans, spans), 0) < iota((spans, spans), 1))
+    rank = jnp.sum(dot(named, earlier) * named.astype(f32), axis=0, keepdims=True)
+    dispatch = onehot(slot == ids * SLOT + rank.astype(jnp.int32))
     for g in range(3):
-        out_ref[:, 512 * g : 512 * g + 512] = dot_tn(dispatch, groups[g]).astype(bf16)
+        out_ref[:, 512 * g : 512 * g + 512] = dot(dispatch, groups[g]).astype(bf16)
 
 
 def pack(observations, rollout, done_flags, member_ids):
@@ -105,98 +105,116 @@
         pack_kernel,
         out_shape=jax.ShapeDtypeStruct((MEMBERS * SLOT, WIDTH), bf16),
         name="pack",
-    )(observations, rollout, done_flags, member_ids)
-
-
-def weights_kernel(which_ref, embed_ref, conv_ref, in_ref, mid_ref, head_ref, embed_out, conv_out, in_out, mid_out, head_out):
-    row, col = iota((128, 256), 0), iota((128, 256), 1)
+    )(observations, rollout, done_flags.T, member_ids.T)
+
+
+def weights_kernel(
+    which_ref, embed_ref, conv_ref, in_ref, mid_ref, head_ref, scale_ref,
+    embed_out, conv_out, in_out, mid_out, head_out, scale_out,
+):
     embed = embed_ref[0].astype(bf16)
     r, k = iota((128, OBS), 0), iota((128, OBS), 1)
     for half in range(2):
         spread = onehot(r == k + REC * half)
         embed_out[:, 256 * half : 256 * half + 256] = dot(spread, embed).astype(bf16)
-    even = (row - 48 == col - FIRST_LANE) & (row >= 48) & (row < 64)
-    odd = (row - 112 == col - 128 - FIRST_LANE) & (row >= 112)
-    embed_out[:, 512:768] = onehot(even | odd)
     for layer in range(3):
         for tap in range(2):
-            conv_out[2 * layer + tap] = conv_ref[0, layer, tap].astype(bf16)
+            conv_out[layer, 256 * tap : 256 * tap + 256, :] = conv_ref[0, layer, tap].astype(bf16)
     in_out[...] = in_ref[0].astype(bf16)
     mid_out[...] = mid_ref[0].astype(bf16)
-    a, lane = iota((ACT + 1, 128), 0), iota((ACT + 1, 128), 1)
-    head_out[...] = dot(head_ref[0].astype(bf16), onehot(a + FIRST_LANE == lane)).astype(bf16)
-
-
-def prepare(which, embed, conv, trunk_in, trunk_mid, head):
+    first = which_ref[0] == 0
+    head = jnp.where(first, head_ref[:, 0, :], head_ref[:, 1, :]).astype(bf16)
+    spread = onehot(iota((16, ACT + 1), 0) == iota((16, ACT + 1), 1) + FIRST_LANE)
+    head_out[...] = dot(spread, head).astype(bf16)
+    scale = jnp.where(first, scale_ref[0:1, :], scale_ref[1:2, :])
+    at = iota((16, ACT), 0) == iota((16, ACT), 1) + FIRST_LANE
+    column = jnp.sum(jnp.where(at, scale, 0.0), axis=1, keepdims=True)
+    scale_out[...] = jnp.broadcast_to(column, (16, 128))
+
+
+def prepare(which, embed, conv, trunk_in, trunk_mid, head, log_std):
     def one(shape):
         return pl.BlockSpec((1,) + shape, lambda i, w: (w[0],) + (0,) * len(shape))
 
     def whole(shape):
         return pl.BlockSpec(shape, lambda i, w: (0,) * len(shape))
 
-    outs = ((128, 768), (6, CH, CH), (CH, UNITS), (UNITS, UNITS), (UNITS, 128))
+    head = head.transpose(2, 0, 1)
+    outs = ((128, 512), (3, 2 * CH, CH), (CH, UNITS), (UNITS, UNITS), (16, UNITS))
     return pl.pallas_call(
         weights_kernel,
         grid_spec=pltpu.PrefetchScalarGridSpec(
             num_scalar_prefetch=1,
             grid=(1,),
-            in_specs=[one(x.shape[1:]) for x in (embed, conv, trunk_in, trunk_mid, head)],
-            out_specs=[whole(s) for s in outs],
+            in_specs=[one(x.shape[1:]) for x in (embed, conv, trunk_in, trunk_mid)] + [whole(head.shape), whole(log_std.shape)],
+            out_specs=[whole(s) for s in outs] + [whole((16, 128))],
         ),
-        out_shape=[jax.ShapeDtypeStruct(s, bf16) for s in outs],
+        out_shape=[jax.ShapeDtypeStruct(s, bf16) for s in outs] + [jax.ShapeDtypeStruct((16, 128), f32)],
         cost_estimate=pl.CostEstimate(flops=0, bytes_accessed=5_000_000, transcendentals=0),
+        compiler_params=pltpu.CompilerParams(vmem_limit_bytes=16 * 1024 * 1024),
         name="weights",
-    )(which, embed, conv, trunk_in, trunk_mid, head)
+    )(which, embed, conv, trunk_in, trunk_mid, head, log_std)
 
 
 def grad_kernel(
     recv_ref, embed_ref, conv_ref, in_ref, mid_ref, head_ref, scale_ref,
     send_ref, stat_ref,
-    xc, hid, rec, c0, c1, c2, c3, g0, g1, g2, first, second, dout, dp2, dp1, dhid, dm0, dm1, dm2, dpair,
-    acc_conv, acc_in, acc_mid, acc_head,
+    xc, xt, hid, c0, c1, c2, c3, g0, g1, g2, first, second, dout, dp2, dp1, dhid, dm0, dm1, dm2, dpair,
+    acc_conv, acc_in, acc_mid, acc_head, acc_stat,
 ):
     cs, gs, dms = (c0, c1, c2), (g0, g1, g2), (dm0, dm1, dm2)
     for ref in cs:
         ref[0:PAD, :] = jnp.zeros((PAD, CH), bf16)
     for ref in dms:
         ref[ALL_ROWS : ALL_ROWS + PAD, :] = jnp.zeros((PAD, CH), bf16)
-    acc_conv[...] = jnp.zeros_like(acc_conv)
-    acc_in[...] = jnp.zeros_like(acc_in)
-    acc_mid[...] = jnp.zeros_like(acc_mid)
-    acc_head[...] = jnp.zeros_like(acc_head)
-    stat_ref[...] = jnp.zeros_like(stat_ref)
+    for ref in (acc_conv, acc_in, acc_mid, acc_head, acc_stat):
+        ref[...] = jnp.zeros_like(ref)
 
     r, k = iota((SPANS, SOURCES * SLOT), 0), iota((SPANS, SOURCES * SLOT), 1)
     compact = onehot(((k & 7) < CAP) & (r == (k >> 3) * CAP + (k & 7)))
-    lane1 = iota((1, 128), 1)
-    is_act = (lane1 >= FIRST_LANE) & (lane1 < FIRST_LANE + ACT)
-    log_scale = scale_ref[0:1, :]
+    r, k = iota((64, 128), 0), iota((64, 128), 1)
+    entry = r & 31
+    select = onehot((entry >= FIRST_LANE) & (entry < FIRST_LANE + 16) & (k == entry + 48 - FIRST_LANE + (r >> 5) * REC))
+    sub = iota((16, 1), 0)
+    is_act = (sub >= FIRST_LANE) & (sub < FIRST_LANE + ACT)
+    log_scale = scale_ref[:, 0:1]
     inverse = jnp.where(is_act, jnp.exp(-log_scale), 0.0)
-    offset = jnp.sum(jnp.where(is_act, log_scale, 0.0), axis=1, keepdims=True) + ACT * half_log_tau
+    offset = jnp.sum(jnp.where(is_act, log_scale, 0.0), axis=0, keepdims=True) + ACT * half_log_tau
+    lane = iota((1, ROWS), 1)
+    odd = lane < 0
+    for s in range(1, CHUNK_STEPS, 2):
+        odd = odd | ((lane >= s * SPANS) & (lane < (s + 1) * SPANS))
 
     @pl.loop(0, CHUNKS)
     def _(i):
         base = i * ROWS
-        for p in range(CHUNK_STEPS // 2):
-            pair = i * (CHUNK_STEPS // 2) + p
-            x = recv_ref[:, pl.ds(pl.multiple_of(pair * 128, 128), 128)]
-            x = dot(compact, x).astype(bf16)
-            xc[pl.ds(pl.multiple_of(pair * SPANS, 16), SPANS), :] = x
-            y = dot(x, embed_ref[...])
+        pairs = CHUNK_STEPS // 2
+        x = recv_ref[:, pl.ds(pl.multiple_of(i * (pairs * 128), 128), pairs * 128)]
+        x = dot(compact, x).astype(bf16)
+        half_rows = pl.ds(pl.multiple_of(i * (ROWS // 2), 16), ROWS // 2)
+        for p in range(pairs):
+            part = x[:, 128 * p : 128 * p + 128]
+            xc[pl.ds(pl.multiple_of(i * (ROWS // 2) + p * SPANS, 16), SPANS), :] = part
+            xt[2 * p * SPANS : (2 * p + 1) * SPANS, :] = part
+            xt[(2 * p + 1) * SPANS : (2 * p + 2) * SPANS, :] = part
+        y = dot(xc[half_rows, :], embed_ref[...])
+        for p in range(pairs):
             for half in range(2):
                 at = (2 * p + half) * SPANS
-                h = y[:, 256 * half : 256 * half + 256]
+                h = y[p * SPANS : (p + 1) * SPANS, 256 * half : 256 * half + 256]
                 hid[at : at + SPANS, :] = h
                 c0[pl.ds(pl.multiple_of(base + PAD + at, 16), SPANS), :] = h.astype(bf16)
-                rec[at : at + SPANS, :] = y[:, 512 + 128 * half : 640 + 128 * half]
         for layer in range(3):
             c, g = cs[layer], gs[layer]
             lag = SPANS * 2**layer
-            mix = dot(c[pl.ds(pl.multiple_of(base + PAD, 16), ROWS), :], conv_ref[2 * layer])
-            mix = mix + dot(c[pl.ds(pl.multiple_of(base + PAD - lag, 16), ROWS), :], conv_ref[2 * layer + 1])
-            grown = jnp.exp(jnp.minimum(mix, 0.0))
-            h = hid[...] + jnp.where(mix > 0, mix, grown - 1.0)
-            g[pl.ds(pl.multiple_of(base, 16), ROWS), :] = grown.astype(bf16)
+            both = jnp.concatenate(
+                [c[pl.ds(pl.multiple_of(base + PAD, 16), ROWS), :], c[pl.ds(pl.multiple_of(base + PAD - lag, 16), ROWS), :]],
+                axis=1,
+            )
+            mix = dot(both, conv_ref[layer])
+            grown = jnp.exp(mix)
+            h = hid[...] + jnp.maximum(mix, jnp.minimum(grown - 1.0, 0.0))
+            g[pl.ds(pl.multiple_of(base, 16), ROWS), :] = jnp.minimum(grown.astype(bf16), jnp.ones((), bf16))
             if layer < 2:
                 hid[...] = h
                 cs[layer + 1][pl.ds(pl.multiple_of(base + PAD, 16), ROWS), :] = h.astype(bf16)
@@ -204,38 +222,40 @@
                 c3[...] = h.astype(bf16)
 
         def elu(x):
-            return jnp.where(x > 0, x, jnp.exp(jnp.minimum(x, 0.0)) - 1.0).astype(bf16)
+            below = jnp.minimum((jnp.exp(x) - 1.0).astype(bf16), jnp.zeros((), bf16))
+            return jnp.maximum(x.astype(bf16), below)
 
         def slope(y):
-            return jnp.minimum(y.astype(f32), 0.0) + 1.0
+            return jnp.minimum(y, jnp.zeros((), bf16)) + jnp.ones((), bf16)
 
         for n in range(0, UNITS, 256):
             first[:, n : n + 256] = elu(dot(c3[...], in_ref[:, n : n + 256]))
         for n in range(0, UNITS, 256):
             second[:, n : n + 256] = elu(dot(first[...], mid_ref[:, n : n + 256]))
-        out = dot(second[...], head_ref[...])
-        record = rec[...]
-        diff = record - out
+        out = dot_nt(head_ref[...], second[...])
+        record = dot_nt(select, xt[...])
+        record = jnp.where(odd, record[32:64], record[0:32])
+        diff = record[0:16] - out
         scaled = diff * inverse
         square = scaled * scaled
-        advantage = record[:, FIRST_LANE + 13 : FIRST_LANE + 14]
-        old_logp = record[:, FIRST_LANE + 14 : FIRST_LANE + 15]
-        live = record[:, FIRST_LANE + 15 : FIRST_LANE + 16]
-        log_ratio = -0.5 * jnp.sum(square, axis=1, keepdims=True) - offset - old_logp
+        advantage = record[FIRST_LANE + 13 : FIRST_LANE + 14]
+        old_logp = record[FIRST_LANE + 14 : FIRST_LANE + 15]
+        live = record[FIRST_LANE + 15 : FIRST_LANE + 16]
+        log_ratio = -0.5 * jnp.sum(square, axis=0, keepdims=True) - offset - old_logp
         ratio = jnp.exp(log_ratio)
         dlog = live * (0.5 * (ratio - 1.0) - ratio * advantage)
         dvalue = -0.5 * live * diff
-        d = jnp.where(lane1 == FIRST_LANE + ACT, dvalue, dlog * scaled * inverse)
+        d = jnp.where(sub == FIRST_LANE + ACT, dvalue, dlog * scaled * inverse)
         dout[...] = d.astype(bf16)
-        stat_ref[0:1, :] += jnp.where(is_act, jnp.sum(dlog * (square - 1.0), axis=0, keepdims=True), 0.0)
+        acc_stat[...] += jnp.sum(dlog * (square - 1.0), axis=1, keepdims=True)
+        acc_head[...] += dot(dout[...], second[...])
         for n in range(0, UNITS, 256):
-            ds = dot_nt(dout[...], head_ref[n : n + 256, :])
-            dp2[:, n : n + 256] = (ds * slope(second[:, n : n + 256])).astype(bf16)
+            ds = dot_tn(dout[...], head_ref[:, n : n + 256])
+            dp2[:, n : n + 256] = ds.astype(bf16) * slope(second[:, n : n + 256])
         for n in range(0, UNITS, 256):
             df = dot_nt(dp2[...], mid_ref[n : n + 256, :])
-            dp1[:, n : n + 256] = (df * slope(first[:, n : n + 256])).astype(bf16)
+            dp1[:, n : n + 256] = df.astype(bf16) * slope(first[:, n : n + 256])
         dhid[pl.ds(pl.multiple_of(base, 16), ROWS), :] = dot_nt(dp1[...], in_ref[...])
-        acc_head[...] += dot_tn(dout[...], second[...])
         for n in range(0, UNITS, 256):
             acc_mid[n : n + 256, :] += dot_tn(first[:, n : n + 256], dp2[...])
         acc_in[...] += dot_tn(c3[...], dp1[...])
@@ -249,9 +269,9 @@
             c, g, dm = cs[layer], gs[layer], dms[layer]
             lag = SPANS * 2**layer
             dh = dhid[here, :]
-            dm[here, :] = (dh * g[here, :].astype(f32)).astype(bf16)
-            dc = dot_nt(dm[here, :], conv_ref[2 * layer])
-            dc = dc + dot_nt(dm[pl.ds(pl.multiple_of(base + lag, 16), ROWS), :], conv_ref[2 * layer + 1])
+            dm[here, :] = dh.astype(bf16) * g[here, :]
+            dc = dot_nt(dm[here, :], conv_ref[layer, 0:256, :])
+            dc = dc + dot_nt(dm[pl.ds(pl.multiple_of(base + lag, 16), ROWS), :], conv_ref[layer, 256:512, :])
             dh = dh + dc
             if layer > 0:
                 dhid[here, :] = dh
@@ -267,7 +287,7 @@
     r, k = iota((SHARDS * 16, OBS), 0), iota((SHARDS * 16, OBS), 1)
     spread = onehot(((r & 15) < 3) & (k == (r >> 4) * 3 + (r & 15)))
     extra = dot(spread, dembed).astype(bf16)
-    dhead = acc_head[0:16, :]
+    dhead = acc_head[...]
     for s in range(SHARDS):
         for q in range(6):
             send_ref[s, 16 * q : 16 * q + 16, :] = acc_conv[q, 16 * s : 16 * s + 16, :].astype(bf16)
@@ -277,6 +297,9 @@
         send_ref[s, 192:208, :] = extra[16 * s : 16 * s + 16, :]
         moved = jnp.where(iota((16, 32), 0) >= FIRST_LANE, dhead[:, 32 * s : 32 * s + 32].astype(bf16).astype(f32), extra[16 * s : 16 * s + 16, 0:32].astype(f32))
         send_ref[s, 192:208, 0:32] = moved.astype(bf16)
+    at = (iota((16, 128), 0) == iota((16, 128), 1)) & is_act
+    line = jnp.sum(jnp.where(at, acc_stat[...], 0.0), axis=0, keepdims=True)
+    stat_ref[...] = jnp.broadcast_to(line, (8, 128))
 
 
 def member_grad(recv, embed, conv, trunk_in, trunk_mid, head, scale):
@@ -289,19 +312,19 @@
             jax.ShapeDtypeStruct((8, 128), f32),
         ),
         scratch_shapes=[
-            v((half, 128), bf16), v((ROWS, CH), f32), v((ROWS, 128), f32),
+            v((half, 128), bf16), v((ROWS, 128), bf16), v((ROWS, CH), f32),
             v((PAD + ALL_ROWS, CH), bf16), v((PAD + ALL_ROWS, CH), bf16), v((PAD + ALL_ROWS, CH), bf16),
             v((ROWS, CH), bf16),
             v((ALL_ROWS, CH), bf16), v((ALL_ROWS, CH), bf16), v((ALL_ROWS, CH), bf16),
-            v((ROWS, UNITS), bf16), v((ROWS, UNITS), bf16), v((ROWS, 128), bf16),
+            v((ROWS, UNITS), bf16), v((ROWS, UNITS), bf16), v((16, ROWS), bf16),
             v((ROWS, UNITS), bf16), v((ROWS, UNITS), bf16),
             v((ALL_ROWS, CH), f32),
             v((ALL_ROWS + PAD, CH), bf16), v((ALL_ROWS + PAD, CH), bf16), v((ALL_ROWS + PAD, CH), bf16),
             v((half, 512), bf16),
-            v((6, CH, CH), f32), v((CH, UNITS), f32), v((UNITS, UNITS), f32), v((128, UNITS), f32),
+            v((6, CH, CH), f32), v((CH, UNITS), f32), v((UNITS, UNITS), f32), v((16, UNITS), f32), v((16, 128), f32),
         ],
         cost_estimate=pl.CostEstimate(flops=11_200_000_000, bytes_accessed=4_000_000, transcendentals=4_000_000),
-        compiler_params=pltpu.CompilerParams(vmem_limit_bytes=56 * 1024 * 1024),
+        compiler_params=pltpu.CompilerParams(vmem_limit_bytes=36 * 1024 * 1024),
         name="grad",
     )(recv, embed, conv, trunk_in, trunk_mid, head, scale)
 
@@ -350,27 +373,26 @@
         for n in range(2):
             in_ref[member, :, 256 * n : 256 * n + 256] = part[96 + 16 * n : 112 + 16 * n, :] * scale
             mid_ref[member, :, 256 * n : 256 * n + 256] = part[128 + 32 * n : 160 + 32 * n, :] * scale
-        embed_ref[member] = part[192:195, :] * scale
-        head = (part[192:208, 0:128] * scale).T
-        head_ref[member] = head[0:32, FIRST_LANE:16]
+        embed_ref[:, member, :] = part[192:195, :] * scale
+        head_ref[:, member, :] = part[192 + FIRST_LANE : 208, 0:32] * scale
 
 
 def finish(sums, cast):
-    shapes = ((2, 3, 256), (2, 3, 2, 16, 256), (2, 16, 512), (2, 32, 512), (2, 32, 13), (2, 12))
-    return pl.pallas_call(
+    shapes = ((3, 2, 256), (2, 3, 2, 16, 256), (2, 16, 512), (2, 32, 512), (13, 2, 32), (2, 12))
+    embed, conv, first, second, head, std = pl.pallas_call(
         finish_kernel,
         out_shape=tuple(jax.ShapeDtypeStruct(s, f32) for s in shapes),
         name="finish",
     )(sums, cast)
+    return embed.transpose(1, 0, 2), conv, first, second, head.transpose(1, 2, 0), std
 
 
 def local(observations, rollout, done_flags, member_ids, embed_weight, conv_weight, trunk_in, trunk_mid, head_weight, log_std):
     which = lax.axis_index("xl").astype(jnp.int32)
     packed = pack(observations, rollout, done_flags, member_ids)
     recv = lax.all_to_all(packed, ("member", "xl"), split_axis=0, concat_axis=0, tiled=True)
-    prepared = prepare(which.reshape(1), embed_weight, conv_weight, trunk_in, trunk_mid, head_weight)
-    scale = jnp.pad(lax.dynamic_index_in_dim(log_std, which, 0), ((0, 7), (FIRST_LANE, 128 - ACT - FIRST_LANE)))
-    send, stat = member_grad(recv, *prepared, scale)
+    prepared = prepare(which.reshape(1), embed_weight, conv_weight, trunk_in, trunk_mid, head_weight, log_std)
+    send, stat = member_grad(recv, *prepared)
     parts = lax.all_to_all(send, ("z", "xh", "xl"), split_axis=0, concat_axis=0, tiled=True)
     sums, cast = reduce_parts(parts, stat)
     cast = lax.all_to_all(cast, ("z", "xh", "xl"), split_axis=0, concat_axis=0, tiled=True)

time: 101 us -> 85.8 us (0.85)
  Pallas kernels: 38.3 us -> 27 us
  local copies, waits for them, and re-layouts: 8.71 us -> 7.08 us
  waiting for transfers between devices: 2.53 us -> 0.96 us
    pallas_call x1, Pallas kernels: 27.2 us -> 19.1 us  [member_grad(): pl.pallas_call(grad_kernel, out_shape=(jax.ShapeDtypeStruct((SHARDS, BLOC...]
    pallas_call x1, Pallas kernels: 3.35 us -> 0.33 us  [prepare(): pl.pallas_call(weights_kernel, grid_spec=pltpu.PrefetchScalarGridSpec(num...]
    pallas_call x2 -> x0, local copies, waits for them, and re-layouts: 2.73 us -> none  [finish(): pl.pallas_call(finish_kernel, out_shape=tuple((jax.ShapeDtypeStruct(s, f3...]
    unnamed x7 -> x14, local copies, waits for them, and re-layouts: 5.31 us -> 7.08 us
    all_to_all x1, waiting for transfers between devices: 2.53 us -> 0.96 us  [local(): lax.all_to_all(packed, ('member', 'xl'), split_axis=0, concat_axis=0, til...]
  transfers between devices with their start and end apart: 1 -> 1, of which waited for: 1 -> 1; matrix products, arithmetic and copies ran while one was open for 2% -> 0% of each run, Pallas kernels for 3% -> 0%
where the time goes in v2:
time: 85.8 us; the launch traced here: 85.2 us
  blocking collectives  43.9 us (51%)
  Pallas kernels  27 us (31%)
  local copies, waits for them, and re-layouts  7.08 us (8%)
  starting transfers between devices  5.61 us (7%)
  waiting for transfers between devices  0.96 us (1%)
    all_to_all x1, blocking collectives, local(): lax.all_to_all(send, ('z', 'xh', 'xl'), split_axis=0, concat_axis=0, tile...  32.1 us
    pallas_call x1, Pallas kernels, member_grad(): pl.pallas_call(grad_kernel, out_shape=(jax.ShapeDtypeStruct((SHARDS, BLOC...  19.1 us
    all_to_all x1, blocking collectives, local(): lax.all_to_all(cast, ('z', 'xh', 'xl'), split_axis=0, concat_axis=0, tile...  11.8 us
    unnamed x14, local copies, waits for them, and re-layouts  7.08 us
    all_to_all x1, starting transfers between devices, local(): lax.all_to_all(packed, ('member', 'xl'), split_axis=0, concat_axis=0, til...  5.61 us
    pallas_call x1, Pallas kernels, pack(): pl.pallas_call(pack_kernel, out_shape=jax.ShapeDtypeStruct((MEMBERS * SLO...  3.02 us
    pallas_call x1, Pallas kernels, reduce_parts(): pl.pallas_call(reduce_kernel, out_shape=(jax.ShapeDtypeStruct((2, BLOCK,...  2.55 us
    pallas_call x1, Pallas kernels, finish(): pl.pallas_call(finish_kernel, out_shape=tuple((jax.ShapeDtypeStruct(s, f3...  1.97 us
  transfers between devices with their start and end apart: 1, of which 1 were waited for; matrix products, arithmetic and copies ran while one was open for 0% of the time, Pallas kernels for 0%

profile of v2, /device:TPU:0, one launch (start us, length us, event | category | flops | bytes accessed | tf_op | source)
XLA Modules:
  0.0 85.2 jit_solution(15948703364939837762)
XLA Ops:
  0.6 3.0 %pack.1 = bf16[128,1536]{1,0:T(8,128)(2,1)} custom-call(bf16[32,1152]{1,0:T(8,128)(2,1)} %obs_ref.1, bf16[32,384]{1,0:T(8,128)(2,1)} %roll_ref.1, s32[24,32]{1,0:T(8,128)} %bitcast.15, s32[1,32]{1,0:T(1,128)} %bitcast.16), custom_call_target="tpu_custom_call" | custom-call | tf_op jit(solution)/shard_map/pack/pallas_call | solution.py:104
  3.7 5.6 %all-to-all-start = ((bf16[16,8,1536]{2,1,0:T(8,128)(2,1)}), bf16[16,8,1536]{2,1,0:T(8,128)(2,1)S(1)}, u32[]{:S(2)}, u32[]{:S(2)}) async-start(bf16[16,8,1536]{2,1,0:T(8,128)(2,1)} %bitcast.12), calls=%async_computation | async-start | bytes 786432 | tf_op jit(solution)/shard_map/all_to_all | solution.py:393
  9.3 0.0 copy-start
  9.3 1.9 %copy-done = f32[2,3,2,256,256]{4,3,2,1,0:T(8,128)S(1)} copy-done((f32[2,3,2,256,256]{4,3,2,1,0:T(8,128)S(1)}, f32[2,3,2,256,256]{4,3,2,1,0:T(8,128)}, u32[]{:S(2)}) %copy-start) | copy-done | bytes 3145752
  11.2 0.0 copy-start.1
  11.2 1.6 %copy-done.1 = f32[2,512,512]{2,1,0:T(8,128)S(1)} copy-done((f32[2,512,512]{2,1,0:T(8,128)S(1)}, f32[2,512,512]{2,1,0:T(8,128)}, u32[]{:S(2)}) %copy-start.1) | copy-done | bytes 2097176
  12.8 0.0 copy-start.2
  12.8 1.2 %copy-done.2 = f32[2,256,512]{2,1,0:T(8,128)S(1)} copy-done((f32[2,256,512]{2,1,0:T(8,128)S(1)}, f32[2,256,512]{2,1,0:T(8,128)}, u32[]{:S(2)}) %copy-start.2) | copy-done | bytes 1048600
  14.0 0.0 copy-start.3
  14.0 0.9 %copy-done.3 = f32[2,48,256]{2,1,0:T(8,128)S(1)} copy-done((f32[2,48,256]{2,1,0:T(8,128)S(1)}, f32[2,48,256]{2,1,0:T(8,128)}, u32[]{:S(2)}) %copy-start.3) | copy-done | bytes 98328
  14.9 0.0 copy-start.4
  14.9 0.8 copy-done.4
  15.7 0.0 copy-start.6
  15.7 0.7 copy-done.6
  16.4 0.3 weights.1
  16.7 1.0 %all-to-all-done = bf16[16,8,1536]{2,1,0:T(8,128)(2,1)S(1)} async-done(((bf16[16,8,1536]{2,1,0:T(8,128)(2,1)}), bf16[16,8,1536]{2,1,0:T(8,128)(2,1)S(1)}, u32[]{:S(2)}, u32[]{:S(2)}) %all-to-all-start) | async-done | bytes 393248 | tf_op jit(solution)/shard_map/all_to_all | solution.py:393
  17.7 19.1 %grad.1 = (bf16[16,208,256]{2,1,0:T(8,128)(2,1)S(1)}, f32[8,128]{1,0:T(8,128)S(1)}) custom-call(bf16[128,1536]{1,0:T(8,128)(2,1)S(1)} %bitcast.10, bf16[128,512]{1,0:T(8,128)(2,1)S(1)} %get-tuple-element.22.embed_ref, bf16[3,512,256]{2,1,0:T(8,128)(2,1)S(1)} %get-tuple-element.23.conv_ref, bf16[256,512]{1,0:T(8,128)(2,1)S(1)} %get-tuple-element.24.in_ref, ...), custom_call_target="tpu_custom_call" | custom-call | flops 11200000000 | bytes 4000000 | tf_op jit(solution)/shard_map/grad/pallas_call | solution.py:308
  36.8 0.0 copy-start.5
  36.8 32.1 %all_to_all.27.recv_ref = bf16[16,208,256]{2,1,0:T(8,128)(2,1)} all-to-all(bf16[16,208,256]{2,1,0:T(8,128)(2,1)S(1)} %get-tuple-element.28), channel_id=1, replica_groups=mesh['member'=8,'z'=4,'xh'=2,'xl'=2] {'z','xh','xl'}, dimensions={0} | all-to-all | bytes 3407872 | tf_op jit(solution)/shard_map/all_to_all | solution.py:396
  68.9 0.0 copy-done.5
  68.9 2.5 %reduce.1 = (f32[2,208,256]{2,1,0:T(8,128)}, f32[128,128]{1,0:T(8,128)}) custom-call(bf16[16,208,256]{2,1,0:T(8,128)(2,1)} %all_to_all.27.recv_ref, f32[8,128]{1,0:T(8,128)} %copy-done.5), custom_call_target="tpu_custom_call" | custom-call | tf_op jit(solution)/shard_map/reduce/pallas_call | solution.py:350
  71.5 11.8 %all_to_all.28 = f32[16,8,128]{2,1,0:T(8,128)} all-to-all(f32[16,8,128]{2,1,0:T(8,128)} %bitcast.14), channel_id=1, replica_groups=mesh['member'=8,'z'=4,'xh'=2,'xl'=2] {'z','xh','xl'}, dimensions={0} | all-to-all | bytes 131072 | tf_op jit(solution)/shard_map/all_to_all | solution.py:398
  83.2 2.0 %finish.1 = (f32[3,2,256]{2,1,0:T(2,128)}, f32[2,3,2,16,256]{4,3,2,1,0:T(8,128)}, f32[2,16,512]{2,1,0:T(8,128)}, f32[2,32,512]{2,1,0:T(8,128)}, f32[13,2,32]{2,1,0:T(2,128)}, /*index=5*/f32[2,12]{1,0:T(2,128)}) custom-call(f32[2,208,256]{2,1,0:T(8,128)} %get-tuple-element.30.sum_ref, f32[128,128]{1,0:T(8,128)} %bitcast.13), custom_call_target="tpu_custom_call" | custom-call | tf_op jit(solution)/shard_map/finish/pallas_call | solution.py:382
Async XLA Ops:
  3.7 14.0 %all-to-all-start = ((bf16[16,8,1536]{2,1,0:T(8,128)(2,1)}), bf16[16,8,1536]{2,1,0:T(8,128)(2,1)S(1)}, u32[]{:S(2)}, u32[]{:S(2)}) async-start(bf16[16,8,1536]{2,1,0:T(8,128)(2,1)} %bitcast.12), calls=%async_computation | async-start | bytes 786432 | tf_op jit(solution)/shard_map/all_to_all | solution.py:393
  9.3 1.9 %copy-start = (f32[2,3,2,256,256]{4,3,2,1,0:T(8,128)S(1)}, f32[2,3,2,256,256]{4,3,2,1,0:T(8,128)}, u32[]{:S(2)}) copy-start(f32[2,3,2,256,256]{4,3,2,1,0:T(8,128)} %conv_ref.1) | copy-start | bytes 9437188
  11.2 1.6 %copy-start.1 = (f32[2,512,512]{2,1,0:T(8,128)S(1)}, f32[2,512,512]{2,1,0:T(8,128)}, u32[]{:S(2)}) copy-start(f32[2,512,512]{2,1,0:T(8,128)} %mid_ref.1) | copy-start | bytes 6291460
  12.8 1.2 %copy-start.2 = (f32[2,256,512]{2,1,0:T(8,128)S(1)}, f32[2,256,512]{2,1,0:T(8,128)}, u32[]{:S(2)}) copy-start(f32[2,256,512]{2,1,0:T(8,128)} %in_ref.1) | copy-start | bytes 3145732
  14.0 0.9 %copy-start.3 = (f32[2,48,256]{2,1,0:T(8,128)S(1)}, f32[2,48,256]{2,1,0:T(8,128)}, u32[]{:S(2)}) copy-start(f32[2,48,256]{2,1,0:T(8,128)} %embed_ref.1) | copy-start | bytes 294916
  14.9 0.8 copy-start.4
  15.7 0.7 copy-start.6
  36.8 32.1 %copy-start.5 = (f32[8,128]{1,0:T(8,128)}, f32[8,128]{1,0:T(8,128)S(1)}, u32[]{:S(2)}) copy-start(f32[8,128]{1,0:T(8,128)S(1)} %get-tuple-element.29.stat_ref) | copy-start | bytes 12292

commit v3 on v2

v3 whole, which is shorter than its diff:
```python
import jax
import jax.numpy as jnp
from jax import lax
from jax.experimental import pallas as pl
from jax.experimental.pallas import tpu as pltpu
from jax.sharding import Mesh, PartitionSpec as P

gamma_rate = 0.99
trace_rate = 0.95
half_log_tau = 0.9189385332046727

OBS = 48
STEPS = 24
ACT = 12
CH = 256
UNITS = 512
MEMBERS = 16
CAP = 6
SLOT = 8
REC = 64
WIDTH = STEPS * REC
ENTRIES = 805388
SOURCES = 16
SPANS = SOURCES * CAP
CHUNK_STEPS = 8
CHUNKS = STEPS // CHUNK_STEPS
ROWS = CHUNK_STEPS * SPANS
ALL_ROWS = STEPS * SPANS
PAD = 4 * SPANS
SHARDS = 16
HALF = 104
W_IN, W_MID, W_EMBED, W_HEAD, W_ROWS = 1536, 2048, 3072, 3328, 3360
f32 = jnp.float32
bf16 = jnp.bfloat16


def iota(shape, dim):
    return lax.broadcasted_iota(jnp.int32, shape, dim)


def dot(a, b):
    return jnp.dot(a, b, preferred_element_type=f32)


def dot_tn(a, b):
    return lax.dot_general(a, b, (((0,), (0,)), ((), ())), preferred_element_type=f32)


def dot_nt(a, b):
    return lax.dot_general(a, b, (((1,), (1,)), ((), ())), preferred_element_type=f32)


def onehot(cond):
    return jnp.where(cond, 1.0, 0.0).astype(bf16)


def pack_kernel(obs_ref, roll_ref, done_ref, ids_ref, out_ref):
    spans = obs_ref.shape[0]
    row, col = iota((STEPS * 16, 512), 0), iota((STEPS * 16, 512), 1)
    step = col & 127
    pick = onehot((row == 16 * step + 12 + (col >> 7)) & (step < STEPS))
    parts = dot(roll_ref[...], pick)
    reward, old_value = parts[:, 0:128], parts[:, 128:256]
    next_value, old_logp = parts[:, 256:384], parts[:, 384:512]
    widen = onehot(iota((STEPS, 128), 0) == iota((STEPS, 128), 1))
    done = dot_tn(done_ref[...].astype(f32).astype(bf16), widen)
    lane = iota((spans, 128), 1)
    alive = jnp.where(lane < STEPS, 1.0 - done, 0.0)
    advantage = reward + gamma_rate * alive * next_value - old_value
    carry = gamma_rate * trace_rate * alive
    for shift in (1, 2, 4, 8, 16):
        advantage = advantage + carry * pltpu.roll(advantage, 128 - shift, 1)
        carry = carry * pltpu.roll(carry, 128 - shift, 1)
    target = jnp.where(lane < STEPS, advantage + old_value, 0.0)
    advantage = jnp.where(lane < STEPS, advantage, 0.0)
    scalars = jnp.concatenate([target.astype(bf16), advantage.astype(bf16), old_logp.astype(bf16)], axis=1)

    col = iota((384, 512), 1)
    row = iota((384, 512), 0)
    spot, within = col & 63, col >> 6
    place_obs = onehot((row == 48 * within + spot) & (spot < 48))
    place_act = onehot((row == 16 * within + spot - 48) & (spot >= 48) & (spot < 60))[0:128]
    live = jnp.where((iota((spans, 512), 1) & 63) == 63, 1.0, 0.0)
    groups = []
    for g in range(3):
        place_scal = onehot((spot >= 60) & (spot < 63) & (row == (spot - 60) * 128 + 8 * g + within))
        placed = dot(obs_ref[:, 384 * g : 384 * g + 384], place_obs)
        placed = placed + dot(roll_ref[:, 128 * g : 128 * g + 128], place_act)
        placed = placed + dot(scalars, place_scal) + live
        groups.append(placed.astype(bf16))

    slots = MEMBERS * SLOT
    ids = ids_ref[...]
    slot, span = iota((slots, spans), 0), iota((slots, spans), 1)
    named = onehot(iota((MEMBERS, spans), 0) == ids)
    earlier = onehot(iota((spans, spans), 0) < iota((spans, spans), 1))
    rank = jnp.sum(dot(named, earlier) * named.astype(f32), axis=0, keepdims=True)
    dispatch = onehot(slot == ids * SLOT + rank.astype(jnp.int32))
    for g in range(3):
        out_ref[:, 512 * g : 512 * g + 512] = dot(dispatch, groups[g]).astype(bf16)


def pack(observations, rollout, done_flags, member_ids):
    return pl.pallas_call(
        pack_kernel,
        out_shape=jax.ShapeDtypeStruct((MEMBERS * SLOT, WIDTH), bf16),
        name="pack",
    )(observations, rollout, done_flags.T, member_ids.T)


def weights_kernel(which_ref, embed_ref, conv_ref, in_ref, mid_ref, head_ref, out_ref):
    for layer in range(3):
        for tap in range(2):
            at = CH * (2 * layer + tap)
            out_ref[at : at + CH, :] = conv_ref[0, layer, tap].astype(bf16)
    head = jnp.where(which_ref[0] == 0, head_ref[:, 0, :], head_ref[:, 1, :]).astype(bf16)
    head = dot(onehot(iota((16, ACT + 1), 0) == iota((16, ACT + 1), 1)), head).astype(bf16)
    embed = embed_ref[0].astype(bf16)
    r, k = iota((128, OBS), 0), iota((128, OBS), 1)
    for n in range(2):
        cols = slice(256 * n, 256 * n + 256)
        out_ref[W_IN + CH * n : W_IN + CH * n + CH, :] = in_ref[0, :, cols].astype(bf16)
        out_ref[W_MID + UNITS * n : W_MID + UNITS * n + UNITS, :] = mid_ref[0, :, cols].astype(bf16)
        out_ref[W_EMBED + 128 * n : W_EMBED + 128 * n + 128, :] = dot(onehot(r == k + REC * n), embed).astype(bf16)
        out_ref[W_HEAD + 16 * n : W_HEAD + 16 * n + 16, :] = head[:, cols]


def prepare(which, embed, conv, trunk_in, trunk_mid, head):
    def one(shape):
        return pl.BlockSpec((1,) + shape, lambda i, w: (w[0],) + (0,) * len(shape))

    def whole(shape):
        return pl.BlockSpec(shape, lambda i, w: (0,) * len(shape))

    head = head.transpose(2, 0, 1)
    return pl.pallas_call(
        weights_kernel,
        grid_spec=pltpu.PrefetchScalarGridSpec(
            num_scalar_prefetch=1,
            grid=(1,),
            in_specs=[one(x.shape[1:]) for x in (embed, conv, trunk_in, trunk_mid)] + [whole(head.shape)],
            out_specs=whole((W_ROWS, CH)),
        ),
        out_shape=jax.ShapeDtypeStruct((W_ROWS, CH), bf16),
        cost_estimate=pl.CostEstimate(flops=0, bytes_accessed=5_000_000, transcendentals=0),
        compiler_params=pltpu.CompilerParams(vmem_limit_bytes=60 * 1024 * 1024),
        name="weights",
    )(which, embed, conv, trunk_in, trunk_mid, head)


def grad_kernel(
    flags_ref, recv_ref, w_ref, scale_ref, other_ref,
    keep_ref, give_ref, stat_ref,
    xc, xt, hid, c0, c1, c2, c3, g0, g1, g2, first, second, dout, dp2, dp1, dhid, dm0, dm1, dm2, dpair,
    acc_conv, acc_in, acc_mid, acc_head, acc_stat,
):
    cs, gs, dms = (c0, c1, c2), (g0, g1, g2), (dm0, dm1, dm2)
    for ref in cs:
        ref[0:PAD, :] = jnp.zeros((PAD, CH), bf16)
    for ref in dms:
        ref[ALL_ROWS : ALL_ROWS + PAD, :] = jnp.zeros((PAD, CH), bf16)
    for ref in (acc_conv, acc_in, acc_mid, acc_head, acc_stat):
        ref[...] = jnp.zeros_like(ref)

    r, k = iota((SPANS, SOURCES * SLOT), 0), iota((SPANS, SOURCES * SLOT), 1)
    compact = onehot(((k & 7) < CAP) & (r == (k >> 3) * CAP + (k & 7)))
    r, k = iota((64, 128), 0), iota((64, 128), 1)
    entry = r & 31
    select = onehot((entry < 16) & (k == entry + OBS + (r >> 5) * REC))
    sub = iota((16, 1), 0)
    is_act = sub < ACT
    scale = jnp.where(flags_ref[1] == 1, scale_ref[...], other_ref[...])
    scale = jnp.where(flags_ref[0] == 0, scale[0:1, :], scale[1:2, :])
    log_scale = jnp.sum(jnp.where(iota((16, ACT), 0) == iota((16, ACT), 1), scale, 0.0), axis=1, keepdims=True)
    conv = [w_ref.at[2 * CH * layer : 2 * CH * layer + 2 * CH] for layer in range(3)]
    in_half = [w_ref.at[W_IN + CH * n : W_IN + CH * n + CH] for n in range(2)]
    mid_half = [w_ref.at[W_MID + UNITS * n : W_MID + UNITS * n + UNITS] for n in range(2)]
    embed_half = [w_ref.at[W_EMBED + 128 * n : W_EMBED + 128 * n + 128] for n in range(2)]
    head_half = [w_ref.at[W_HEAD + 16 * n : W_HEAD + 16 * n + 16] for n in range(2)]

    def across(halves, rows):
        return jnp.concatenate([half[rows, :] for half in halves], axis=1)
    inverse = jnp.where(is_act, jnp.exp(-log_scale), 0.0)
    offset = jnp.sum(jnp.where(is_act, log_scale, 0.0), axis=0, keepdims=True) + ACT * half_log_tau
    lane = iota((1, ROWS), 1)
    odd = lane < 0
    for s in range(1, CHUNK_STEPS, 2):
        odd = odd | ((lane >= s * SPANS) & (lane < (s + 1) * SPANS))

    @pl.loop(0, CHUNKS)
    def _(i):
        base = i * ROWS
        pairs = CHUNK_STEPS // 2
        x = recv_ref[:, pl.ds(pl.multiple_of(i * (pairs * 128), 128), pairs * 128)]
        x = dot(compact, x).astype(bf16)
        half_rows = pl.ds(pl.multiple_of(i * (ROWS // 2), 16), ROWS // 2)
        for p in range(pairs):
            part = x[:, 128 * p : 128 * p + 128]
            xc[pl.ds(pl.multiple_of(i * (ROWS // 2) + p * SPANS, 16), SPANS), :] = part
            xt[2 * p * SPANS : (2 * p + 1) * SPANS, :] = part
            xt[(2 * p + 1) * SPANS : (2 * p + 2) * SPANS, :] = part
        y = [dot(xc[half_rows, :], half[...]) for half in embed_half]
        for p in range(pairs):
            for half in range(2):
                at = (2 * p + half) * SPANS
                h = y[half][p * SPANS : (p + 1) * SPANS, :]
                hid[at : at + SPANS, :] = h
                c0[pl.ds(pl.multiple_of(base + PAD + at, 16), SPANS), :] = h.astype(bf16)
        for layer in range(3):
            c, g = cs[layer], gs[layer]
            lag = SPANS * 2**layer
            both = jnp.concatenate(
                [c[pl.ds(pl.multiple_of(base + PAD, 16), ROWS), :], c[pl.ds(pl.multiple_of(base + PAD - lag, 16), ROWS), :]],
                axis=1,
            )
            mix = dot(both, conv[layer][...])
            grown = jnp.exp(mix)
            h = hid[...] + jnp.maximum(mix, jnp.minimum(grown - 1.0, 0.0))
            g[pl.ds(pl.multiple_of(base, 16), ROWS), :] = jnp.minimum(grown.astype(bf16), jnp.ones((), bf16))
            if layer < 2:
                hid[...] = h
                cs[layer + 1][pl.ds(pl.multiple_of(base + PAD, 16), ROWS), :] = h.astype(bf16)
            else:
                c3[...] = h.astype(bf16)

        def elu(x):
            below = jnp.minimum((jnp.exp(x) - 1.0).astype(bf16), jnp.zeros((), bf16))
            return jnp.maximum(x.astype(bf16), below)

        def slope(y):
            return jnp.minimum(y, jnp.zeros((), bf16)) + jnp.ones((), bf16)

        for n in range(0, UNITS, 256):
            first[:, n : n + 256] = elu(dot(c3[...], in_half[n // 256][...]))
        for n in range(0, UNITS, 256):
            second[:, n : n + 256] = elu(dot(first[...], mid_half[n // 256][...]))
        out = dot_nt(across(head_half, slice(0, 16)), second[...])
        record = dot_nt(select, xt[...])
        record = jnp.where(odd, record[32:64], record[0:32])
        diff = record[0:16] - out
        scaled = diff * inverse
        square = scaled * scaled
        advantage = record[13:14]
        old_logp = record[14:15]
        live = record[15:16]
        log_ratio = -0.5 * jnp.sum(square, axis=0, keepdims=True) - offset - old_logp
        ratio = jnp.exp(log_ratio)
        dlog = live * (0.5 * (ratio - 1.0) - ratio * advantage)
        dvalue = -0.5 * live * diff
        d = jnp.where(sub == ACT, dvalue, dlog * scaled * inverse)
        dout[...] = d.astype(bf16)
        acc_stat[...] += jnp.sum(dlog * (square - 1.0), axis=1, keepdims=True)
        acc_head[...] += dot(dout[...], second[...])
        for n in range(0, UNITS, 256):
            ds = dot_tn(dout[...], head_half[n // 256][...])
            dp2[:, n : n + 256] = ds.astype(bf16) * slope(second[:, n : n + 256])
        for n in range(0, UNITS, 256):
            df = dot_nt(dp2[...], across(mid_half, slice(n, n + 256)))
            dp1[:, n : n + 256] = df.astype(bf16) * slope(first[:, n : n + 256])
        dhid[pl.ds(pl.multiple_of(base, 16), ROWS), :] = dot_nt(dp1[...], across(in_half, slice(0, CH)))
        for n in range(0, UNITS, 256):
            acc_mid[n : n + 256, :] += dot_tn(first[:, n : n + 256], dp2[...])
        acc_in[...] += dot_tn(c3[...], dp1[...])

    @pl.loop(0, CHUNKS)
    def _(j):
        i = CHUNKS - 1 - j
        base = i * ROWS
        here = pl.ds(pl.multiple_of(base, 16), ROWS)
        for layer in (2, 1, 0):
            c, g, dm = cs[layer], gs[layer], dms[layer]
            lag = SPANS * 2**layer
            dh = dhid[here, :]
            dm[here, :] = dh.astype(bf16) * g[here, :]
            dc = dot_nt(dm[here, :], conv[layer][0:256, :])
            dc = dc + dot_nt(dm[pl.ds(pl.multiple_of(base + lag, 16), ROWS), :], conv[layer][256:512, :])
            dh = dh + dc
            if layer > 0:
                dhid[here, :] = dh
            else:
                for s in range(CHUNK_STEPS):
                    at = pl.ds(pl.multiple_of(i * (ROWS // 2) + (s // 2) * SPANS, 16), SPANS)
                    dpair[at, 256 * (s % 2) : 256 * (s % 2) + 256] = dh[s * SPANS : s * SPANS + SPANS].astype(bf16)
            acc_conv[2 * layer] += dot_tn(c[pl.ds(pl.multiple_of(base + PAD, 16), ROWS), :], dm[here, :])
            acc_conv[2 * layer + 1] += dot_tn(c[pl.ds(pl.multiple_of(base + PAD - lag, 16), ROWS), :], dm[here, :])

    dembed = dot_tn(xc[...], dpair[...])
    dembed = (dembed[0:OBS, 0:256] + dembed[REC : REC + OBS, 256:512]).astype(bf16)
    r, k = iota((SHARDS * 8, OBS), 0), iota((SHARDS * 8, OBS), 1)
    spread = onehot(((r & 7) < 3) & (k == (r >> 3) * 3 + (r & 7)))
    extra = dot(spread, dembed).astype(bf16)
    dhead = acc_head[...].astype(bf16)

    def write(encoder_ref, trunk_ref):
        for s in range(SHARDS):
            for q in range(6):
                encoder_ref[s, 16 * q : 16 * q + 16, :] = acc_conv[q, 16 * s : 16 * s + 16, :].astype(bf16)
            encoder_ref[s, 96:104, :] = extra[8 * s : 8 * s + 8, :]
            for n in range(2):
                cols = slice(256 * n, 256 * n + 256)
                trunk_ref[s, 16 * n : 16 * n + 16, :] = acc_in[16 * s : 16 * s + 16, cols].astype(bf16)
                trunk_ref[s, 32 + 32 * n : 64 + 32 * n, :] = acc_mid[32 * s : 32 * s + 32, cols].astype(bf16)
            trunk_ref[s, 96:104, :] = jnp.zeros((8, 256), bf16)
            for n in range(2):
                trunk_ref[s, 96:104, 32 * n : 32 * n + 32] = dhead[8 * n : 8 * n + 8, 32 * s : 32 * s + 32]

    @pl.when(flags_ref[2] == 0)
    def _():
        write(keep_ref, give_ref)

    @pl.when(flags_ref[2] == 1)
    def _():
        write(give_ref, keep_ref)

    at = (iota((16, 128), 0) == iota((16, 128), 1)) & is_act
    line = jnp.sum(jnp.where(at, acc_stat[...], 0.0), axis=0, keepdims=True)
    stat_ref[...] = jnp.broadcast_to(line, (8, 128))


def member_grad(flags, recv, weights, scale, other):
    v = pltpu.VMEM
    half = ALL_ROWS // 2
    return pl.pallas_call(
        grad_kernel,
        out_shape=(
            jax.ShapeDtypeStruct((SHARDS, HALF, 256), bf16),
            jax.ShapeDtypeStruct((SHARDS, HALF, 256), bf16),
            jax.ShapeDtypeStruct((8, 128), f32),
        ),
        in_specs=[pl.BlockSpec(memory_space=pltpu.SMEM)] + [pl.BlockSpec(memory_space=v)] * 4,
        scratch_shapes=[
            v((half, 128), bf16), v((ROWS, 128), bf16), v((ROWS, CH), f32),
            v((PAD + ALL_ROWS, CH), bf16), v((PAD + ALL_ROWS, CH), bf16), v((PAD + ALL_ROWS, CH), bf16),
            v((ROWS, CH), bf16),
            v((ALL_ROWS, CH), bf16), v((ALL_ROWS, CH), bf16), v((ALL_ROWS, CH), bf16),
            v((ROWS, UNITS), bf16), v((ROWS, UNITS), bf16), v((16, ROWS), bf16),
            v((ROWS, UNITS), bf16), v((ROWS, UNITS), bf16),
            v((ALL_ROWS, CH), f32),
            v((ALL_ROWS + PAD, CH), bf16), v((ALL_ROWS + PAD, CH), bf16), v((ALL_ROWS + PAD, CH), bf16),
            v((half, 512), bf16),
            v((6, CH, CH), f32), v((CH, UNITS), f32), v((UNITS, UNITS), f32), v((16, UNITS), f32), v((16, 128), f32),
        ],
        cost_estimate=pl.CostEstimate(flops=11_200_000_000, bytes_accessed=4_000_000, transcendentals=4_000_000),
        compiler_params=pltpu.CompilerParams(vmem_limit_bytes=36 * 1024 * 1024),
        name="grad",
    )(flags, recv, weights, scale, other)


def reduce_kernel(flags_ref, recv_ref, stat_ref, mine_ref, theirs_ref, cast_ref):
    lane1 = iota((1, 128), 1)
    line = pltpu.roll(stat_ref[0:1, :], 32, 1)
    for whose, out_ref in ((flags_ref[2], mine_ref), (1 - flags_ref[2], theirs_ref)):
        for j in range(2):
            kind = 2 * whose + j
            total = recv_ref[kind].astype(f32)
            for z in range(1, 4):
                total = total + recv_ref[4 * z + kind].astype(f32)
            out_ref[j] = total
            line = line + jnp.where(lane1 == kind, jnp.sum(total * total), 0.0)
    for s in range(SHARDS):
        cast_ref[8 * s : 8 * s + 8, :] = jnp.broadcast_to(line, (8, 128))


def reduce_parts(flags, recv, stat):
    part = jax.ShapeDtypeStruct((2, HALF, 256), f32)
    return pl.pallas_call(
        reduce_kernel,
        out_shape=(part, part, jax.ShapeDtypeStruct((SHARDS * 8, 128), f32)),
        in_specs=[pl.BlockSpec(memory_space=pltpu.SMEM)] + [pl.BlockSpec(memory_space=pltpu.VMEM)] * 2,
        compiler_params=pltpu.CompilerParams(vmem_limit_bytes=16 * 1024 * 1024),
        name="reduce",
    )(flags, recv, stat)


def finish_kernel(flags_ref, mine_ref, theirs_ref, near_ref, far_ref, embed_ref, conv_ref, in_ref, mid_ref, head_ref, std_ref):
    core = flags_ref[2]
    lane1 = iota((1, 128), 1)
    total = jnp.sum(near_ref[...] + far_ref[...], axis=0, keepdims=True) * 0.125
    scales = []
    for j in range(2):
        kind = 2 * core + j
        std = jnp.zeros((1, 128), f32)
        for z in range(4):
            at = pl.ds(pl.multiple_of(8 * (4 * z + kind), 8), 8)
            std = std + near_ref[at, :][0:1] + far_ref[at, :][0:1]
        std = jnp.where((lane1 >= 32) & (lane1 < 32 + ACT), std, 0.0)
        square = jnp.sum(std * std + jnp.where(lane1 == kind, total, 0.0), axis=1, keepdims=True)
        scale = 1.0 / jnp.sqrt(square / ENTRIES + 1e-06)
        std_ref[j : j + 1, :] = (std * scale)[:, 32 : 32 + ACT]
        scales.append(scale)

    def write(encoder_ref, trunk_ref):
        for j, scale in enumerate(scales):
            for q in range(6):
                conv_ref[j, q // 2, q % 2] = encoder_ref[j, 16 * q : 16 * q + 16, :] * scale
            embed_ref[:, j, :] = encoder_ref[j, 96:99, :] * scale
            for n in range(2):
                cols = slice(256 * n, 256 * n + 256)
                in_ref[j, :, cols] = trunk_ref[j, 16 * n : 16 * n + 16, :] * scale
                mid_ref[j, :, cols] = trunk_ref[j, 32 + 32 * n : 64 + 32 * n, :] * scale
            head_ref[0:8, j, :] = trunk_ref[j, 96:104, 0:32] * scale
            head_ref[8:13, j, :] = trunk_ref[j, 96:101, 32:64] * scale

    @pl.when(core == 0)
    def _():
        write(mine_ref, theirs_ref)

    @pl.when(core == 1)
    def _():
        write(theirs_ref, mine_ref)


def finish(flags, mine, theirs, near, far):
    shapes = ((3, 2, 256), (2, 3, 2, 16, 256), (2, 16, 512), (2, 32, 512), (13, 2, 32), (2, 12))
    embed, conv, first, second, head, std = pl.pallas_call(
        finish_kernel,
        out_shape=tuple(jax.ShapeDtypeStruct(s, f32) for s in shapes),
        in_specs=[pl.BlockSpec(memory_space=pltpu.SMEM)] + [pl.BlockSpec(memory_space=pltpu.VMEM)] * 4,
        compiler_params=pltpu.CompilerParams(vmem_limit_bytes=16 * 1024 * 1024),
        name="finish",
    )(flags, mine, theirs, near, far)
    return embed.transpose(1, 0, 2), conv, first, second, head.transpose(1, 2, 0), std


def swap(value):
    return lax.ppermute(value, "core", [(0, 1), (1, 0)])


def local(observations, rollout, done_flags, member_ids, embed_weight, conv_weight, trunk_in, trunk_mid, head_weight, log_std):
    x, core = lax.axis_index("x"), lax.axis_index("core")
    own = core == x // 2
    flags = jnp.stack([x % 2, own.astype(jnp.int32), core]).astype(jnp.int32)
    packed = pack(observations, rollout, done_flags, member_ids)
    packed, flags = lax.optimization_barrier((packed, flags))
    recv = lax.all_to_all(packed, ("y", "x"), split_axis=0, concat_axis=0, tiled=True)
    weights = prepare(flags, embed_weight, conv_weight, trunk_in, trunk_mid, head_weight)
    weights = jnp.where(own, weights, swap(weights))
    keep, give, stat = member_grad(flags, recv, weights, log_std, swap(log_std))
    both = (keep.astype(f32) + swap(give).astype(f32)).astype(bf16)
    parts = lax.all_to_all(both, ("z", "x"), split_axis=0, concat_axis=0, tiled=True)
    mine, theirs, cast = reduce_parts(flags, parts, stat)
    near = lax.all_to_all(cast, ("z", "x"), split_axis=0, concat_axis=0, tiled=True)
    return finish(flags, mine, swap(theirs), near, swap(near))


def solution(mesh):
    fine = Mesh(mesh.devices.reshape(4, 2, 4, 4), ("y", "core", "z", "x"))
    member, dp = ("y", "core"), ("z", "x")
    every = member + dp
    return jax.shard_map(
        local,
        mesh=fine,
        in_specs=(P(every), P(every), P(every), P(every)) + (P(member),) * 6,
        out_specs=(
            P(member, dp),
            P(member, None, None, dp),
            P(member, dp),
            P(member, dp),
            P(member, dp),
            P(member),
        ),
        check_vma=False,
    )
```

time: 85.8 us -> 85.3 us (level)
  blocking collectives: 43.9 us -> 31.4 us
  waiting for transfers between devices: 0.96 us -> 12.4 us
  local copies, waits for them, and re-layouts: 7.08 us -> 0.01 us
  other arithmetic: 0 us -> 2.5 us
  Pallas kernels: 27 us -> 29.3 us
  starting transfers between devices: 5.61 us -> 7.63 us
    all_to_all x2, blocking collectives: 43.9 us -> 31.4 us  [the longest x1 20.9 us: local(): lax.all_to_all(both, ('z', 'x'), split_axis=0, concat_axis=0, tiled=True)]
    all_to_all x1, waiting for transfers between devices: 0.96 us -> 8.77 us  [local(): lax.all_to_all(packed, ('y', 'x'), split_axis=0, concat_axis=0, tiled=True)]
    unnamed x14 -> x4, local copies, waits for them, and re-layouts: 7.08 us -> 0.01 us
    pallas_call x1, Pallas kernels: 0.33 us -> 4.18 us  [prepare(): pl.pallas_call(weights_kernel, grid_spec=pltpu.PrefetchScalarGridSpec(num...]
    ppermute x0 -> x5, waiting for transfers between devices: none -> 3.63 us  [swap(): return lax.ppermute(value, 'core', [(0, 1), (1, 0)])]
    select_n x0 -> x1, other arithmetic: none -> 1.64 us  [local(): weights = jnp.where(own, weights, swap(weights))]
    all_to_all x1, starting transfers between devices: 5.61 us -> 7.14 us  [local(): lax.all_to_all(packed, ('y', 'x'), split_axis=0, concat_axis=0, tiled=True)]
    pallas_call x2, Pallas kernels: 21.7 us -> 20.5 us  [the longest x1 19.7 us: member_grad(): pl.pallas_call(grad_kernel, out_shape=(jax.ShapeDtypeStruct((SHARDS, HALF...]
  transfers between devices with their start and end apart: 1 -> 6, of which waited for: 1 -> 3; matrix products, arithmetic and copies ran while one was open for 0% -> 2% of each run, Pallas kernels for 0% -> 0%
where the time goes in v3:
time: 85.3 us; the launch traced here: 83.9 us
  blocking collectives  31.4 us (37%)
  Pallas kernels  29.3 us (34%)
  waiting for transfers between devices  12.4 us (15%)
  starting transfers between devices  7.63 us (9%)
  other arithmetic  2.5 us (3%)
    all_to_all x1, blocking collectives, local(): lax.all_to_all(both, ('z', 'x'), split_axis=0, concat_axis=0, tiled=True)  20.9 us
    pallas_call x1, Pallas kernels, member_grad(): pl.pallas_call(grad_kernel, out_shape=(jax.ShapeDtypeStruct((SHARDS, HALF...  19.7 us
    all_to_all x1, blocking collectives, local(): lax.all_to_all(cast, ('z', 'x'), split_axis=0, concat_axis=0, tiled=True)  10.5 us
    all_to_all x1, waiting for transfers between devices, local(): lax.all_to_all(packed, ('y', 'x'), split_axis=0, concat_axis=0, tiled=True)  8.77 us
    all_to_all x1, starting transfers between devices, local(): lax.all_to_all(packed, ('y', 'x'), split_axis=0, concat_axis=0, tiled=True)  7.14 us
    pallas_call x1, Pallas kernels, prepare(): pl.pallas_call(weights_kernel, grid_spec=pltpu.PrefetchScalarGridSpec(num...  4.18 us
    ppermute x5, waiting for transfers between devices, swap(): return lax.ppermute(value, 'core', [(0, 1), (1, 0)])  3.63 us
    pallas_call x1, Pallas kernels, pack(): pl.pallas_call(pack_kernel, out_shape=jax.ShapeDtypeStruct((MEMBERS * SLO...  3.01 us
  transfers between devices with their start and end apart: 6, of which 3 were waited for; matrix products, arithmetic and copies ran while one was open for 2% of the time, Pallas kernels for 0%

profile of v3, /device:TPU:0, one launch (start us, length us, event | category | flops | bytes accessed | tf_op | source)
XLA Modules:
  0.0 83.9 jit_solution(16968141463971083196)
XLA Ops:
  0.7 0.6 pad_add_fusion.which_ref.flags_ref
  1.2 3.0 %pack.1 = bf16[128,1536]{1,0:T(8,128)(2,1)} custom-call(bf16[32,1152]{1,0:T(8,128)(2,1)} %obs_ref.1, bf16[32,384]{1,0:T(8,128)(2,1)} %roll_ref.1, s32[24,32]{1,0:T(8,128)} %bitcast.17, s32[1,32]{1,0:T(1,128)} %bitcast.18), custom_call_target="tpu_custom_call" | custom-call | tf_op jit(solution)/shard_map/pack/pallas_call | solution.py:104
  4.3 4.2 %weights.1 = bf16[3360,256]{1,0:T(8,128)(2,1)} custom-call(s32[3]{0:T(128)} %pad_add_fusion.which_ref.flags_ref, f32[2,48,256]{2,1,0:T(8,128)} %embed_ref.1, f32[2,3,2,256,256]{4,3,2,1,0:T(8,128)} %conv_ref.1, f32[2,256,512]{2,1,0:T(8,128)} %in_ref.1, f32[2,512,512]{2,1,0:T(8,128)} %mid_ref.1, f32[13,2,512]{2,1,0:T(2,128)} %bitcast.16), custom_call_target="tpu_custom_call" | custom-call | bytes 5000000 | tf_op jit(solution)/shard_map/weights/pallas_call | solution.py:136
  8.4 0.0 collective-permute-start
  8.4 7.1 %all-to-all-start = ((bf16[16,8,1536]{2,1,0:T(8,128)(2,1)}), bf16[16,8,1536]{2,1,0:T(8,128)(2,1)S(1)}, u32[]{:S(2)}, u32[]{:S(2)}) async-start(bf16[16,8,1536]{2,1,0:T(8,128)(2,1)} %bitcast.5), calls=%async_computation | async-start | bytes 786432 | tf_op jit(solution)/shard_map/all_to_all | solution.py:435
  15.6 0.0 copy-start
  15.6 0.3 collective-permute-start.1
  15.9 0.0 collective-permute-done
  15.9 1.6 %broadcast_select_fusion.w_ref = bf16[3360,256]{1,0:T(8,128)(2,1)S(1)} fusion(bf16[3360,256]{1,0:T(8,128)(2,1)} %weights.1, bf16[3360,256]{1,0:T(8,128)(2,1)} %collective-permute-done, pred[]{:T(512)S(6)} %eq.5), kind=kLoop, calls=%fused_computation | loop fusion | flops 860160 | bytes 5160961 | tf_op jit(solution)/shard_map/jit(_where)/select_n | solution.py:437
  17.6 0.0 collective-permute-done.1.other_ref
  17.6 8.8 %all-to-all-done = bf16[16,8,1536]{2,1,0:T(8,128)(2,1)S(1)} async-done(((bf16[16,8,1536]{2,1,0:T(8,128)(2,1)}), bf16[16,8,1536]{2,1,0:T(8,128)(2,1)S(1)}, u32[]{:S(2)}, u32[]{:S(2)}) %all-to-all-start) | async-done | bytes 393248 | tf_op jit(solution)/shard_map/all_to_all | solution.py:435
  26.3 0.0 copy-done
  26.4 19.7 %grad.1 = (bf16[16,104,256]{2,1,0:T(8,128)(2,1)S(1)}, bf16[16,104,256]{2,1,0:T(8,128)(2,1)S(1)}, f32[8,128]{1,0:T(8,128)S(1)}) custom-call(s32[3]{0:T(128)S(1)} %copy-done, bf16[128,1536]{1,0:T(8,128)(2,1)S(1)} %bitcast.12, bf16[3360,256]{1,0:T(8,128)(2,1)S(1)} %broadcast_select_fusion.w_ref, f32[2,12]{1,0:T(2,128)S(1)} %copy-done.1, ...), custom_call_target="tpu_custom_call" | custom-call | flops 11200000000 | bytes 4000000 | tf_op jit(solution)/shard_map/grad/pallas_call | solution.py:323
  46.0 0.1 collective-permute-start.2
  46.1 2.4 %collective-permute-done.2 = bf16[16,104,256]{2,1,0:T(8,128)(2,1)S(1)} collective-permute-done((bf16[16,104,256]{2,1,0:T(8,128)(2,1)S(1)}, bf16[16,104,256]{2,1,0:T(8,128)(2,1)S(1)}, u32[]{:S(2)}, u32[]{:S(2)}) %collective-permute-start.2) | collective-permute-done | bytes 852000 | tf_op jit(solution)/shard_map/ppermute | solution.py:426
  48.5 0.3 add_convert_fusion
  48.8 20.9 %all_to_all.27.recv_ref = bf16[16,104,256]{2,1,0:T(8,128)(2,1)S(1)} all-to-all(bf16[16,104,256]{2,1,0:T(8,128)(2,1)S(1)} %add_convert_fusion), channel_id=1, replica_groups=mesh['y'=4,'core'=2,'z'=4,'x'=4] {'z','x'}, dimensions={0} | all-to-all | bytes 1703936 | tf_op jit(solution)/shard_map/all_to_all | solution.py:440
  69.6 0.8 reduce.1
  70.5 0.1 collective-permute-start.3
  70.6 10.5 %all_to_all.28 = f32[16,8,128]{2,1,0:T(8,128)S(1)} all-to-all(f32[16,8,128]{2,1,0:T(8,128)S(1)} %bitcast.15), channel_id=1, replica_groups=mesh['y'=4,'core'=2,'z'=4,'x'=4] {'z','x'}, dimensions={0} | all-to-all | bytes 131072 | tf_op jit(solution)/shard_map/all_to_all | solution.py:442
  81.1 0.0 collective-permute-start.4
  81.1 1.3 %collective-permute-done.4.far_ref = f32[128,128]{1,0:T(8,128)S(1)} collective-permute-done((f32[128,128]{1,0:T(8,128)S(1)}, f32[128,128]{1,0:T(8,128)S(1)}, u32[]{:S(2)}, u32[]{:S(2)}) %collective-permute-start.4) | collective-permute-done | bytes 65568 | tf_op jit(solution)/shard_map/ppermute | solution.py:426
  82.3 0.0 collective-permute-done.3.theirs_ref
  82.3 1.6 %finish.1 = (f32[3,2,256]{2,1,0:T(2,128)}, f32[2,3,2,16,256]{4,3,2,1,0:T(8,128)}, f32[2,16,512]{2,1,0:T(8,128)}, f32[2,32,512]{2,1,0:T(8,128)}, f32[13,2,32]{2,1,0:T(2,128)}, /*index=5*/f32[2,12]{1,0:T(2,128)}) custom-call(s32[3]{0:T(128)S(1)} %copy-done, f32[2,104,256]{2,1,0:T(8,128)S(1)} %get-tuple-element.25.mine_ref, ...), custom_call_target="tpu_custom_call" | custom-call | tf_op jit(solution)/shard_map/finish/pallas_call | solution.py:415
  (2 shorter events, 0.0 us)
Async XLA Ops:
  4.3 11.3 %copy-start.1 = (f32[2,12]{1,0:T(2,128)S(1)}, f32[2,12]{1,0:T(2,128)}, u32[]{:S(2)}) copy-start(f32[2,12]{1,0:T(2,128)} %scale_ref.1) | copy-start | bytes 292
  8.4 7.5 %collective-permute-start = (bf16[3360,256]{1,0:T(8,128)(2,1)}, bf16[3360,256]{1,0:T(8,128)(2,1)}, u32[]{:S(2)}, u32[]{:S(2)}) collective-permute-start(bf16[3360,256]{1,0:T(8,128)(2,1)} %weights.1), channel_id=1, source_target_pairs={{0,16},{16,0},{1,17},{17,1},{2,18},{18,2},{3,19},{19,3},{4,20},{20... | collective-permute-start | bytes 5160968 | tf_op jit(solution)/shard_map/ppermute | solution.py:426
  8.4 17.9 %all-to-all-start = ((bf16[16,8,1536]{2,1,0:T(8,128)(2,1)}), bf16[16,8,1536]{2,1,0:T(8,128)(2,1)S(1)}, u32[]{:S(2)}, u32[]{:S(2)}) async-start(bf16[16,8,1536]{2,1,0:T(8,128)(2,1)} %bitcast.5), calls=%async_computation | async-start | bytes 786432 | tf_op jit(solution)/shard_map/all_to_all | solution.py:435
  15.6 10.8 %copy-start = (s32[3]{0:T(128)S(1)}, s32[3]{0:T(128)}, u32[]{:S(2)}) copy-start(s32[3]{0:T(128)} %pad_add_fusion.which_ref.flags_ref) | copy-start | bytes 40
  15.6 2.0 %collective-permute-start.1 = (f32[2,12]{1,0:T(2,128)S(1)}, f32[2,12]{1,0:T(2,128)S(1)}, u32[]{:S(2)}, u32[]{:S(2)}) collective-permute-start(f32[2,12]{1,0:T(2,128)S(1)} %copy-done.1), channel_id=1, source_target_pairs={{0,16},{16,0},{1,17},{17,1},{2,18},{18,2},{3,19},{19,3},{4,20},{20... | collective-permute-start | bytes 296 | tf_op jit(solution)/shard_map/ppermute | solution.py:426
  46.0 2.5 %collective-permute-start.2 = (bf16[16,104,256]{2,1,0:T(8,128)(2,1)S(1)}, bf16[16,104,256]{2,1,0:T(8,128)(2,1)S(1)}, u32[]{:S(2)}, u32[]{:S(2)}) collective-permute-start(bf16[16,104,256]{2,1,0:T(8,128)(2,1)S(1)} %get-tuple-element.23), channel_id=1, source_target_pairs={{0,16},{16,0},{1,17},{17,1},{2,18},{18,2},{3,19},{19,3},{4,20},{20... | collective-permute-start | bytes 2555912 | tf_op jit(solution)/shard_map/ppermute | solution.py:426
  70.5 11.8 %collective-permute-start.3 = (f32[2,104,256]{2,1,0:T(8,128)S(1)}, f32[2,104,256]{2,1,0:T(8,128)S(1)}, u32[]{:S(2)}, u32[]{:S(2)}) collective-permute-start(f32[2,104,256]{2,1,0:T(8,128)S(1)} %get-tuple-element.26), channel_id=1, source_target_pairs={{0,16},{16,0},{1,17},{17,1},{2,18},{18,2},{3,19},{19,3},{4,20},{20... | collective-permute-start | bytes 638984 | tf_op jit(solution)/shard_map/ppermute | solution.py:426
  81.1 1.3 %collective-permute-start.4 = (f32[128,128]{1,0:T(8,128)S(1)}, f32[128,128]{1,0:T(8,128)S(1)}, u32[]{:S(2)}, u32[]{:S(2)}) collective-permute-start(f32[128,128]{1,0:T(8,128)S(1)} %bitcast.13), channel_id=1, source_target_pairs={{0,16},{16,0},{1,17},{17,1},{2,18},{18,2},{3,19},{19,3},{4,20},{20... | collective-permute-start | bytes 196616 | tf_op jit(solution)/shard_map/ppermute | solution.py:426

commit v4 on v3

--- a/solution.py
+++ b/solution.py
@@ -4,6 +4,7 @@
 from jax.experimental import pallas as pl
 from jax.experimental.pallas import tpu as pltpu
 from jax.sharding import Mesh, PartitionSpec as P
+
 
 gamma_rate = 0.99
 trace_rate = 0.95
@@ -108,40 +109,54 @@
     )(observations, rollout, done_flags.T, member_ids.T)
 
 
-def weights_kernel(which_ref, embed_ref, conv_ref, in_ref, mid_ref, head_ref, out_ref):
+def weights_kernel(
+    which_ref, embed_hbm, conv_hbm, in_hbm, mid_hbm, head_hbm, out_ref,
+    embed_ref, conv_ref, in_ref, mid_ref, head_ref, sems,
+):
+    which = which_ref[0]
+    moves = [
+        pltpu.make_async_copy(conv_hbm.at[which, layer], conv_ref.at[layer], sems.at[layer]) for layer in range(3)
+    ]
+    moves.append(pltpu.make_async_copy(mid_hbm.at[which], mid_ref, sems.at[3]))
+    moves.append(pltpu.make_async_copy(in_hbm.at[which], in_ref, sems.at[4]))
+    moves.append(pltpu.make_async_copy(embed_hbm.at[which], embed_ref, sems.at[5]))
+    moves.append(pltpu.make_async_copy(head_hbm, head_ref, sems.at[6]))
+    for move in moves:
+        move.start()
     for layer in range(3):
+        moves[layer].wait()
         for tap in range(2):
             at = CH * (2 * layer + tap)
-            out_ref[at : at + CH, :] = conv_ref[0, layer, tap].astype(bf16)
-    head = jnp.where(which_ref[0] == 0, head_ref[:, 0, :], head_ref[:, 1, :]).astype(bf16)
-    head = dot(onehot(iota((16, ACT + 1), 0) == iota((16, ACT + 1), 1)), head).astype(bf16)
-    embed = embed_ref[0].astype(bf16)
+            out_ref[at : at + CH, :] = conv_ref[layer, tap].astype(bf16)
+    halves = (slice(0, 256), slice(256, 512))
+    moves[3].wait()
+    for n in range(2):
+        out_ref[W_MID + UNITS * n : W_MID + UNITS * n + UNITS, :] = mid_ref[:, halves[n]].astype(bf16)
+    moves[4].wait()
+    for n in range(2):
+        out_ref[W_IN + CH * n : W_IN + CH * n + CH, :] = in_ref[:, halves[n]].astype(bf16)
+    moves[5].wait()
+    embed = embed_ref[...].astype(bf16)
     r, k = iota((128, OBS), 0), iota((128, OBS), 1)
     for n in range(2):
-        cols = slice(256 * n, 256 * n + 256)
-        out_ref[W_IN + CH * n : W_IN + CH * n + CH, :] = in_ref[0, :, cols].astype(bf16)
-        out_ref[W_MID + UNITS * n : W_MID + UNITS * n + UNITS, :] = mid_ref[0, :, cols].astype(bf16)
         out_ref[W_EMBED + 128 * n : W_EMBED + 128 * n + 128, :] = dot(onehot(r == k + REC * n), embed).astype(bf16)
-        out_ref[W_HEAD + 16 * n : W_HEAD + 16 * n + 16, :] = head[:, cols]
+    moves[6].wait()
+    head = jnp.where(which == 0, head_ref[:, 0, :], head_ref[:, 1, :]).astype(bf16)
+    head = dot(onehot(iota((16, ACT + 1), 0) == iota((16, ACT + 1), 1)), head).astype(bf16)
+    for n in range(2):
+        out_ref[W_HEAD + 16 * n : W_HEAD + 16 * n + 16, :] = head[:, halves[n]]
 
 
 def prepare(which, embed, conv, trunk_in, trunk_mid, head):
-    def one(shape):
-        return pl.BlockSpec((1,) + shape, lambda i, w: (w[0],) + (0,) * len(shape))
-
-    def whole(shape):
-        return pl.BlockSpec(shape, lambda i, w: (0,) * len(shape))
-
     head = head.transpose(2, 0, 1)
+    v = pltpu.VMEM
     return pl.pallas_call(
         weights_kernel,
-        grid_spec=pltpu.PrefetchScalarGridSpec(
-            num_scalar_prefetch=1,
-            grid=(1,),
-            in_specs=[one(x.shape[1:]) for x in (embed, conv, trunk_in, trunk_mid)] + [whole(head.shape)],
-            out_specs=whole((W_ROWS, CH)),
-        ),
+        in_specs=[pl.BlockSpec(memory_space=pltpu.SMEM)] + [pl.BlockSpec(memory_space=pltpu.HBM)] * 5,
+        out_specs=pl.BlockSpec(memory_space=v),
         out_shape=jax.ShapeDtypeStruct((W_ROWS, CH), bf16),
+        scratch_shapes=[v(x.shape[1:], f32) for x in (embed, conv, trunk_in, trunk_mid)]
+        + [v(head.shape, f32), pltpu.SemaphoreType.DMA((7,))],
         cost_estimate=pl.CostEstimate(flops=0, bytes_accessed=5_000_000, transcendentals=0),
         compiler_params=pltpu.CompilerParams(vmem_limit_bytes=60 * 1024 * 1024),
         name="weights",
@@ -149,11 +164,12 @@
 
 
 def grad_kernel(
-    flags_ref, recv_ref, w_ref, scale_ref, other_ref,
+    which_ref, own_ref, core_ref, recv_ref, w_ref, scale_ref, other_ref,
     keep_ref, give_ref, stat_ref,
     xc, xt, hid, c0, c1, c2, c3, g0, g1, g2, first, second, dout, dp2, dp1, dhid, dm0, dm1, dm2, dpair,
     acc_conv, acc_in, acc_mid, acc_head, acc_stat,
 ):
+    own = own_ref[0] == 1
     cs, gs, dms = (c0, c1, c2), (g0, g1, g2), (dm0, dm1, dm2)
     for ref in cs:
         ref[0:PAD, :] = jnp.zeros((PAD, CH), bf16)
@@ -169,8 +185,8 @@
     select = onehot((entry < 16) & (k == entry + OBS + (r >> 5) * REC))
     sub = iota((16, 1), 0)
     is_act = sub < ACT
-    scale = jnp.where(flags_ref[1] == 1, scale_ref[...], other_ref[...])
-    scale = jnp.where(flags_ref[0] == 0, scale[0:1, :], scale[1:2, :])
+    scale = jnp.where(own, scale_ref[...], other_ref[...])
+    scale = jnp.where(which_ref[0] == 0, scale[0:1, :], scale[1:2, :])
     log_scale = jnp.sum(jnp.where(iota((16, ACT), 0) == iota((16, ACT), 1), scale, 0.0), axis=1, keepdims=True)
     conv = [w_ref.at[2 * CH * layer : 2 * CH * layer + 2 * CH] for layer in range(3)]
     in_half = [w_ref.at[W_IN + CH * n : W_IN + CH * n + CH] for n in range(2)]
@@ -180,6 +196,7 @@
 
     def across(halves, rows):
         return jnp.concatenate([half[rows, :] for half in halves], axis=1)
+
     inverse = jnp.where(is_act, jnp.exp(-log_scale), 0.0)
     offset = jnp.sum(jnp.where(is_act, log_scale, 0.0), axis=0, keepdims=True) + ACT * half_log_tau
     lane = iota((1, ROWS), 1)
@@ -304,11 +321,11 @@
             for n in range(2):
                 trunk_ref[s, 96:104, 32 * n : 32 * n + 32] = dhead[8 * n : 8 * n + 8, 32 * s : 32 * s + 32]
 
-    @pl.when(flags_ref[2] == 0)
+    @pl.when(core_ref[0] == 0)
     def _():
         write(keep_ref, give_ref)
 
-    @pl.when(flags_ref[2] == 1)
+    @pl.when(core_ref[0] == 1)
     def _():
         write(give_ref, keep_ref)
 
@@ -317,7 +334,7 @@
     stat_ref[...] = jnp.broadcast_to(line, (8, 128))
 
 
-def member_grad(flags, recv, weights, scale, other):
+def member_grad(which, own, core, recv, weights, scale, other):
     v = pltpu.VMEM
     half = ALL_ROWS // 2
     return pl.pallas_call(
@@ -327,7 +344,7 @@
             jax.ShapeDtypeStruct((SHARDS, HALF, 256), bf16),
             jax.ShapeDtypeStruct((8, 128), f32),
         ),
-        in_specs=[pl.BlockSpec(memory_space=pltpu.SMEM)] + [pl.BlockSpec(memory_space=v)] * 4,
+        in_specs=[pl.BlockSpec(memory_space=pltpu.SMEM)] * 3 + [pl.BlockSpec(memory_space=v)] * 4,
         scratch_shapes=[
             v((half, 128), bf16), v((ROWS, 128), bf16), v((ROWS, CH), f32),
             v((PAD + ALL_ROWS, CH), bf16), v((PAD + ALL_ROWS, CH), bf16), v((PAD + ALL_ROWS, CH), bf16),
@@ -341,15 +358,15 @@
             v((6, CH, CH), f32), v((CH, UNITS), f32), v((UNITS, UNITS), f32), v((16, UNITS), f32), v((16, 128), f32),
         ],
         cost_estimate=pl.CostEstimate(flops=11_200_000_000, bytes_accessed=4_000_000, transcendentals=4_000_000),
-        compiler_params=pltpu.CompilerParams(vmem_limit_bytes=36 * 1024 * 1024),
+        compiler_params=pltpu.CompilerParams(vmem_limit_bytes=34 * 1024 * 1024),
         name="grad",
-    )(flags, recv, weights, scale, other)
-
-
-def reduce_kernel(flags_ref, recv_ref, stat_ref, mine_ref, theirs_ref, cast_ref):
+    )(which, own, core, recv, weights, scale, other)
+
+
+def reduce_kernel(core_ref, recv_ref, stat_ref, mine_ref, theirs_ref, cast_ref):
     lane1 = iota((1, 128), 1)
     line = pltpu.roll(stat_ref[0:1, :], 32, 1)
-    for whose, out_ref in ((flags_ref[2], mine_ref), (1 - flags_ref[2], theirs_ref)):
+    for whose, out_ref in ((core_ref[0], mine_ref), (1 - core_ref[0], theirs_ref)):
         for j in range(2):
             kind = 2 * whose + j
             total = recv_ref[kind].astype(f32)
@@ -361,7 +378,7 @@
         cast_ref[8 * s : 8 * s + 8, :] = jnp.broadcast_to(line, (8, 128))
 
 
-def reduce_parts(flags, recv, stat):
+def reduce_parts(core, recv, stat):
     part = jax.ShapeDtypeStruct((2, HALF, 256), f32)
     return pl.pallas_call(
         reduce_kernel,
@@ -369,11 +386,11 @@
         in_specs=[pl.BlockSpec(memory_space=pltpu.SMEM)] + [pl.BlockSpec(memory_space=pltpu.VMEM)] * 2,
         compiler_params=pltpu.CompilerParams(vmem_limit_bytes=16 * 1024 * 1024),
         name="reduce",
-    )(flags, recv, stat)
-
-
-def finish_kernel(flags_ref, mine_ref, theirs_ref, near_ref, far_ref, embed_ref, conv_ref, in_ref, mid_ref, head_ref, std_ref):
-    core = flags_ref[2]
+    )(core, recv, stat)
+
+
+def finish_kernel(core_ref, mine_ref, theirs_ref, near_ref, far_ref, embed_ref, conv_ref, in_ref, mid_ref, head_ref, std_ref):
+    core = core_ref[0]
     lane1 = iota((1, 128), 1)
     total = jnp.sum(near_ref[...] + far_ref[...], axis=0, keepdims=True) * 0.125
     scales = []
@@ -410,7 +427,7 @@
         write(theirs_ref, mine_ref)
 
 
-def finish(flags, mine, theirs, near, far):
+def finish(core, mine, theirs, near, far):
     shapes = ((3, 2, 256), (2, 3, 2, 16, 256), (2, 16, 512), (2, 32, 512), (13, 2, 32), (2, 12))
     embed, conv, first, second, head, std = pl.pallas_call(
         finish_kernel,
@@ -418,7 +435,7 @@
         in_specs=[pl.BlockSpec(memory_space=pltpu.SMEM)] + [pl.BlockSpec(memory_space=pltpu.VMEM)] * 4,
         compiler_params=pltpu.CompilerParams(vmem_limit_bytes=16 * 1024 * 1024),
         name="finish",
-    )(flags, mine, theirs, near, far)
+    )(core, mine, theirs, near, far)
     return embed.transpose(1, 0, 2), conv, first, second, head.transpose(1, 2, 0), std
 
 
@@ -428,19 +445,18 @@
 
 def local(observations, rollout, done_flags, member_ids, embed_weight, conv_weight, trunk_in, trunk_mid, head_weight, log_std):
     x, core = lax.axis_index("x"), lax.axis_index("core")
-    own = core == x // 2
-    flags = jnp.stack([x % 2, own.astype(jnp.int32), core]).astype(jnp.int32)
+    which, own = (x % 2).reshape(1), (core == x // 2).astype(jnp.int32).reshape(1)
+    core = core.reshape(1)
     packed = pack(observations, rollout, done_flags, member_ids)
-    packed, flags = lax.optimization_barrier((packed, flags))
     recv = lax.all_to_all(packed, ("y", "x"), split_axis=0, concat_axis=0, tiled=True)
-    weights = prepare(flags, embed_weight, conv_weight, trunk_in, trunk_mid, head_weight)
-    weights = jnp.where(own, weights, swap(weights))
-    keep, give, stat = member_grad(flags, recv, weights, log_std, swap(log_std))
+    weights = prepare(which, embed_weight, conv_weight, trunk_in, trunk_mid, head_weight)
+    weights = jnp.where(own[0] == 1, weights, swap(weights))
+    keep, give, stat = member_grad(which, own, core, recv, weights, log_std, swap(log_std))
     both = (keep.astype(f32) + swap(give).astype(f32)).astype(bf16)
     parts = lax.all_to_all(both, ("z", "x"), split_axis=0, concat_axis=0, tiled=True)
-    mine, theirs, cast = reduce_parts(flags, parts, stat)
+    mine, theirs, cast = reduce_parts(core, parts, stat)
     near = lax.all_to_all(cast, ("z", "x"), split_axis=0, concat_axis=0, tiled=True)
-    return finish(flags, mine, swap(theirs), near, swap(near))
+    return finish(core, mine, swap(theirs), near, swap(near))
 
 
 def solution(mesh):

time: 85.3 us -> 82.6 us (0.968)
  Pallas kernels: 29.3 us -> 27 us
  transfers between devices with their start and end apart: 6 -> 6, of which waited for: 3 -> 3; matrix products, arithmetic and copies ran while one was open for 2% -> 2% of each run, Pallas kernels for 0% -> 4%
where the time goes in v4:
time: 82.6 us; the launch traced here: 81.1 us
  blocking collectives  31.3 us (38%)
  Pallas kernels  27 us (33%)
  waiting for transfers between devices  12.4 us (15%)
  starting transfers between devices  7.71 us (9%)
  other arithmetic  1.91 us (2%)
    all_to_all x1, blocking collectives, local(): lax.all_to_all(both, ('z', 'x'), split_axis=0, concat_axis=0, tiled=True)  20.8 us
    pallas_call x1, Pallas kernels, member_grad(): pl.pallas_call(grad_kernel, out_shape=(jax.ShapeDtypeStruct((SHARDS, HALF...  19.3 us
    all_to_all x1, blocking collectives, local(): lax.all_to_all(cast, ('z', 'x'), split_axis=0, concat_axis=0, tiled=True)  10.5 us
    all_to_all x1, waiting for transfers between devices, local(): lax.all_to_all(packed, ('y', 'x'), split_axis=0, concat_axis=0, tiled=True)  8.78 us
    all_to_all x1, starting transfers between devices, local(): lax.all_to_all(packed, ('y', 'x'), split_axis=0, concat_axis=0, tiled=True)  7.16 us
    ppermute x5, waiting for transfers between devices, swap(): return lax.ppermute(value, 'core', [(0, 1), (1, 0)])  3.63 us
    pallas_call x1, Pallas kernels, prepare(): pl.pallas_call(weights_kernel, in_specs=[pl.BlockSpec(memory_space=pltpu....  3.48 us
    pallas_call x1, Pallas kernels, pack(): pl.pallas_call(pack_kernel, out_shape=jax.ShapeDtypeStruct((MEMBERS * SLO...  3.01 us
  transfers between devices with their start and end apart: 6, of which 3 were waited for; matrix products, arithmetic and copies ran while one was open for 2% of the time, Pallas kernels for 4%

profile of v4, /device:TPU:0, one launch (start us, length us, event | category | flops | bytes accessed | tf_op | source)
XLA Modules:
  0.0 81.1 jit_solution(1447361059531321170)
XLA Ops:
  0.6 0.0 copy-start
  0.7 3.5 %weights.1 = bf16[3360,256]{1,0:T(8,128)(2,1)} custom-call(s32[1]{0:T(128)} %bitcast.1.which_ref, f32[2,48,256]{2,1,0:T(8,128)} %embed_hbm.1, f32[2,3,2,256,256]{4,3,2,1,0:T(8,128)} %conv_hbm.1, f32[2,256,512]{2,1,0:T(8,128)} %in_hbm.1, f32[2,512,512]{2,1,0:T(8,128)} %mid_hbm.1, f32[13,2,512]{2,1,0:T(2,128)} %bitcast.17), custom_call_target="tpu_custom_call" | custom-call | bytes 5000000 | tf_op jit(solution)/shard_map/weights/pallas_call | solution.py:153
  4.1 0.1 collective-permute-start
  4.2 3.0 %pack.1 = bf16[128,1536]{1,0:T(8,128)(2,1)} custom-call(bf16[32,1152]{1,0:T(8,128)(2,1)} %obs_ref.1, bf16[32,384]{1,0:T(8,128)(2,1)} %roll_ref.1, s32[24,32]{1,0:T(8,128)} %bitcast.18, s32[1,32]{1,0:T(1,128)} %bitcast.19), custom_call_target="tpu_custom_call" | custom-call | tf_op jit(solution)/shard_map/pack/pallas_call | solution.py:105
  7.3 7.2 %all-to-all-start = ((bf16[16,8,1536]{2,1,0:T(8,128)(2,1)}), bf16[16,8,1536]{2,1,0:T(8,128)(2,1)S(1)}, u32[]{:S(2)}, u32[]{:S(2)}) async-start(bf16[16,8,1536]{2,1,0:T(8,128)(2,1)} %bitcast.16), calls=%async_computation | async-start | bytes 786432 | tf_op jit(solution)/shard_map/all_to_all | solution.py:451
  14.4 0.0 copy-done
  14.4 0.3 collective-permute-start.1
  14.7 0.0 collective-permute-done
  14.7 1.6 %broadcast_select_fusion.w_ref = bf16[3360,256]{1,0:T(8,128)(2,1)S(1)} fusion(bf16[3360,256]{1,0:T(8,128)(2,1)} %weights.1, bf16[3360,256]{1,0:T(8,128)(2,1)} %collective-permute-done, pred[]{:T(512)S(6)} %eq.9), kind=kLoop, calls=%fused_computation | loop fusion | flops 860160 | bytes 5160961 | tf_op jit(solution)/shard_map/jit(_where)/select_n | solution.py:453
  16.4 0.0 collective-permute-done.1.other_ref
  16.4 8.8 %all-to-all-done = bf16[16,8,1536]{2,1,0:T(8,128)(2,1)S(1)} async-done(((bf16[16,8,1536]{2,1,0:T(8,128)(2,1)}), bf16[16,8,1536]{2,1,0:T(8,128)(2,1)S(1)}, u32[]{:S(2)}, u32[]{:S(2)}) %all-to-all-start) | async-done | bytes 393248 | tf_op jit(solution)/shard_map/all_to_all | solution.py:451
  25.2 19.3 %grad.1 = (bf16[16,104,256]{2,1,0:T(8,128)(2,1)S(1)}, bf16[16,104,256]{2,1,0:T(8,128)(2,1)S(1)}, f32[8,128]{1,0:T(8,128)S(1)}) custom-call(s32[1]{0:T(128)} %bitcast.1.which_ref, s32[1]{0:T(128)} %bitcast.2.own_ref, s32[1]{0:T(128)} %bitcast.core_ref, bf16[128,1536]{1,0:T(8,128)(2,1)S(1)} %bitcast.12, bf16[3360,256]{1,0:T(8,128)(2,1)S(1)} %broadcast_select_fusion.w_ref, ...), custom_call_target="tpu_custom_call" | custom-call | flops 11200000000 | bytes 4000000 | tf_op jit(solution)/shard_map/grad/pallas_call | solution.py:340
  44.4 0.1 collective-permute-start.2
  44.5 2.4 %collective-permute-done.2 = bf16[16,104,256]{2,1,0:T(8,128)(2,1)S(1)} collective-permute-done((bf16[16,104,256]{2,1,0:T(8,128)(2,1)S(1)}, bf16[16,104,256]{2,1,0:T(8,128)(2,1)S(1)}, u32[]{:S(2)}, u32[]{:S(2)}) %collective-permute-start.2) | collective-permute-done | bytes 852000 | tf_op jit(solution)/shard_map/ppermute | solution.py:443
  46.9 0.3 add_convert_fusion
  47.1 20.8 %all_to_all.27.recv_ref = bf16[16,104,256]{2,1,0:T(8,128)(2,1)S(1)} all-to-all(bf16[16,104,256]{2,1,0:T(8,128)(2,1)S(1)} %add_convert_fusion), channel_id=1, replica_groups=mesh['y'=4,'core'=2,'z'=4,'x'=4] {'z','x'}, dimensions={0} | all-to-all | bytes 1703936 | tf_op jit(solution)/shard_map/all_to_all | solution.py:456
  68.0 0.3 reduce.1
  68.3 0.1 collective-permute-start.3
  68.4 10.5 %all_to_all.28 = f32[16,8,128]{2,1,0:T(8,128)S(1)} all-to-all(f32[16,8,128]{2,1,0:T(8,128)S(1)} %bitcast.15), channel_id=1, replica_groups=mesh['y'=4,'core'=2,'z'=4,'x'=4] {'z','x'}, dimensions={0} | all-to-all | bytes 131072 | tf_op jit(solution)/shard_map/all_to_all | solution.py:458
  78.9 0.0 collective-permute-start.4
  78.9 1.3 %collective-permute-done.4.far_ref = f32[128,128]{1,0:T(8,128)S(1)} collective-permute-done((f32[128,128]{1,0:T(8,128)S(1)}, f32[128,128]{1,0:T(8,128)S(1)}, u32[]{:S(2)}, u32[]{:S(2)}) %collective-permute-start.4) | collective-permute-done | bytes 65568 | tf_op jit(solution)/shard_map/ppermute | solution.py:443
  80.1 0.0 collective-permute-done.3.theirs_ref
  80.1 1.0 %finish.1 = (f32[3,2,256]{2,1,0:T(2,128)}, f32[2,3,2,16,256]{4,3,2,1,0:T(8,128)}, f32[2,16,512]{2,1,0:T(8,128)}, f32[2,32,512]{2,1,0:T(8,128)}, f32[13,2,32]{2,1,0:T(2,128)}, /*index=5*/f32[2,12]{1,0:T(2,128)}) custom-call(s32[1]{0:T(128)} %bitcast.core_ref, f32[2,104,256]{2,1,0:T(8,128)S(1)} %get-tuple-element.21.mine_ref, ...), custom_call_target="tpu_custom_call" | custom-call | tf_op jit(solution)/shard_map/finish/pallas_call | solution.py:432
Async XLA Ops:
  0.6 13.8 %copy-start = (f32[2,12]{1,0:T(2,128)S(1)}, f32[2,12]{1,0:T(2,128)}, u32[]{:S(2)}) copy-start(f32[2,12]{1,0:T(2,128)} %scale_ref.1) | copy-start | bytes 292
  4.1 10.6 %collective-permute-start = (bf16[3360,256]{1,0:T(8,128)(2,1)}, bf16[3360,256]{1,0:T(8,128)(2,1)}, u32[]{:S(2)}, u32[]{:S(2)}) collective-permute-start(bf16[3360,256]{1,0:T(8,128)(2,1)} %weights.1), channel_id=1, source_target_pairs={{0,16},{16,0},{1,17},{17,1},{2,18},{18,2},{3,19},{19,3},{4,20},{20... | collective-permute-start | bytes 5160968 | tf_op jit(solution)/shard_map/ppermute | solution.py:443
  7.3 17.9 %all-to-all-start = ((bf16[16,8,1536]{2,1,0:T(8,128)(2,1)}), bf16[16,8,1536]{2,1,0:T(8,128)(2,1)S(1)}, u32[]{:S(2)}, u32[]{:S(2)}) async-start(bf16[16,8,1536]{2,1,0:T(8,128)(2,1)} %bitcast.16), calls=%async_computation | async-start | bytes 786432 | tf_op jit(solution)/shard_map/all_to_all | solution.py:451
  14.4 1.9 %collective-permute-start.1 = (f32[2,12]{1,0:T(2,128)S(1)}, f32[2,12]{1,0:T(2,128)S(1)}, u32[]{:S(2)}, u32[]{:S(2)}) collective-permute-start(f32[2,12]{1,0:T(2,128)S(1)} %copy-done), channel_id=1, source_target_pairs={{0,16},{16,0},{1,17},{17,1},{2,18},{18,2},{3,19},{19,3},{4,20},{20... | collective-permute-start | bytes 296 | tf_op jit(solution)/shard_map/ppermute | solution.py:443
  44.4 2.5 %collective-permute-start.2 = (bf16[16,104,256]{2,1,0:T(8,128)(2,1)S(1)}, bf16[16,104,256]{2,1,0:T(8,128)(2,1)S(1)}, u32[]{:S(2)}, u32[]{:S(2)}) collective-permute-start(bf16[16,104,256]{2,1,0:T(8,128)(2,1)S(1)} %get-tuple-element.19), channel_id=1, source_target_pairs={{0,16},{16,0},{1,17},{17,1},{2,18},{18,2},{3,19},{19,3},{4,20},{20... | collective-permute-start | bytes 2555912 | tf_op jit(solution)/shard_map/ppermute | solution.py:443
  68.3 11.8 %collective-permute-start.3 = (f32[2,104,256]{2,1,0:T(8,128)S(1)}, f32[2,104,256]{2,1,0:T(8,128)S(1)}, u32[]{:S(2)}, u32[]{:S(2)}) collective-permute-start(f32[2,104,256]{2,1,0:T(8,128)S(1)} %get-tuple-element.22), channel_id=1, source_target_pairs={{0,16},{16,0},{1,17},{17,1},{2,18},{18,2},{3,19},{19,3},{4,20},{20... | collective-permute-start | bytes 638984 | tf_op jit(solution)/shard_map/ppermute | solution.py:443
  78.9 1.3 %collective-permute-start.4 = (f32[128,128]{1,0:T(8,128)S(1)}, f32[128,128]{1,0:T(8,128)S(1)}, u32[]{:S(2)}, u32[]{:S(2)}) collective-permute-start(f32[128,128]{1,0:T(8,128)S(1)} %bitcast.13), channel_id=1, source_target_pairs={{0,16},{16,0},{1,17},{17,1},{2,18},{18,2},{3,19},{19,3},{4,20},{20... | collective-permute-start | bytes 196616 | tf_op jit(solution)/shard_map/ppermute | solution.py:443

commit v5 on v4

--- a/solution.py
+++ b/solution.py
@@ -30,7 +30,8 @@
 PAD = 4 * SPANS
 SHARDS = 16
 HALF = 104
-W_IN, W_MID, W_EMBED, W_HEAD, W_ROWS = 1536, 2048, 3072, 3328, 3360
+CONV_ROWS = 1536
+W_IN, W_MID, W_EMBED, W_HEAD, W_ROWS = 0, 512, 1536, 1792, 1824
 f32 = jnp.float32
 bf16 = jnp.bfloat16
 
@@ -109,18 +110,10 @@
     )(observations, rollout, done_flags.T, member_ids.T)
 
 
-def weights_kernel(
-    which_ref, embed_hbm, conv_hbm, in_hbm, mid_hbm, head_hbm, out_ref,
-    embed_ref, conv_ref, in_ref, mid_ref, head_ref, sems,
-):
-    which = which_ref[0]
+def conv_weights_kernel(which_ref, conv_hbm, out_ref, conv_ref, sems):
     moves = [
-        pltpu.make_async_copy(conv_hbm.at[which, layer], conv_ref.at[layer], sems.at[layer]) for layer in range(3)
+        pltpu.make_async_copy(conv_hbm.at[which_ref[0], layer], conv_ref.at[layer], sems.at[layer]) for layer in range(3)
     ]
-    moves.append(pltpu.make_async_copy(mid_hbm.at[which], mid_ref, sems.at[3]))
-    moves.append(pltpu.make_async_copy(in_hbm.at[which], in_ref, sems.at[4]))
-    moves.append(pltpu.make_async_copy(embed_hbm.at[which], embed_ref, sems.at[5]))
-    moves.append(pltpu.make_async_copy(head_hbm, head_ref, sems.at[6]))
     for move in moves:
         move.start()
     for layer in range(3):
@@ -128,43 +121,55 @@
         for tap in range(2):
             at = CH * (2 * layer + tap)
             out_ref[at : at + CH, :] = conv_ref[layer, tap].astype(bf16)
+
+
+def trunk_weights_kernel(
+    which_ref, embed_hbm, in_hbm, mid_hbm, head_hbm, out_ref,
+    embed_ref, in_ref, mid_ref, head_ref, sems,
+):
+    which = which_ref[0]
+    moves = [
+        pltpu.make_async_copy(head_hbm, head_ref, sems.at[0]),
+        pltpu.make_async_copy(embed_hbm.at[which], embed_ref, sems.at[1]),
+        pltpu.make_async_copy(in_hbm.at[which], in_ref, sems.at[2]),
+        pltpu.make_async_copy(mid_hbm.at[which], mid_ref, sems.at[3]),
+    ]
+    for move in moves:
+        move.start()
     halves = (slice(0, 256), slice(256, 512))
-    moves[3].wait()
+    moves[0].wait()
+    head = jnp.where(which == 0, head_ref[:, 0, :], head_ref[:, 1, :]).astype(bf16)
+    head = dot(onehot(iota((16, ACT + 1), 0) == iota((16, ACT + 1), 1)), head).astype(bf16)
     for n in range(2):
-        out_ref[W_MID + UNITS * n : W_MID + UNITS * n + UNITS, :] = mid_ref[:, halves[n]].astype(bf16)
-    moves[4].wait()
-    for n in range(2):
-        out_ref[W_IN + CH * n : W_IN + CH * n + CH, :] = in_ref[:, halves[n]].astype(bf16)
-    moves[5].wait()
+        out_ref[W_HEAD + 16 * n : W_HEAD + 16 * n + 16, :] = head[:, halves[n]]
+    moves[1].wait()
     embed = embed_ref[...].astype(bf16)
     r, k = iota((128, OBS), 0), iota((128, OBS), 1)
     for n in range(2):
         out_ref[W_EMBED + 128 * n : W_EMBED + 128 * n + 128, :] = dot(onehot(r == k + REC * n), embed).astype(bf16)
-    moves[6].wait()
-    head = jnp.where(which == 0, head_ref[:, 0, :], head_ref[:, 1, :]).astype(bf16)
-    head = dot(onehot(iota((16, ACT + 1), 0) == iota((16, ACT + 1), 1)), head).astype(bf16)
+    moves[2].wait()
     for n in range(2):
-        out_ref[W_HEAD + 16 * n : W_HEAD + 16 * n + 16, :] = head[:, halves[n]]
-
-
-def prepare(which, embed, conv, trunk_in, trunk_mid, head):
-    head = head.transpose(2, 0, 1)
+        out_ref[W_IN + CH * n : W_IN + CH * n + CH, :] = in_ref[:, halves[n]].astype(bf16)
+    moves[3].wait()
+    for n in range(2):
+        out_ref[W_MID + UNITS * n : W_MID + UNITS * n + UNITS, :] = mid_ref[:, halves[n]].astype(bf16)
+
+
+def prepare(kernel, rows, which, arrays, shapes):
     v = pltpu.VMEM
     return pl.pallas_call(
-        weights_kernel,
-        in_specs=[pl.BlockSpec(memory_space=pltpu.SMEM)] + [pl.BlockSpec(memory_space=pltpu.HBM)] * 5,
+        kernel,
+        in_specs=[pl.BlockSpec(memory_space=pltpu.SMEM)] + [pl.BlockSpec(memory_space=pltpu.HBM)] * len(arrays),
         out_specs=pl.BlockSpec(memory_space=v),
-        out_shape=jax.ShapeDtypeStruct((W_ROWS, CH), bf16),
-        scratch_shapes=[v(x.shape[1:], f32) for x in (embed, conv, trunk_in, trunk_mid)]
-        + [v(head.shape, f32), pltpu.SemaphoreType.DMA((7,))],
-        cost_estimate=pl.CostEstimate(flops=0, bytes_accessed=5_000_000, transcendentals=0),
+        out_shape=jax.ShapeDtypeStruct((rows, CH), bf16),
+        scratch_shapes=[v(shape, f32) for shape in shapes] + [pltpu.SemaphoreType.DMA((4,))],
+        cost_estimate=pl.CostEstimate(flops=0, bytes_accessed=2_500_000, transcendentals=0),
         compiler_params=pltpu.CompilerParams(vmem_limit_bytes=60 * 1024 * 1024),
-        name="weights",
-    )(which, embed, conv, trunk_in, trunk_mid, head)
+    )(which, *arrays)
 
 
 def grad_kernel(
-    which_ref, own_ref, core_ref, recv_ref, w_ref, scale_ref, other_ref,
+    which_ref, own_ref, core_ref, recv_ref, conv_ref, w_ref, scale_ref, other_ref,
     keep_ref, give_ref, stat_ref,
     xc, xt, hid, c0, c1, c2, c3, g0, g1, g2, first, second, dout, dp2, dp1, dhid, dm0, dm1, dm2, dpair,
     acc_conv, acc_in, acc_mid, acc_head, acc_stat,
@@ -175,8 +180,6 @@
         ref[0:PAD, :] = jnp.zeros((PAD, CH), bf16)
     for ref in dms:
         ref[ALL_ROWS : ALL_ROWS + PAD, :] = jnp.zeros((PAD, CH), bf16)
-    for ref in (acc_conv, acc_in, acc_mid, acc_head, acc_stat):
-        ref[...] = jnp.zeros_like(ref)
 
     r, k = iota((SPANS, SOURCES * SLOT), 0), iota((SPANS, SOURCES * SLOT), 1)
     compact = onehot(((k & 7) < CAP) & (r == (k >> 3) * CAP + (k & 7)))
@@ -188,7 +191,7 @@
     scale = jnp.where(own, scale_ref[...], other_ref[...])
     scale = jnp.where(which_ref[0] == 0, scale[0:1, :], scale[1:2, :])
     log_scale = jnp.sum(jnp.where(iota((16, ACT), 0) == iota((16, ACT), 1), scale, 0.0), axis=1, keepdims=True)
-    conv = [w_ref.at[2 * CH * layer : 2 * CH * layer + 2 * CH] for layer in range(3)]
+    conv = [conv_ref.at[2 * CH * layer : 2 * CH * layer + 2 * CH] for layer in range(3)]
     in_half = [w_ref.at[W_IN + CH * n : W_IN + CH * n + CH] for n in range(2)]
     mid_half = [w_ref.at[W_MID + UNITS * n : W_MID + UNITS * n + UNITS] for n in range(2)]
     embed_half = [w_ref.at[W_EMBED + 128 * n : W_EMBED + 128 * n + 128] for n in range(2)]
@@ -204,102 +207,150 @@
     for s in range(1, CHUNK_STEPS, 2):
         odd = odd | ((lane >= s * SPANS) & (lane < (s + 1) * SPANS))
 
-    @pl.loop(0, CHUNKS)
-    def _(i):
-        base = i * ROWS
-        pairs = CHUNK_STEPS // 2
-        x = recv_ref[:, pl.ds(pl.multiple_of(i * (pairs * 128), 128), pairs * 128)]
-        x = dot(compact, x).astype(bf16)
-        half_rows = pl.ds(pl.multiple_of(i * (ROWS // 2), 16), ROWS // 2)
-        for p in range(pairs):
-            part = x[:, 128 * p : 128 * p + 128]
-            xc[pl.ds(pl.multiple_of(i * (ROWS // 2) + p * SPANS, 16), SPANS), :] = part
-            xt[2 * p * SPANS : (2 * p + 1) * SPANS, :] = part
-            xt[(2 * p + 1) * SPANS : (2 * p + 2) * SPANS, :] = part
-        y = [dot(xc[half_rows, :], half[...]) for half in embed_half]
-        for p in range(pairs):
-            for half in range(2):
-                at = (2 * p + half) * SPANS
-                h = y[half][p * SPANS : (p + 1) * SPANS, :]
-                hid[at : at + SPANS, :] = h
-                c0[pl.ds(pl.multiple_of(base + PAD + at, 16), SPANS), :] = h.astype(bf16)
-        for layer in range(3):
-            c, g = cs[layer], gs[layer]
-            lag = SPANS * 2**layer
-            both = jnp.concatenate(
-                [c[pl.ds(pl.multiple_of(base + PAD, 16), ROWS), :], c[pl.ds(pl.multiple_of(base + PAD - lag, 16), ROWS), :]],
-                axis=1,
-            )
+    pairs = CHUNK_STEPS // 2
+    blocks = (0, 256)
+
+    def rows(i, shift=0):
+        return slice(i * ROWS + shift, (i + 1) * ROWS + shift)
+
+    def add(ref, at, value, start):
+        if start:
+            ref[at] = value
+        else:
+            ref[at] += value
+
+    def elu(x):
+        below = jnp.minimum((jnp.exp(x) - 1.0).astype(bf16), jnp.zeros((), bf16))
+        return jnp.maximum(x.astype(bf16), below)
+
+    def slope(y):
+        return jnp.minimum(y, jnp.zeros((), bf16)) + jnp.ones((), bf16)
+
+    def forward(i):
+        def enter():
+            x = dot(compact, recv_ref[:, i * pairs * 128 : (i + 1) * pairs * 128]).astype(bf16)
+            for p in range(pairs):
+                part = x[:, 128 * p : 128 * p + 128]
+                at = i * (ROWS // 2) + p * SPANS
+                xc[at : at + SPANS, :] = part
+                for half in range(2):
+                    at = i * ROWS + (2 * p + half) * SPANS
+                    xt[at : at + SPANS, :] = part
+            y = [dot(xc[i * (ROWS // 2) : (i + 1) * (ROWS // 2), :], half[...]) for half in embed_half]
+            for p in range(pairs):
+                for half in range(2):
+                    at = i * ROWS + (2 * p + half) * SPANS
+                    h = y[half][p * SPANS : (p + 1) * SPANS, :]
+                    hid[at - i * ROWS : at - i * ROWS + SPANS, :] = h
+                    c0[PAD + at : PAD + at + SPANS, :] = h.astype(bf16)
+
+        def encode(layer):
+            c, lag = cs[layer], SPANS * 2**layer
+            both = jnp.concatenate([c[rows(i, PAD), :], c[rows(i, PAD - lag), :]], axis=1)
             mix = dot(both, conv[layer][...])
             grown = jnp.exp(mix)
             h = hid[...] + jnp.maximum(mix, jnp.minimum(grown - 1.0, 0.0))
-            g[pl.ds(pl.multiple_of(base, 16), ROWS), :] = jnp.minimum(grown.astype(bf16), jnp.ones((), bf16))
+            gs[layer][rows(i), :] = grown.astype(bf16)
             if layer < 2:
                 hid[...] = h
-                cs[layer + 1][pl.ds(pl.multiple_of(base + PAD, 16), ROWS), :] = h.astype(bf16)
+                cs[layer + 1][rows(i, PAD), :] = h.astype(bf16)
             else:
-                c3[...] = h.astype(bf16)
-
-        def elu(x):
-            below = jnp.minimum((jnp.exp(x) - 1.0).astype(bf16), jnp.zeros((), bf16))
-            return jnp.maximum(x.astype(bf16), below)
-
-        def slope(y):
-            return jnp.minimum(y, jnp.zeros((), bf16)) + jnp.ones((), bf16)
-
-        for n in range(0, UNITS, 256):
-            first[:, n : n + 256] = elu(dot(c3[...], in_half[n // 256][...]))
-        for n in range(0, UNITS, 256):
-            second[:, n : n + 256] = elu(dot(first[...], mid_half[n // 256][...]))
-        out = dot_nt(across(head_half, slice(0, 16)), second[...])
-        record = dot_nt(select, xt[...])
-        record = jnp.where(odd, record[32:64], record[0:32])
-        diff = record[0:16] - out
-        scaled = diff * inverse
-        square = scaled * scaled
-        advantage = record[13:14]
-        old_logp = record[14:15]
-        live = record[15:16]
-        log_ratio = -0.5 * jnp.sum(square, axis=0, keepdims=True) - offset - old_logp
-        ratio = jnp.exp(log_ratio)
-        dlog = live * (0.5 * (ratio - 1.0) - ratio * advantage)
-        dvalue = -0.5 * live * diff
-        d = jnp.where(sub == ACT, dvalue, dlog * scaled * inverse)
-        dout[...] = d.astype(bf16)
-        acc_stat[...] += jnp.sum(dlog * (square - 1.0), axis=1, keepdims=True)
-        acc_head[...] += dot(dout[...], second[...])
-        for n in range(0, UNITS, 256):
+                c3[rows(i), :] = h.astype(bf16)
+
+        def widen(n):
+            first[rows(i), n : n + 256] = elu(dot(c3[rows(i), :], in_half[n // 256][...]))
+
+        def deepen(n):
+            second[rows(i), n : n + 256] = elu(dot(first[rows(i), :], mid_half[n // 256][...]))
+
+        yield enter
+        for layer in range(3):
+            yield lambda layer=layer: encode(layer)
+        for n in blocks:
+            yield lambda n=n: widen(n)
+        for n in blocks:
+            yield lambda n=n: deepen(n)
+
+    def backward(i):
+        def loss():
+            out = dot_nt(across(head_half, slice(0, 16)), second[rows(i), :])
+            record = dot_nt(select, xt[rows(i), :])
+            record = jnp.where(odd, record[32:64], record[0:32])
+            diff = record[0:16] - out
+            scaled = diff * inverse
+            square = scaled * scaled
+            advantage, old_logp, live = record[13:14], record[14:15], record[15:16]
+            log_ratio = -0.5 * jnp.sum(square, axis=0, keepdims=True) - offset - old_logp
+            ratio = jnp.exp(log_ratio)
+            dlog = live * (0.5 * (ratio - 1.0) - ratio * advantage)
+            dvalue = -0.5 * live * diff
+            d = jnp.where(sub == ACT, dvalue, dlog * scaled * inverse)
+            dout[...] = d.astype(bf16)
+            total = jnp.sum(dlog * (square - 1.0), axis=1, keepdims=True)
+            add(acc_stat, Ellipsis, jnp.broadcast_to(total, acc_stat.shape), i == 0)
+
+        def down(n):
             ds = dot_tn(dout[...], head_half[n // 256][...])
-            dp2[:, n : n + 256] = ds.astype(bf16) * slope(second[:, n : n + 256])
-        for n in range(0, UNITS, 256):
+            dp2[:, n : n + 256] = ds.astype(bf16) * slope(second[rows(i), n : n + 256])
+
+        def head():
+            add(acc_head, Ellipsis, dot(dout[...], second[rows(i), :]), i == 0)
+
+        def middle(n):
             df = dot_nt(dp2[...], across(mid_half, slice(n, n + 256)))
-            dp1[:, n : n + 256] = df.astype(bf16) * slope(first[:, n : n + 256])
-        dhid[pl.ds(pl.multiple_of(base, 16), ROWS), :] = dot_nt(dp1[...], across(in_half, slice(0, CH)))
-        for n in range(0, UNITS, 256):
-            acc_mid[n : n + 256, :] += dot_tn(first[:, n : n + 256], dp2[...])
-        acc_in[...] += dot_tn(c3[...], dp1[...])
-
-    @pl.loop(0, CHUNKS)
-    def _(j):
-        i = CHUNKS - 1 - j
-        base = i * ROWS
-        here = pl.ds(pl.multiple_of(base, 16), ROWS)
+            dp1[:, n : n + 256] = df.astype(bf16) * slope(first[rows(i), n : n + 256])
+
+        def top():
+            dhid[rows(i), :] = dot_nt(dp1[...], across(in_half, slice(0, CH)))
+
+        def grad_mid():
+            add(acc_mid, Ellipsis, dot_tn(first[rows(i), :], dp2[...]), i == 0)
+
+        def grad_in():
+            add(acc_in, Ellipsis, dot_tn(c3[rows(i), :], dp1[...]), i == 0)
+
+        yield loss
+        for n in blocks:
+            yield lambda n=n: down(n)
+        yield head
+        for n in blocks:
+            yield lambda n=n: middle(n)
+        yield top
+        yield grad_mid
+        yield grad_in
+
+    def decode(i):
+        start = i == CHUNKS - 1
         for layer in (2, 1, 0):
-            c, g, dm = cs[layer], gs[layer], dms[layer]
-            lag = SPANS * 2**layer
-            dh = dhid[here, :]
-            dm[here, :] = dh.astype(bf16) * g[here, :]
-            dc = dot_nt(dm[here, :], conv[layer][0:256, :])
-            dc = dc + dot_nt(dm[pl.ds(pl.multiple_of(base + lag, 16), ROWS), :], conv[layer][256:512, :])
+            c, dm, lag = cs[layer], dms[layer], SPANS * 2**layer
+            dh = dhid[rows(i), :]
+            dm[rows(i), :] = dh.astype(bf16) * jnp.minimum(gs[layer][rows(i), :], jnp.ones((), bf16))
+            dc = dot_nt(dm[rows(i), :], conv[layer][0:256, :])
+            dc = dc + dot_nt(dm[rows(i, lag), :], conv[layer][256:512, :])
             dh = dh + dc
             if layer > 0:
-                dhid[here, :] = dh
+                dhid[rows(i), :] = dh
             else:
                 for s in range(CHUNK_STEPS):
-                    at = pl.ds(pl.multiple_of(i * (ROWS // 2) + (s // 2) * SPANS, 16), SPANS)
-                    dpair[at, 256 * (s % 2) : 256 * (s % 2) + 256] = dh[s * SPANS : s * SPANS + SPANS].astype(bf16)
-            acc_conv[2 * layer] += dot_tn(c[pl.ds(pl.multiple_of(base + PAD, 16), ROWS), :], dm[here, :])
-            acc_conv[2 * layer + 1] += dot_tn(c[pl.ds(pl.multiple_of(base + PAD - lag, 16), ROWS), :], dm[here, :])
+                    at = i * (ROWS // 2) + (s // 2) * SPANS
+                    part = dh[s * SPANS : s * SPANS + SPANS].astype(bf16)
+                    dpair[at : at + SPANS, 256 * (s % 2) : 256 * (s % 2) + 256] = part
+            both = jnp.concatenate([c[rows(i, PAD), :], c[rows(i, PAD - lag), :]], axis=1)
+            add(acc_conv, layer, dot_tn(both, dm[rows(i), :]), start)
+
+    def weave(left, right):
+        left, right = list(left), list(right)
+        order = [((k + 0.5) / len(left), 0, f) for k, f in enumerate(left)]
+        order += [((k + 0.5) / len(right), 1, f) for k, f in enumerate(right)]
+        for _, _, run in sorted(order, key=lambda item: item[:2]):
+            run()
+
+    weave(forward(0), [])
+    for i in range(1, CHUNKS):
+        weave(forward(i), backward(i - 1))
+    weave(backward(CHUNKS - 1), [])
+    for i in range(CHUNKS - 1, -1, -1):
+        decode(i)
 
     dembed = dot_tn(xc[...], dpair[...])
     dembed = (dembed[0:OBS, 0:256] + dembed[REC : REC + OBS, 256:512]).astype(bf16)
@@ -311,7 +362,7 @@
     def write(encoder_ref, trunk_ref):
         for s in range(SHARDS):
             for q in range(6):
-                encoder_ref[s, 16 * q : 16 * q + 16, :] = acc_conv[q, 16 * s : 16 * s + 16, :].astype(bf16)
+                encoder_ref[s, 16 * q : 16 * q + 16, :] = acc_conv[q // 2, 256 * (q % 2) + 16 * s : 256 * (q % 2) + 16 * s + 16, :].astype(bf16)
             encoder_ref[s, 96:104, :] = extra[8 * s : 8 * s + 8, :]
             for n in range(2):
                 cols = slice(256 * n, 256 * n + 256)
@@ -334,7 +385,7 @@
     stat_ref[...] = jnp.broadcast_to(line, (8, 128))
 
 
-def member_grad(which, own, core, recv, weights, scale, other):
+def member_grad(which, own, core, recv, conv, trunk, scale, other):
     v = pltpu.VMEM
     half = ALL_ROWS // 2
     return pl.pallas_call(
@@ -344,23 +395,23 @@
             jax.ShapeDtypeStruct((SHARDS, HALF, 256), bf16),
             jax.ShapeDtypeStruct((8, 128), f32),
         ),
-        in_specs=[pl.BlockSpec(memory_space=pltpu.SMEM)] * 3 + [pl.BlockSpec(memory_space=v)] * 4,
+        in_specs=[pl.BlockSpec(memory_space=pltpu.SMEM)] * 3 + [pl.BlockSpec(memory_space=v)] * 5,
         scratch_shapes=[
-            v((half, 128), bf16), v((ROWS, 128), bf16), v((ROWS, CH), f32),
+            v((half, 128), bf16), v((ALL_ROWS, 128), bf16), v((ROWS, CH), f32),
             v((PAD + ALL_ROWS, CH), bf16), v((PAD + ALL_ROWS, CH), bf16), v((PAD + ALL_ROWS, CH), bf16),
-            v((ROWS, CH), bf16),
+            v((ALL_ROWS, CH), bf16),
             v((ALL_ROWS, CH), bf16), v((ALL_ROWS, CH), bf16), v((ALL_ROWS, CH), bf16),
-            v((ROWS, UNITS), bf16), v((ROWS, UNITS), bf16), v((16, ROWS), bf16),
+            v((ALL_ROWS, UNITS), bf16), v((ALL_ROWS, UNITS), bf16), v((16, ROWS), bf16),
             v((ROWS, UNITS), bf16), v((ROWS, UNITS), bf16),
             v((ALL_ROWS, CH), f32),
             v((ALL_ROWS + PAD, CH), bf16), v((ALL_ROWS + PAD, CH), bf16), v((ALL_ROWS + PAD, CH), bf16),
             v((half, 512), bf16),
-            v((6, CH, CH), f32), v((CH, UNITS), f32), v((UNITS, UNITS), f32), v((16, UNITS), f32), v((16, 128), f32),
+            v((3, 2 * CH, CH), f32), v((CH, UNITS), f32), v((UNITS, UNITS), f32), v((16, UNITS), f32), v((16, 128), f32),
         ],
         cost_estimate=pl.CostEstimate(flops=11_200_000_000, bytes_accessed=4_000_000, transcendentals=4_000_000),
-        compiler_params=pltpu.CompilerParams(vmem_limit_bytes=34 * 1024 * 1024),
+        compiler_params=pltpu.CompilerParams(vmem_limit_bytes=42 * 1024 * 1024),
         name="grad",
-    )(which, own, core, recv, weights, scale, other)
+    )(which, own, core, recv, conv, trunk, scale, other)
 
 
 def reduce_kernel(core_ref, recv_ref, stat_ref, mine_ref, theirs_ref, cast_ref):
@@ -449,9 +500,16 @@
     core = core.reshape(1)
     packed = pack(observations, rollout, done_flags, member_ids)
     recv = lax.all_to_all(packed, ("y", "x"), split_axis=0, concat_axis=0, tiled=True)
-    weights = prepare(which, embed_weight, conv_weight, trunk_in, trunk_mid, head_weight)
-    weights = jnp.where(own[0] == 1, weights, swap(weights))
-    keep, give, stat = member_grad(which, own, core, recv, weights, log_std, swap(log_std))
+    conv = prepare(conv_weights_kernel, CONV_ROWS, which, (conv_weight,), (conv_weight.shape[1:],))
+    conv_far = swap(conv)
+    head = head_weight.transpose(2, 0, 1)
+    arrays = (embed_weight, trunk_in, trunk_mid, head)
+    shapes = tuple(x.shape[1:] for x in arrays[:3]) + (head.shape,)
+    trunk = prepare(trunk_weights_kernel, W_ROWS, which, arrays, shapes)
+    mine = own[0] == 1
+    conv = jnp.where(mine, conv, conv_far)
+    trunk = jnp.where(mine, trunk, swap(trunk))
+    keep, give, stat = member_grad(which, own, core, recv, conv, trunk, log_std, swap(log_std))
     both = (keep.astype(f32) + swap(give).astype(f32)).astype(bf16)
     parts = lax.all_to_all(both, ("z", "x"), split_axis=0, concat_axis=0, tiled=True)
     mine, theirs, cast = reduce_parts(core, parts, stat)

time: 82.6 us -> 81.5 us (0.987)
  Pallas kernels: 27 us -> 25.2 us
  waiting for transfers between devices: 12.4 us -> 14 us
  other arithmetic: 1.91 us -> 0.49 us
    pallas_call x1, Pallas kernels: 19.3 us -> 16.1 us  [member_grad(): pl.pallas_call(grad_kernel, out_shape=(jax.ShapeDtypeStruct((SHARDS, HALF...]
    all_to_all x1, waiting for transfers between devices: 8.78 us -> 10.3 us  [local(): lax.all_to_all(packed, ('y', 'x'), split_axis=0, concat_axis=0, tiled=True)]
    select_n x1 -> x2, other arithmetic: 1.64 us -> 0.25 us  [the longest x1 0.14 us: local(): trunk = jnp.where(mine, trunk, swap(trunk))]
    pallas_call x1 -> x2, Pallas kernels: 3.48 us -> 4.81 us  [prepare(): pl.pallas_call(kernel, in_specs=[pl.BlockSpec(memory_space=pltpu.SMEM)] +...]
    ppermute x5 -> x6, waiting for transfers between devices: 3.63 us -> 3.63 us  [swap(): return lax.ppermute(value, 'core', [(0, 1), (1, 0)])]
  transfers between devices with their start and end apart: 6 -> 7, of which waited for: 3 -> 3; matrix products, arithmetic and copies ran while one was open for 2% -> 0% of each run, Pallas kernels for 4% -> 7%
where the time goes in v5:
time: 81.5 us; the launch traced here: 80 us
  blocking collectives  31.3 us (38%)
  Pallas kernels  25.2 us (31%)
  waiting for transfers between devices  14 us (17%)
  starting transfers between devices  8.2 us (10%)
    all_to_all x1, blocking collectives, local(): lax.all_to_all(both, ('z', 'x'), split_axis=0, concat_axis=0, tiled=True)  20.9 us
    pallas_call x1, Pallas kernels, member_grad(): pl.pallas_call(grad_kernel, out_shape=(jax.ShapeDtypeStruct((SHARDS, HALF...  16.1 us
    all_to_all x1, blocking collectives, local(): lax.all_to_all(cast, ('z', 'x'), split_axis=0, concat_axis=0, tiled=True)  10.5 us
    all_to_all x1, waiting for transfers between devices, local(): lax.all_to_all(packed, ('y', 'x'), split_axis=0, concat_axis=0, tiled=True)  10.3 us
    all_to_all x1, starting transfers between devices, local(): lax.all_to_all(packed, ('y', 'x'), split_axis=0, concat_axis=0, tiled=True)  7.27 us
    pallas_call x2, Pallas kernels, prepare(): pl.pallas_call(kernel, in_specs=[pl.BlockSpec(memory_space=pltpu.SMEM)] +...  4.81 us
    ppermute x6, waiting for transfers between devices, swap(): return lax.ppermute(value, 'core', [(0, 1), (1, 0)])  3.63 us
    pallas_call x1, Pallas kernels, pack(): pl.pallas_call(pack_kernel, out_shape=jax.ShapeDtypeStruct((MEMBERS * SLO...  3.02 us
  transfers between devices with their start and end apart: 7, of which 3 were waited for; matrix products, arithmetic and copies ran while one was open for 0% of the time, Pallas kernels for 7%

profile of v5, /device:TPU:0, one launch (start us, length us, event | category | flops | bytes accessed | tf_op | source)
XLA Modules:
  0.0 80.0 jit_solution(1672825508617927095)
XLA Ops:
  0.6 2.3 %shard_map.145 = bf16[1536,256]{1,0:T(8,128)(2,1)} custom-call(s32[1]{0:T(128)} %bitcast.1.which_ref, f32[2,3,2,256,256]{4,3,2,1,0:T(8,128)} %conv_hbm.1), custom_call_target="tpu_custom_call" | custom-call | bytes 2500000 | tf_op jit(solution)/shard_map/pallas_call | solution.py:160
  3.0 0.1 collective-permute-start
  3.1 0.0 copy-start
  3.1 2.5 %shard_map.146 = bf16[1824,256]{1,0:T(8,128)(2,1)} custom-call(s32[1]{0:T(128)} %bitcast.1.which_ref, f32[2,48,256]{2,1,0:T(8,128)} %embed_hbm.1, f32[2,256,512]{2,1,0:T(8,128)} %in_hbm.1, f32[2,512,512]{2,1,0:T(8,128)} %mid_hbm.1, f32[13,2,512]{2,1,0:T(2,128)} %bitcast.17), custom_call_target="tpu_custom_call" | custom-call | bytes 2500000 | tf_op jit(solution)/shard_map/pallas_call | solution.py:160
  5.6 0.6 collective-permute-start.1
  6.2 0.1 collective-permute-start.2
  6.3 3.0 %pack.1 = bf16[128,1536]{1,0:T(8,128)(2,1)} custom-call(bf16[32,1152]{1,0:T(8,128)(2,1)} %obs_ref.1, bf16[32,384]{1,0:T(8,128)(2,1)} %roll_ref.1, s32[24,32]{1,0:T(8,128)} %bitcast.18, s32[1,32]{1,0:T(1,128)} %bitcast.19), custom_call_target="tpu_custom_call" | custom-call | tf_op jit(solution)/shard_map/pack/pallas_call | solution.py:106
  9.3 7.3 %all-to-all-start = ((bf16[16,8,1536]{2,1,0:T(8,128)(2,1)}), bf16[16,8,1536]{2,1,0:T(8,128)(2,1)S(1)}, u32[]{:S(2)}, u32[]{:S(2)}) async-start(bf16[16,8,1536]{2,1,0:T(8,128)(2,1)} %bitcast.16), calls=%async_computation | async-start | bytes 786432 | tf_op jit(solution)/shard_map/all_to_all | solution.py:502
  16.6 0.0 collective-permute-done
  16.6 0.1 broadcast_select_fusion.1.conv_ref
  16.7 0.0 collective-permute-done.1
  16.7 0.1 broadcast_select_fusion.w_ref
  16.9 0.0 collective-permute-done.2.other_ref
  16.9 10.3 %all-to-all-done = bf16[16,8,1536]{2,1,0:T(8,128)(2,1)S(1)} async-done(((bf16[16,8,1536]{2,1,0:T(8,128)(2,1)}), bf16[16,8,1536]{2,1,0:T(8,128)(2,1)S(1)}, u32[]{:S(2)}, u32[]{:S(2)}) %all-to-all-start) | async-done | bytes 393248 | tf_op jit(solution)/shard_map/all_to_all | solution.py:502
  27.2 16.1 %grad.1 = (bf16[16,104,256]{2,1,0:T(8,128)(2,1)S(1)}, bf16[16,104,256]{2,1,0:T(8,128)(2,1)S(1)}, f32[8,128]{1,0:T(8,128)S(1)}) custom-call(s32[1]{0:T(128)} %bitcast.1.which_ref, s32[1]{0:T(128)} %bitcast.2.own_ref, s32[1]{0:T(128)} %bitcast.core_ref, bf16[128,1536]{1,0:T(8,128)(2,1)S(1)} %bitcast.12, bf16[1536,256]{1,0:T(8,128)(2,1)S(1)} %broadcast_select_fusion.1.conv_ref, ...), custom_call_target="tpu_custom_call" | custom-call | flops 11200000000 | bytes 4000000 | tf_op jit(solution)/shard_map/grad/pallas_call | solution.py:391
  43.3 0.1 collective-permute-start.3
  43.4 2.4 %collective-permute-done.3 = bf16[16,104,256]{2,1,0:T(8,128)(2,1)S(1)} collective-permute-done((bf16[16,104,256]{2,1,0:T(8,128)(2,1)S(1)}, bf16[16,104,256]{2,1,0:T(8,128)(2,1)S(1)}, u32[]{:S(2)}, u32[]{:S(2)}) %collective-permute-start.3) | collective-permute-done | bytes 852000 | tf_op jit(solution)/shard_map/ppermute | solution.py:494
  45.8 0.2 add_convert_fusion
  46.0 20.9 %all_to_all.27.recv_ref = bf16[16,104,256]{2,1,0:T(8,128)(2,1)S(1)} all-to-all(bf16[16,104,256]{2,1,0:T(8,128)(2,1)S(1)} %add_convert_fusion), channel_id=1, replica_groups=mesh['y'=4,'core'=2,'z'=4,'x'=4] {'z','x'}, dimensions={0} | all-to-all | bytes 1703936 | tf_op jit(solution)/shard_map/all_to_all | solution.py:514
  66.9 0.3 reduce.1
  67.2 0.1 collective-permute-start.4
  67.3 10.5 %all_to_all.28 = f32[16,8,128]{2,1,0:T(8,128)S(1)} all-to-all(f32[16,8,128]{2,1,0:T(8,128)S(1)} %bitcast.15), channel_id=1, replica_groups=mesh['y'=4,'core'=2,'z'=4,'x'=4] {'z','x'}, dimensions={0} | all-to-all | bytes 131072 | tf_op jit(solution)/shard_map/all_to_all | solution.py:516
  77.8 1.3 %collective-permute-done.5.far_ref = f32[128,128]{1,0:T(8,128)S(1)} collective-permute-done((f32[128,128]{1,0:T(8,128)S(1)}, f32[128,128]{1,0:T(8,128)S(1)}, u32[]{:S(2)}, u32[]{:S(2)}) %collective-permute-start.5) | collective-permute-done | bytes 65568 | tf_op jit(solution)/shard_map/ppermute | solution.py:494
  79.0 1.0 %finish.1 = (f32[3,2,256]{2,1,0:T(2,128)}, f32[2,3,2,16,256]{4,3,2,1,0:T(8,128)}, f32[2,16,512]{2,1,0:T(8,128)}, f32[2,32,512]{2,1,0:T(8,128)}, f32[13,2,32]{2,1,0:T(2,128)}, /*index=5*/f32[2,12]{1,0:T(2,128)}) custom-call(s32[1]{0:T(128)} %bitcast.core_ref, f32[2,104,256]{2,1,0:T(8,128)S(1)} %get-tuple-element.21.mine_ref, ...), custom_call_target="tpu_custom_call" | custom-call | tf_op jit(solution)/shard_map/finish/pallas_call | solution.py:483
  (7 shorter events, 0.0 us)
Async XLA Ops:
  3.0 13.6 %collective-permute-start = (bf16[1536,256]{1,0:T(8,128)(2,1)}, bf16[1536,256]{1,0:T(8,128)(2,1)}, u32[]{:S(2)}, u32[]{:S(2)}) collective-permute-start(bf16[1536,256]{1,0:T(8,128)(2,1)} %shard_map.145), channel_id=1, source_target_pairs={{0,16},{16,0},{1,17},{17,1},{2,18},{18,2},{3,19},{19,3},{4,20},{20... | collective-permute-start | bytes 2359304 | tf_op jit(solution)/shard_map/ppermute | solution.py:494
  3.1 3.1 %copy-start = (f32[2,12]{1,0:T(2,128)S(1)}, f32[2,12]{1,0:T(2,128)}, u32[]{:S(2)}) copy-start(f32[2,12]{1,0:T(2,128)} %scale_ref.1) | copy-start | bytes 292
  5.6 11.0 %copy-start.2 = (bf16[1536,256]{1,0:T(8,128)(2,1)S(1)}, bf16[1536,256]{1,0:T(8,128)(2,1)}, u32[]{:S(2)}) copy-start(bf16[1536,256]{1,0:T(8,128)(2,1)} %shard_map.145) | copy-start | bytes 2359300
  5.6 11.1 %collective-permute-start.1 = (bf16[1824,256]{1,0:T(8,128)(2,1)}, bf16[1824,256]{1,0:T(8,128)(2,1)}, u32[]{:S(2)}, u32[]{:S(2)}) collective-permute-start(bf16[1824,256]{1,0:T(8,128)(2,1)} %shard_map.146), channel_id=1, source_target_pairs={{0,16},{16,0},{1,17},{17,1},{2,18},{18,2},{3,19},{19,3},{4,20},{20... | collective-permute-start | bytes 2801672 | tf_op jit(solution)/shard_map/ppermute | solution.py:494
  6.2 10.7 %collective-permute-start.2 = (f32[2,12]{1,0:T(2,128)S(1)}, f32[2,12]{1,0:T(2,128)S(1)}, u32[]{:S(2)}, u32[]{:S(2)}) collective-permute-start(f32[2,12]{1,0:T(2,128)S(1)} %copy-done), channel_id=1, source_target_pairs={{0,16},{16,0},{1,17},{17,1},{2,18},{18,2},{3,19},{19,3},{4,20},{20... | collective-permute-start | bytes 296 | tf_op jit(solution)/shard_map/ppermute | solution.py:494
  9.3 7.5 %copy-start.1 = (bf16[1824,256]{1,0:T(8,128)(2,1)S(1)}, bf16[1824,256]{1,0:T(8,128)(2,1)}, u32[]{:S(2)}) copy-start(bf16[1824,256]{1,0:T(8,128)(2,1)} %shard_map.146) | copy-start | bytes 2801668
  9.3 17.9 %all-to-all-start = ((bf16[16,8,1536]{2,1,0:T(8,128)(2,1)}), bf16[16,8,1536]{2,1,0:T(8,128)(2,1)S(1)}, u32[]{:S(2)}, u32[]{:S(2)}) async-start(bf16[16,8,1536]{2,1,0:T(8,128)(2,1)} %bitcast.16), calls=%async_computation | async-start | bytes 786432 | tf_op jit(solution)/shard_map/all_to_all | solution.py:502
  43.3 2.5 %collective-permute-start.3 = (bf16[16,104,256]{2,1,0:T(8,128)(2,1)S(1)}, bf16[16,104,256]{2,1,0:T(8,128)(2,1)S(1)}, u32[]{:S(2)}, u32[]{:S(2)}) collective-permute-start(bf16[16,104,256]{2,1,0:T(8,128)(2,1)S(1)} %get-tuple-element.19), channel_id=1, source_target_pairs={{0,16},{16,0},{1,17},{17,1},{2,18},{18,2},{3,19},{19,3},{4,20},{20... | collective-permute-start | bytes 2555912 | tf_op jit(solution)/shard_map/ppermute | solution.py:494
  67.2 11.8 %collective-permute-start.4 = (f32[2,104,256]{2,1,0:T(8,128)S(1)}, f32[2,104,256]{2,1,0:T(8,128)S(1)}, u32[]{:S(2)}, u32[]{:S(2)}) collective-permute-start(f32[2,104,256]{2,1,0:T(8,128)S(1)} %get-tuple-element.22), channel_id=1, source_target_pairs={{0,16},{16,0},{1,17},{17,1},{2,18},{18,2},{3,19},{19,3},{4,20},{20... | collective-permute-start | bytes 638984 | tf_op jit(solution)/shard_map/ppermute | solution.py:494
  77.7 1.3 %collective-permute-start.5 = (f32[128,128]{1,0:T(8,128)S(1)}, f32[128,128]{1,0:T(8,128)S(1)}, u32[]{:S(2)}, u32[]{:S(2)}) collective-permute-start(f32[128,128]{1,0:T(8,128)S(1)} %bitcast.13), channel_id=1, source_target_pairs={{0,16},{16,0},{1,17},{17,1},{2,18},{18,2},{3,19},{19,3},{4,20},{20... | collective-permute-start | bytes 196616 | tf_op jit(solution)/shard_map/ppermute | solution.py:494

commit v6 on v5

--- a/solution.py
+++ b/solution.py
@@ -30,8 +30,9 @@
 PAD = 4 * SPANS
 SHARDS = 16
 HALF = 104
-CONV_ROWS = 1536
-W_IN, W_MID, W_EMBED, W_HEAD, W_ROWS = 0, 512, 1536, 1792, 1824
+BIG_ROWS, SMALL_ROWS = 2560, 800
+W_MID = 1536
+W_IN, W_EMBED, W_HEAD = 0, 512, 768
 f32 = jnp.float32
 bf16 = jnp.bfloat16
 
@@ -56,12 +57,26 @@
     return jnp.where(cond, 1.0, 0.0).astype(bf16)
 
 
-def pack_kernel(obs_ref, roll_ref, done_ref, ids_ref, out_ref):
+def pack_kernel(obs_hbm, roll_hbm, done_hbm, ids_hbm, out_ref, obs_ref, roll_ref, done_ref, ids_ref, pick_ref, obs_at, act_at, scal_at, sems):
+    moves = [
+        pltpu.make_async_copy(source, target, sems.at[k])
+        for k, (source, target) in enumerate(
+            ((roll_hbm, roll_ref), (done_hbm, done_ref), (obs_hbm, obs_ref), (ids_hbm, ids_ref))
+        )
+    ]
+    for move in moves:
+        move.start()
     spans = obs_ref.shape[0]
-    row, col = iota((STEPS * 16, 512), 0), iota((STEPS * 16, 512), 1)
-    step = col & 127
-    pick = onehot((row == 16 * step + 12 + (col >> 7)) & (step < STEPS))
-    parts = dot(roll_ref[...], pick)
+    col = iota((1, 512), 1)
+    spot, within, step = col & 63, col >> 6, col & 127
+    row = iota((384, 512), 0)
+    obs_at[...] = onehot(row == jnp.where(spot < 48, 48 * within + spot, -1))
+    act_at[...] = onehot(row[0:128] == jnp.where((spot >= 48) & (spot < 60), 16 * within + spot - 48, -1))
+    scal_at[...] = onehot(row == jnp.where((spot >= 60) & (spot < 63), (spot - 60) * 128 + within, -1))
+    pick_ref[...] = onehot(row == jnp.where(step < STEPS, 16 * step + 12 + (col >> 7), -1))
+    for move in moves:
+        move.wait()
+    parts = dot(roll_ref[...], pick_ref[...])
     reward, old_value = parts[:, 0:128], parts[:, 128:256]
     next_value, old_logp = parts[:, 256:384], parts[:, 384:512]
     widen = onehot(iota((STEPS, 128), 0) == iota((STEPS, 128), 1))
@@ -75,20 +90,16 @@
         carry = carry * pltpu.roll(carry, 128 - shift, 1)
     target = jnp.where(lane < STEPS, advantage + old_value, 0.0)
     advantage = jnp.where(lane < STEPS, advantage, 0.0)
-    scalars = jnp.concatenate([target.astype(bf16), advantage.astype(bf16), old_logp.astype(bf16)], axis=1)
-
-    col = iota((384, 512), 1)
-    row = iota((384, 512), 0)
-    spot, within = col & 63, col >> 6
-    place_obs = onehot((row == 48 * within + spot) & (spot < 48))
-    place_act = onehot((row == 16 * within + spot - 48) & (spot >= 48) & (spot < 60))[0:128]
+    scalars = [target, advantage, old_logp]
+
     live = jnp.where((iota((spans, 512), 1) & 63) == 63, 1.0, 0.0)
     groups = []
     for g in range(3):
-        place_scal = onehot((spot >= 60) & (spot < 63) & (row == (spot - 60) * 128 + 8 * g + within))
-        placed = dot(obs_ref[:, 384 * g : 384 * g + 384], place_obs)
-        placed = placed + dot(roll_ref[:, 128 * g : 128 * g + 128], place_act)
-        placed = placed + dot(scalars, place_scal) + live
+        placed = dot(obs_ref[:, 384 * g : 384 * g + 384], obs_at[...])
+        placed = placed + dot(roll_ref[:, 128 * g : 128 * g + 128], act_at[...])
+        turned = [pltpu.roll(x, (128 - 8 * g) % 128, 1) if g else x for x in scalars]
+        turned = jnp.concatenate([x.astype(bf16) for x in turned], axis=1)
+        placed = placed + dot(turned, scal_at[...]) + live
         groups.append(placed.astype(bf16))
 
     slots = MEMBERS * SLOT
@@ -103,17 +114,24 @@
 
 
 def pack(observations, rollout, done_flags, member_ids):
+    arrays = (observations, rollout, done_flags.T, member_ids.T)
     return pl.pallas_call(
         pack_kernel,
         out_shape=jax.ShapeDtypeStruct((MEMBERS * SLOT, WIDTH), bf16),
+        in_specs=[pl.BlockSpec(memory_space=pltpu.HBM)] * 4,
+        out_specs=pl.BlockSpec(memory_space=pltpu.VMEM),
+        scratch_shapes=[pltpu.VMEM(x.shape, x.dtype) for x in arrays]
+        + [pltpu.VMEM((384, 512), bf16), pltpu.VMEM((384, 512), bf16), pltpu.VMEM((128, 512), bf16)]
+        + [pltpu.VMEM((384, 512), bf16), pltpu.SemaphoreType.DMA((4,))],
+        compiler_params=pltpu.CompilerParams(vmem_limit_bytes=60 * 1024 * 1024),
         name="pack",
-    )(observations, rollout, done_flags.T, member_ids.T)
-
-
-def conv_weights_kernel(which_ref, conv_hbm, out_ref, conv_ref, sems):
-    moves = [
-        pltpu.make_async_copy(conv_hbm.at[which_ref[0], layer], conv_ref.at[layer], sems.at[layer]) for layer in range(3)
-    ]
+    )(*arrays)
+
+
+def big_weights_kernel(which_ref, conv_hbm, mid_hbm, out_ref, conv_ref, mid_ref, sems):
+    which = which_ref[0]
+    moves = [pltpu.make_async_copy(conv_hbm.at[which, layer], conv_ref.at[layer], sems.at[layer]) for layer in range(3)]
+    moves.append(pltpu.make_async_copy(mid_hbm.at[which], mid_ref, sems.at[3]))
     for move in moves:
         move.start()
     for layer in range(3):
@@ -121,18 +139,17 @@
         for tap in range(2):
             at = CH * (2 * layer + tap)
             out_ref[at : at + CH, :] = conv_ref[layer, tap].astype(bf16)
-
-
-def trunk_weights_kernel(
-    which_ref, embed_hbm, in_hbm, mid_hbm, head_hbm, out_ref,
-    embed_ref, in_ref, mid_ref, head_ref, sems,
-):
+    moves[3].wait()
+    for n in range(2):
+        out_ref[W_MID + UNITS * n : W_MID + UNITS * n + UNITS, :] = mid_ref[:, 256 * n : 256 * n + 256].astype(bf16)
+
+
+def small_weights_kernel(which_ref, embed_hbm, in_hbm, head_hbm, out_ref, embed_ref, in_ref, head_ref, sems):
     which = which_ref[0]
     moves = [
         pltpu.make_async_copy(head_hbm, head_ref, sems.at[0]),
         pltpu.make_async_copy(embed_hbm.at[which], embed_ref, sems.at[1]),
         pltpu.make_async_copy(in_hbm.at[which], in_ref, sems.at[2]),
-        pltpu.make_async_copy(mid_hbm.at[which], mid_ref, sems.at[3]),
     ]
     for move in moves:
         move.start()
@@ -150,9 +167,6 @@
     moves[2].wait()
     for n in range(2):
         out_ref[W_IN + CH * n : W_IN + CH * n + CH, :] = in_ref[:, halves[n]].astype(bf16)
-    moves[3].wait()
-    for n in range(2):
-        out_ref[W_MID + UNITS * n : W_MID + UNITS * n + UNITS, :] = mid_ref[:, halves[n]].astype(bf16)
 
 
 def prepare(kernel, rows, which, arrays, shapes):
@@ -169,7 +183,7 @@
 
 
 def grad_kernel(
-    which_ref, own_ref, core_ref, recv_ref, conv_ref, w_ref, scale_ref, other_ref,
+    which_ref, own_ref, core_ref, recv_ref, big_ref, w_ref, scale_ref, other_ref,
     keep_ref, give_ref, stat_ref,
     xc, xt, hid, c0, c1, c2, c3, g0, g1, g2, first, second, dout, dp2, dp1, dhid, dm0, dm1, dm2, dpair,
     acc_conv, acc_in, acc_mid, acc_head, acc_stat,
@@ -191,9 +205,9 @@
     scale = jnp.where(own, scale_ref[...], other_ref[...])
     scale = jnp.where(which_ref[0] == 0, scale[0:1, :], scale[1:2, :])
     log_scale = jnp.sum(jnp.where(iota((16, ACT), 0) == iota((16, ACT), 1), scale, 0.0), axis=1, keepdims=True)
-    conv = [conv_ref.at[2 * CH * layer : 2 * CH * layer + 2 * CH] for layer in range(3)]
+    conv = [big_ref.at[2 * CH * layer : 2 * CH * layer + 2 * CH] for layer in range(3)]
     in_half = [w_ref.at[W_IN + CH * n : W_IN + CH * n + CH] for n in range(2)]
-    mid_half = [w_ref.at[W_MID + UNITS * n : W_MID + UNITS * n + UNITS] for n in range(2)]
+    mid_half = [big_ref.at[W_MID + UNITS * n : W_MID + UNITS * n + UNITS] for n in range(2)]
     embed_half = [w_ref.at[W_EMBED + 128 * n : W_EMBED + 128 * n + 128] for n in range(2)]
     head_half = [w_ref.at[W_HEAD + 16 * n : W_HEAD + 16 * n + 16] for n in range(2)]
 
@@ -385,7 +399,7 @@
     stat_ref[...] = jnp.broadcast_to(line, (8, 128))
 
 
-def member_grad(which, own, core, recv, conv, trunk, scale, other):
+def member_grad(which, own, core, recv, big, small, scale, other):
     v = pltpu.VMEM
     half = ALL_ROWS // 2
     return pl.pallas_call(
@@ -411,7 +425,7 @@
         cost_estimate=pl.CostEstimate(flops=11_200_000_000, bytes_accessed=4_000_000, transcendentals=4_000_000),
         compiler_params=pltpu.CompilerParams(vmem_limit_bytes=42 * 1024 * 1024),
         name="grad",
-    )(which, own, core, recv, conv, trunk, scale, other)
+    )(which, own, core, recv, big, small, scale, other)
 
 
 def reduce_kernel(core_ref, recv_ref, stat_ref, mine_ref, theirs_ref, cast_ref):
@@ -500,20 +514,23 @@
     core = core.reshape(1)
     packed = pack(observations, rollout, done_flags, member_ids)
     recv = lax.all_to_all(packed, ("y", "x"), split_axis=0, concat_axis=0, tiled=True)
-    conv = prepare(conv_weights_kernel, CONV_ROWS, which, (conv_weight,), (conv_weight.shape[1:],))
-    conv_far = swap(conv)
+    arrays = (conv_weight, trunk_mid)
+    shapes = tuple(x.shape[1:] for x in arrays)
+    big = prepare(big_weights_kernel, BIG_ROWS, which, arrays, shapes)
+    big_far = swap(big)
     head = head_weight.transpose(2, 0, 1)
-    arrays = (embed_weight, trunk_in, trunk_mid, head)
-    shapes = tuple(x.shape[1:] for x in arrays[:3]) + (head.shape,)
-    trunk = prepare(trunk_weights_kernel, W_ROWS, which, arrays, shapes)
+    arrays = (embed_weight, trunk_in, head)
+    shapes = tuple(x.shape[1:] for x in arrays[:2]) + (head.shape,)
+    small = prepare(small_weights_kernel, SMALL_ROWS, which, arrays, shapes)
     mine = own[0] == 1
-    conv = jnp.where(mine, conv, conv_far)
-    trunk = jnp.where(mine, trunk, swap(trunk))
-    keep, give, stat = member_grad(which, own, core, recv, conv, trunk, log_std, swap(log_std))
+    big = jnp.where(mine, big, big_far)
+    small = jnp.where(mine, small, swap(small))
+    keep, give, stat = member_grad(which, own, core, recv, big, small, log_std, swap(log_std))
     both = (keep.astype(f32) + swap(give).astype(f32)).astype(bf16)
     parts = lax.all_to_all(both, ("z", "x"), split_axis=0, concat_axis=0, tiled=True)
     mine, theirs, cast = reduce_parts(core, parts, stat)
     near = lax.all_to_all(cast, ("z", "x"), split_axis=0, concat_axis=0, tiled=True)
+    theirs, near = lax.optimization_barrier((theirs, near))
     return finish(core, mine, swap(theirs), near, swap(near))
 
 

time: 81.5 us -> 81.7 us (level)
  waiting for transfers between devices: 14 us -> 12.6 us
  other arithmetic: 0.49 us -> 1.5 us
    all_to_all x1, waiting for transfers between devices: 10.3 us -> 9.17 us  [local(): lax.all_to_all(packed, ('y', 'x'), split_axis=0, concat_axis=0, tiled=True)]
    select_n x2, other arithmetic: 0.25 us -> 1.25 us  [the longest x1 1.07 us: local(): small = jnp.where(mine, small, swap(small))]
  transfers between devices with their start and end apart: 7 -> 7, of which waited for: 3 -> 3; matrix products, arithmetic and copies ran while one was open for 0% -> 2% of each run, Pallas kernels for 7% -> 6%
where the time goes in v6:
time: 81.7 us; the launch traced here: 80.1 us
  blocking collectives  31.3 us (38%)
  Pallas kernels  25.3 us (31%)
  waiting for transfers between devices  12.6 us (15%)
  starting transfers between devices  8.67 us (11%)
  other arithmetic  1.5 us (2%)
    all_to_all x1, blocking collectives, local(): lax.all_to_all(both, ('z', 'x'), split_axis=0, concat_axis=0, tiled=True)  20.8 us
    pallas_call x1, Pallas kernels, member_grad(): pl.pallas_call(grad_kernel, out_shape=(jax.ShapeDtypeStruct((SHARDS, HALF...  16.1 us
    all_to_all x1, blocking collectives, local(): lax.all_to_all(cast, ('z', 'x'), split_axis=0, concat_axis=0, tiled=True)  10.5 us
    all_to_all x1, waiting for transfers between devices, local(): lax.all_to_all(packed, ('y', 'x'), split_axis=0, concat_axis=0, tiled=True)  9.17 us
    all_to_all x1, starting transfers between devices, local(): lax.all_to_all(packed, ('y', 'x'), split_axis=0, concat_axis=0, tiled=True)  7.32 us
    pallas_call x2, Pallas kernels, prepare(): pl.pallas_call(kernel, in_specs=[pl.BlockSpec(memory_space=pltpu.SMEM)] +...  4.87 us
    ppermute x6, waiting for transfers between devices, swap(): return lax.ppermute(value, 'core', [(0, 1), (1, 0)])  3.42 us
    pallas_call x1, Pallas kernels, pack(): pl.pallas_call(pack_kernel, out_shape=jax.ShapeDtypeStruct((MEMBERS * SLO...  2.96 us
  transfers between devices with their start and end apart: 7, of which 3 were waited for; matrix products, arithmetic and copies ran while one was open for 2% of the time, Pallas kernels for 6%

profile of v6, /device:TPU:0, one launch (start us, length us, event | category | flops | bytes accessed | tf_op | source)
XLA Modules:
  0.0 80.1 jit_solution(2581930227181481508)
XLA Ops:
  0.6 2.9 %shard_map.145 = bf16[2560,256]{1,0:T(8,128)(2,1)} custom-call(s32[1]{0:T(128)} %bitcast.1.which_ref, f32[2,3,2,256,256]{4,3,2,1,0:T(8,128)} %conv_hbm.1, f32[2,512,512]{2,1,0:T(8,128)} %mid_hbm.1), custom_call_target="tpu_custom_call" | custom-call | bytes 2500000 | tf_op jit(solution)/shard_map/pallas_call | solution.py:174
  3.5 0.0 copy-start
  3.6 0.1 collective-permute-start
  3.6 2.0 %shard_map.146 = bf16[800,256]{1,0:T(8,128)(2,1)} custom-call(s32[1]{0:T(128)} %bitcast.1.which_ref, f32[2,48,256]{2,1,0:T(8,128)} %embed_hbm.1, f32[2,256,512]{2,1,0:T(8,128)} %in_hbm.1, f32[13,2,512]{2,1,0:T(2,128)} %bitcast.17), custom_call_target="tpu_custom_call" | custom-call | bytes 2500000 | tf_op jit(solution)/shard_map/pallas_call | solution.py:174
  5.6 0.6 collective-permute-start.1
  6.2 0.1 collective-permute-start.2
  6.3 3.0 %pack.1 = bf16[128,1536]{1,0:T(8,128)(2,1)} custom-call(bf16[32,1152]{1,0:T(8,128)(2,1)} %obs_hbm.1, bf16[32,384]{1,0:T(8,128)(2,1)} %roll_hbm.1, s32[24,32]{1,0:T(8,128)} %bitcast.18, s32[1,32]{1,0:T(1,128)} %bitcast.19), custom_call_target="tpu_custom_call" | custom-call | tf_op jit(solution)/shard_map/pack/pallas_call | solution.py:118
  9.3 7.3 %all-to-all-start = ((bf16[16,8,1536]{2,1,0:T(8,128)(2,1)}), bf16[16,8,1536]{2,1,0:T(8,128)(2,1)S(1)}, u32[]{:S(2)}, u32[]{:S(2)}) async-start(bf16[16,8,1536]{2,1,0:T(8,128)(2,1)} %bitcast.16), calls=%async_computation | async-start | bytes 786432 | tf_op jit(solution)/shard_map/all_to_all | solution.py:516
  16.6 0.0 collective-permute-done.1
  16.6 1.1 %broadcast_select_fusion.1.w_ref = bf16[800,256]{1,0:T(8,128)(2,1)S(1)} fusion(bf16[800,256]{1,0:T(8,128)(2,1)} %shard_map.146, bf16[800,256]{1,0:T(8,128)(2,1)S(1)} %collective-permute-done.1, pred[]{:T(512)S(6)} %eq.9), kind=kLoop, calls=%fused_computation.2 | loop fusion | flops 204800 | bytes 1228801 | tf_op jit(solution)/shard_map/jit(_where)/select_n | solution.py:527
  17.7 0.0 collective-permute-done
  17.7 0.2 broadcast_select_fusion.big_ref
  17.9 9.2 %all-to-all-done = bf16[16,8,1536]{2,1,0:T(8,128)(2,1)S(1)} async-done(((bf16[16,8,1536]{2,1,0:T(8,128)(2,1)}), bf16[16,8,1536]{2,1,0:T(8,128)(2,1)S(1)}, u32[]{:S(2)}, u32[]{:S(2)}) %all-to-all-start) | async-done | bytes 393248 | tf_op jit(solution)/shard_map/all_to_all | solution.py:516
  27.1 16.1 %grad.1 = (bf16[16,104,256]{2,1,0:T(8,128)(2,1)S(1)}, bf16[16,104,256]{2,1,0:T(8,128)(2,1)S(1)}, f32[8,128]{1,0:T(8,128)S(1)}) custom-call(s32[1]{0:T(128)} %bitcast.1.which_ref, s32[1]{0:T(128)} %bitcast.2.own_ref, s32[1]{0:T(128)} %bitcast.core_ref, bf16[128,1536]{1,0:T(8,128)(2,1)S(1)} %bitcast.12, bf16[2560,256]{1,0:T(8,128)(2,1)S(1)} %broadcast_select_fusion.big_ref, ...), custom_call_target="tpu_custom_call" | custom-call | flops 11200000000 | bytes 4000000 | tf_op jit(solution)/shard_map/grad/pallas_call | solution.py:405
  43.2 0.1 collective-permute-start.3
  43.3 2.4 %collective-permute-done.3 = bf16[16,104,256]{2,1,0:T(8,128)(2,1)S(1)} collective-permute-done((bf16[16,104,256]{2,1,0:T(8,128)(2,1)S(1)}, bf16[16,104,256]{2,1,0:T(8,128)(2,1)S(1)}, u32[]{:S(2)}, u32[]{:S(2)}) %collective-permute-start.3) | collective-permute-done | bytes 852000 | tf_op jit(solution)/shard_map/ppermute | solution.py:508
  45.7 0.2 add_convert_fusion
  46.0 20.8 %all_to_all.28.recv_ref = bf16[16,104,256]{2,1,0:T(8,128)(2,1)S(1)} all-to-all(bf16[16,104,256]{2,1,0:T(8,128)(2,1)S(1)} %add_convert_fusion), channel_id=1, replica_groups=mesh['y'=4,'core'=2,'z'=4,'x'=4] {'z','x'}, dimensions={0} | all-to-all | bytes 1703936 | tf_op jit(solution)/shard_map/all_to_all | solution.py:530
  66.8 0.3 reduce.1
  67.1 10.5 %all_to_all.29 = f32[16,8,128]{2,1,0:T(8,128)S(1)} all-to-all(f32[16,8,128]{2,1,0:T(8,128)S(1)} %bitcast.15), channel_id=1, replica_groups=mesh['y'=4,'core'=2,'z'=4,'x'=4] {'z','x'}, dimensions={0} | all-to-all | bytes 131072 | tf_op jit(solution)/shard_map/all_to_all | solution.py:532
  77.6 0.0 collective-permute-start.4
  77.6 0.5 collective-permute-start.5
  78.1 1.0 %collective-permute-done.5.far_ref = f32[128,128]{1,0:T(8,128)S(1)} collective-permute-done((f32[128,128]{1,0:T(8,128)S(1)}, f32[128,128]{1,0:T(8,128)S(1)}, u32[]{:S(2)}, u32[]{:S(2)}) %collective-permute-start.5) | collective-permute-done | bytes 65568 | tf_op jit(solution)/shard_map/ppermute | solution.py:508
  79.1 1.0 %finish.1 = (f32[3,2,256]{2,1,0:T(2,128)}, f32[2,3,2,16,256]{4,3,2,1,0:T(8,128)}, f32[2,16,512]{2,1,0:T(8,128)}, f32[2,32,512]{2,1,0:T(8,128)}, f32[13,2,32]{2,1,0:T(2,128)}, /*index=5*/f32[2,12]{1,0:T(2,128)}) custom-call(s32[1]{0:T(128)} %bitcast.core_ref, f32[2,104,256]{2,1,0:T(8,128)S(1)} %get-tuple-element.23.mine_ref, ...), custom_call_target="tpu_custom_call" | custom-call | tf_op jit(solution)/shard_map/finish/pallas_call | solution.py:497
  (5 shorter events, 0.0 us)
Async XLA Ops:
  3.5 2.7 %copy-start = (f32[2,12]{1,0:T(2,128)S(1)}, f32[2,12]{1,0:T(2,128)}, u32[]{:S(2)}) copy-start(f32[2,12]{1,0:T(2,128)} %scale_ref.1) | copy-start | bytes 292
  3.6 14.2 %collective-permute-start = (bf16[2560,256]{1,0:T(8,128)(2,1)}, bf16[2560,256]{1,0:T(8,128)(2,1)}, u32[]{:S(2)}, u32[]{:S(2)}) collective-permute-start(bf16[2560,256]{1,0:T(8,128)(2,1)} %shard_map.145), channel_id=1, source_target_pairs={{0,16},{16,0},{1,17},{17,1},{2,18},{18,2},{3,19},{19,3},{4,20},{20... | collective-permute-start | bytes 3932168 | tf_op jit(solution)/shard_map/ppermute | solution.py:508
  5.6 12.1 %copy-start.1 = (bf16[2560,256]{1,0:T(8,128)(2,1)S(1)}, bf16[2560,256]{1,0:T(8,128)(2,1)}, u32[]{:S(2)}) copy-start(bf16[2560,256]{1,0:T(8,128)(2,1)} %shard_map.145) | copy-start | bytes 3932164
  5.6 11.0 %collective-permute-start.1 = (bf16[800,256]{1,0:T(8,128)(2,1)}, bf16[800,256]{1,0:T(8,128)(2,1)S(1)}, u32[]{:S(2)}, u32[]{:S(2)}) collective-permute-start(bf16[800,256]{1,0:T(8,128)(2,1)} %shard_map.146), channel_id=1, source_target_pairs={{0,16},{16,0},{1,17},{17,1},{2,18},{18,2},{3,19},{19,3},{4,20},{20... | collective-permute-start | bytes 1228808 | tf_op jit(solution)/shard_map/ppermute | solution.py:508
  6.2 11.7 %collective-permute-start.2 = (f32[2,12]{1,0:T(2,128)S(1)}, f32[2,12]{1,0:T(2,128)S(1)}, u32[]{:S(2)}, u32[]{:S(2)}) collective-permute-start(f32[2,12]{1,0:T(2,128)S(1)} %copy-done), channel_id=1, source_target_pairs={{0,16},{16,0},{1,17},{17,1},{2,18},{18,2},{3,19},{19,3},{4,20},{20... | collective-permute-start | bytes 296 | tf_op jit(solution)/shard_map/ppermute | solution.py:508
  9.3 17.8 %all-to-all-start = ((bf16[16,8,1536]{2,1,0:T(8,128)(2,1)}), bf16[16,8,1536]{2,1,0:T(8,128)(2,1)S(1)}, u32[]{:S(2)}, u32[]{:S(2)}) async-start(bf16[16,8,1536]{2,1,0:T(8,128)(2,1)} %bitcast.16), calls=%async_computation | async-start | bytes 786432 | tf_op jit(solution)/shard_map/all_to_all | solution.py:516
  43.2 2.5 %collective-permute-start.3 = (bf16[16,104,256]{2,1,0:T(8,128)(2,1)S(1)}, bf16[16,104,256]{2,1,0:T(8,128)(2,1)S(1)}, u32[]{:S(2)}, u32[]{:S(2)}) collective-permute-start(bf16[16,104,256]{2,1,0:T(8,128)(2,1)S(1)} %get-tuple-element.21), channel_id=1, source_target_pairs={{0,16},{16,0},{1,17},{17,1},{2,18},{18,2},{3,19},{19,3},{4,20},{20... | collective-permute-start | bytes 2555912 | tf_op jit(solution)/shard_map/ppermute | solution.py:508
  77.6 1.6 %collective-permute-start.4 = (f32[2,104,256]{2,1,0:T(8,128)S(1)}, f32[2,104,256]{2,1,0:T(8,128)S(1)}, u32[]{:S(2)}, u32[]{:S(2)}) collective-permute-start(f32[2,104,256]{2,1,0:T(8,128)S(1)} %get-tuple-element.26), channel_id=1, source_target_pairs={{0,16},{16,0},{1,17},{17,1},{2,18},{18,2},{3,19},{19,3},{4,20},{20... | collective-permute-start | bytes 638984 | tf_op jit(solution)/shard_map/ppermute | solution.py:508
  77.6 1.6 %collective-permute-start.5 = (f32[128,128]{1,0:T(8,128)S(1)}, f32[128,128]{1,0:T(8,128)S(1)}, u32[]{:S(2)}, u32[]{:S(2)}) collective-permute-start(f32[128,128]{1,0:T(8,128)S(1)} %bitcast.13), channel_id=1, source_target_pairs={{0,16},{16,0},{1,17},{17,1},{2,18},{18,2},{3,19},{19,3},{4,20},{20... | collective-permute-start | bytes 196616 | tf_op jit(solution)/shard_map/ppermute | solution.py:508

commit v7 on v6

--- a/solution.py
+++ b/solution.py
@@ -30,9 +30,7 @@
 PAD = 4 * SPANS
 SHARDS = 16
 HALF = 104
-BIG_ROWS, SMALL_ROWS = 2560, 800
-W_MID = 1536
-W_IN, W_EMBED, W_HEAD = 0, 512, 768
+W_MID, W_IN, W_EMBED, W_HEAD, W_ROWS = 1536, 2560, 3072, 3328, 3360
 f32 = jnp.float32
 bf16 = jnp.bfloat16
 
@@ -57,14 +55,21 @@
     return jnp.where(cond, 1.0, 0.0).astype(bf16)
 
 
-def pack_kernel(obs_hbm, roll_hbm, done_hbm, ids_hbm, out_ref, obs_ref, roll_ref, done_ref, ids_ref, pick_ref, obs_at, act_at, scal_at, sems):
-    moves = [
-        pltpu.make_async_copy(source, target, sems.at[k])
-        for k, (source, target) in enumerate(
-            ((roll_hbm, roll_ref), (done_hbm, done_ref), (obs_hbm, obs_ref), (ids_hbm, ids_ref))
-        )
+def pack_kernel(
+    which_ref, obs_hbm, roll_hbm, done_hbm, ids_hbm, embed_hbm, conv_hbm, in_hbm, mid_hbm, head_hbm,
+    out_ref, w_ref,
+    obs_ref, roll_ref, done_ref, ids_ref, embed_ref, conv_ref, in_ref, mid_ref, head_ref,
+    pick_ref, obs_at, act_at, scal_at, sems,
+):
+    which = which_ref[0]
+    sources = [roll_hbm, done_hbm, obs_hbm, ids_hbm, head_hbm]
+    sources += [conv_hbm.at[which], mid_hbm.at[which], in_hbm.at[which], embed_hbm.at[which]]
+    targets = [roll_ref, done_ref, obs_ref, ids_ref, head_ref, conv_ref, mid_ref, in_ref, embed_ref]
+    copies = [
+        pltpu.make_async_copy(source, target, sems.at[k]) for k, (source, target) in enumerate(zip(sources, targets))
     ]
-    for move in moves:
+    moves, head_move, (conv_move, mid_move, in_move, embed_move) = copies[:4], copies[4], copies[5:]
+    for move in copies:
         move.start()
     spans = obs_ref.shape[0]
     col = iota((1, 512), 1)
@@ -112,78 +117,52 @@
     for g in range(3):
         out_ref[:, 512 * g : 512 * g + 512] = dot(dispatch, groups[g]).astype(bf16)
 
-
-def pack(observations, rollout, done_flags, member_ids):
-    arrays = (observations, rollout, done_flags.T, member_ids.T)
-    return pl.pallas_call(
-        pack_kernel,
-        out_shape=jax.ShapeDtypeStruct((MEMBERS * SLOT, WIDTH), bf16),
-        in_specs=[pl.BlockSpec(memory_space=pltpu.HBM)] * 4,
-        out_specs=pl.BlockSpec(memory_space=pltpu.VMEM),
-        scratch_shapes=[pltpu.VMEM(x.shape, x.dtype) for x in arrays]
-        + [pltpu.VMEM((384, 512), bf16), pltpu.VMEM((384, 512), bf16), pltpu.VMEM((128, 512), bf16)]
-        + [pltpu.VMEM((384, 512), bf16), pltpu.SemaphoreType.DMA((4,))],
-        compiler_params=pltpu.CompilerParams(vmem_limit_bytes=60 * 1024 * 1024),
-        name="pack",
-    )(*arrays)
-
-
-def big_weights_kernel(which_ref, conv_hbm, mid_hbm, out_ref, conv_ref, mid_ref, sems):
-    which = which_ref[0]
-    moves = [pltpu.make_async_copy(conv_hbm.at[which, layer], conv_ref.at[layer], sems.at[layer]) for layer in range(3)]
-    moves.append(pltpu.make_async_copy(mid_hbm.at[which], mid_ref, sems.at[3]))
-    for move in moves:
-        move.start()
-    for layer in range(3):
-        moves[layer].wait()
-        for tap in range(2):
-            at = CH * (2 * layer + tap)
-            out_ref[at : at + CH, :] = conv_ref[layer, tap].astype(bf16)
-    moves[3].wait()
-    for n in range(2):
-        out_ref[W_MID + UNITS * n : W_MID + UNITS * n + UNITS, :] = mid_ref[:, 256 * n : 256 * n + 256].astype(bf16)
-
-
-def small_weights_kernel(which_ref, embed_hbm, in_hbm, head_hbm, out_ref, embed_ref, in_ref, head_ref, sems):
-    which = which_ref[0]
-    moves = [
-        pltpu.make_async_copy(head_hbm, head_ref, sems.at[0]),
-        pltpu.make_async_copy(embed_hbm.at[which], embed_ref, sems.at[1]),
-        pltpu.make_async_copy(in_hbm.at[which], in_ref, sems.at[2]),
-    ]
-    for move in moves:
-        move.start()
     halves = (slice(0, 256), slice(256, 512))
-    moves[0].wait()
+    head_move.wait()
     head = jnp.where(which == 0, head_ref[:, 0, :], head_ref[:, 1, :]).astype(bf16)
     head = dot(onehot(iota((16, ACT + 1), 0) == iota((16, ACT + 1), 1)), head).astype(bf16)
     for n in range(2):
-        out_ref[W_HEAD + 16 * n : W_HEAD + 16 * n + 16, :] = head[:, halves[n]]
-    moves[1].wait()
+        w_ref[W_HEAD + 16 * n : W_HEAD + 16 * n + 16, :] = head[:, halves[n]]
+    conv_move.wait()
+    for layer in range(3):
+        for tap in range(2):
+            at = CH * (2 * layer + tap)
+            w_ref[at : at + CH, :] = conv_ref[layer, tap].astype(bf16)
+    mid_move.wait()
+    for n in range(2):
+        w_ref[W_MID + UNITS * n : W_MID + UNITS * n + UNITS, :] = mid_ref[:, halves[n]].astype(bf16)
+    in_move.wait()
+    for n in range(2):
+        w_ref[W_IN + CH * n : W_IN + CH * n + CH, :] = in_ref[:, halves[n]].astype(bf16)
+    embed_move.wait()
     embed = embed_ref[...].astype(bf16)
     r, k = iota((128, OBS), 0), iota((128, OBS), 1)
     for n in range(2):
-        out_ref[W_EMBED + 128 * n : W_EMBED + 128 * n + 128, :] = dot(onehot(r == k + REC * n), embed).astype(bf16)
-    moves[2].wait()
-    for n in range(2):
-        out_ref[W_IN + CH * n : W_IN + CH * n + CH, :] = in_ref[:, halves[n]].astype(bf16)
-
-
-def prepare(kernel, rows, which, arrays, shapes):
+        w_ref[W_EMBED + 128 * n : W_EMBED + 128 * n + 128, :] = dot(onehot(r == k + REC * n), embed).astype(bf16)
+
+
+def pack(which, observations, rollout, done_flags, member_ids, embed, conv, trunk_in, trunk_mid, head):
     v = pltpu.VMEM
+    spans = (observations, rollout, done_flags.T, member_ids.T)
+    weights = (embed, conv, trunk_in, trunk_mid)
+    head = head.transpose(2, 0, 1)
     return pl.pallas_call(
-        kernel,
-        in_specs=[pl.BlockSpec(memory_space=pltpu.SMEM)] + [pl.BlockSpec(memory_space=pltpu.HBM)] * len(arrays),
-        out_specs=pl.BlockSpec(memory_space=v),
-        out_shape=jax.ShapeDtypeStruct((rows, CH), bf16),
-        scratch_shapes=[v(shape, f32) for shape in shapes] + [pltpu.SemaphoreType.DMA((4,))],
-        cost_estimate=pl.CostEstimate(flops=0, bytes_accessed=2_500_000, transcendentals=0),
+        pack_kernel,
+        out_shape=(jax.ShapeDtypeStruct((MEMBERS * SLOT, WIDTH), bf16), jax.ShapeDtypeStruct((W_ROWS, CH), bf16)),
+        in_specs=[pl.BlockSpec(memory_space=pltpu.SMEM)] + [pl.BlockSpec(memory_space=pltpu.HBM)] * 9,
+        out_specs=(pl.BlockSpec(memory_space=v), pl.BlockSpec(memory_space=v)),
+        scratch_shapes=[v(x.shape, x.dtype) for x in spans]
+        + [v(x.shape[1:], f32) for x in weights]
+        + [v(head.shape, f32)]
+        + [v((384, 512), bf16), v((384, 512), bf16), v((128, 512), bf16), v((384, 512), bf16)]
+        + [pltpu.SemaphoreType.DMA((9,))],
         compiler_params=pltpu.CompilerParams(vmem_limit_bytes=60 * 1024 * 1024),
-    )(which, *arrays)
+        name="pack",
+    )(which, *spans, *weights, head)
 
 
 def grad_kernel(
-    which_ref, own_ref, core_ref, recv_ref, big_ref, w_ref, scale_ref, other_ref,
+    which_ref, own_ref, core_ref, recv_ref, w_ref, scale_ref, other_ref,
     keep_ref, give_ref, stat_ref,
     xc, xt, hid, c0, c1, c2, c3, g0, g1, g2, first, second, dout, dp2, dp1, dhid, dm0, dm1, dm2, dpair,
     acc_conv, acc_in, acc_mid, acc_head, acc_stat,
@@ -205,9 +184,9 @@
     scale = jnp.where(own, scale_ref[...], other_ref[...])
     scale = jnp.where(which_ref[0] == 0, scale[0:1, :], scale[1:2, :])
     log_scale = jnp.sum(jnp.where(iota((16, ACT), 0) == iota((16, ACT), 1), scale, 0.0), axis=1, keepdims=True)
-    conv = [big_ref.at[2 * CH * layer : 2 * CH * layer + 2 * CH] for layer in range(3)]
+    conv = [w_ref.at[2 * CH * layer : 2 * CH * layer + 2 * CH] for layer in range(3)]
     in_half = [w_ref.at[W_IN + CH * n : W_IN + CH * n + CH] for n in range(2)]
-    mid_half = [big_ref.at[W_MID + UNITS * n : W_MID + UNITS * n + UNITS] for n in range(2)]
+    mid_half = [w_ref.at[W_MID + UNITS * n : W_MID + UNITS * n + UNITS] for n in range(2)]
     embed_half = [w_ref.at[W_EMBED + 128 * n : W_EMBED + 128 * n + 128] for n in range(2)]
     head_half = [w_ref.at[W_HEAD + 16 * n : W_HEAD + 16 * n + 16] for n in range(2)]
 
@@ -399,7 +378,7 @@
     stat_ref[...] = jnp.broadcast_to(line, (8, 128))
 
 
-def member_grad(which, own, core, recv, big, small, scale, other):
+def member_grad(which, own, core, recv, weights, scale, other):
     v = pltpu.VMEM
     half = ALL_ROWS // 2
     return pl.pallas_call(
@@ -409,7 +388,7 @@
             jax.ShapeDtypeStruct((SHARDS, HALF, 256), bf16),
             jax.ShapeDtypeStruct((8, 128), f32),
         ),
-        in_specs=[pl.BlockSpec(memory_space=pltpu.SMEM)] * 3 + [pl.BlockSpec(memory_space=v)] * 5,
+        in_specs=[pl.BlockSpec(memory_space=pltpu.SMEM)] * 3 + [pl.BlockSpec(memory_space=v)] * 4,
         scratch_shapes=[
             v((half, 128), bf16), v((ALL_ROWS, 128), bf16), v((ROWS, CH), f32),
             v((PAD + ALL_ROWS, CH), bf16), v((PAD + ALL_ROWS, CH), bf16), v((PAD + ALL_ROWS, CH), bf16),
@@ -425,7 +404,7 @@
         cost_estimate=pl.CostEstimate(flops=11_200_000_000, bytes_accessed=4_000_000, transcendentals=4_000_000),
         compiler_params=pltpu.CompilerParams(vmem_limit_bytes=42 * 1024 * 1024),
         name="grad",
-    )(which, own, core, recv, big, small, scale, other)
+    )(which, own, core, recv, weights, scale, other)
 
 
 def reduce_kernel(core_ref, recv_ref, stat_ref, mine_ref, theirs_ref, cast_ref):
@@ -439,7 +418,7 @@
                 total = total + recv_ref[4 * z + kind].astype(f32)
             out_ref[j] = total
             line = line + jnp.where(lane1 == kind, jnp.sum(total * total), 0.0)
-    for s in range(SHARDS):
+    for s in range(2 * SHARDS):
         cast_ref[8 * s : 8 * s + 8, :] = jnp.broadcast_to(line, (8, 128))
 
 
@@ -447,24 +426,24 @@
     part = jax.ShapeDtypeStruct((2, HALF, 256), f32)
     return pl.pallas_call(
         reduce_kernel,
-        out_shape=(part, part, jax.ShapeDtypeStruct((SHARDS * 8, 128), f32)),
+        out_shape=(part, part, jax.ShapeDtypeStruct((2 * SHARDS * 8, 128), f32)),
         in_specs=[pl.BlockSpec(memory_space=pltpu.SMEM)] + [pl.BlockSpec(memory_space=pltpu.VMEM)] * 2,
         compiler_params=pltpu.CompilerParams(vmem_limit_bytes=16 * 1024 * 1024),
         name="reduce",
     )(core, recv, stat)
 
 
-def finish_kernel(core_ref, mine_ref, theirs_ref, near_ref, far_ref, embed_ref, conv_ref, in_ref, mid_ref, head_ref, std_ref):
+def finish_kernel(core_ref, mine_ref, theirs_ref, lines_ref, embed_ref, conv_ref, in_ref, mid_ref, head_ref, std_ref):
     core = core_ref[0]
     lane1 = iota((1, 128), 1)
-    total = jnp.sum(near_ref[...] + far_ref[...], axis=0, keepdims=True) * 0.125
+    total = jnp.sum(lines_ref[...], axis=0, keepdims=True) * 0.125
     scales = []
     for j in range(2):
         kind = 2 * core + j
         std = jnp.zeros((1, 128), f32)
-        for z in range(4):
+        for z in range(8):
             at = pl.ds(pl.multiple_of(8 * (4 * z + kind), 8), 8)
-            std = std + near_ref[at, :][0:1] + far_ref[at, :][0:1]
+            std = std + lines_ref[at, :][0:1]
         std = jnp.where((lane1 >= 32) & (lane1 < 32 + ACT), std, 0.0)
         square = jnp.sum(std * std + jnp.where(lane1 == kind, total, 0.0), axis=1, keepdims=True)
         scale = 1.0 / jnp.sqrt(square / ENTRIES + 1e-06)
@@ -492,15 +471,15 @@
         write(theirs_ref, mine_ref)
 
 
-def finish(core, mine, theirs, near, far):
+def finish(core, mine, theirs, lines):
     shapes = ((3, 2, 256), (2, 3, 2, 16, 256), (2, 16, 512), (2, 32, 512), (13, 2, 32), (2, 12))
     embed, conv, first, second, head, std = pl.pallas_call(
         finish_kernel,
         out_shape=tuple(jax.ShapeDtypeStruct(s, f32) for s in shapes),
-        in_specs=[pl.BlockSpec(memory_space=pltpu.SMEM)] + [pl.BlockSpec(memory_space=pltpu.VMEM)] * 4,
+        in_specs=[pl.BlockSpec(memory_space=pltpu.SMEM)] + [pl.BlockSpec(memory_space=pltpu.VMEM)] * 3,
         compiler_params=pltpu.CompilerParams(vmem_limit_bytes=16 * 1024 * 1024),
         name="finish",
-    )(core, mine, theirs, near, far)
+    )(core, mine, theirs, lines)
     return embed.transpose(1, 0, 2), conv, first, second, head.transpose(1, 2, 0), std
 
 
@@ -512,26 +491,19 @@
     x, core = lax.axis_index("x"), lax.axis_index("core")
     which, own = (x % 2).reshape(1), (core == x // 2).astype(jnp.int32).reshape(1)
     core = core.reshape(1)
-    packed = pack(observations, rollout, done_flags, member_ids)
+    packed, weights = pack(
+        which, observations, rollout, done_flags, member_ids, embed_weight, conv_weight, trunk_in, trunk_mid, head_weight
+    )
+    far = swap(weights)
     recv = lax.all_to_all(packed, ("y", "x"), split_axis=0, concat_axis=0, tiled=True)
-    arrays = (conv_weight, trunk_mid)
-    shapes = tuple(x.shape[1:] for x in arrays)
-    big = prepare(big_weights_kernel, BIG_ROWS, which, arrays, shapes)
-    big_far = swap(big)
-    head = head_weight.transpose(2, 0, 1)
-    arrays = (embed_weight, trunk_in, head)
-    shapes = tuple(x.shape[1:] for x in arrays[:2]) + (head.shape,)
-    small = prepare(small_weights_kernel, SMALL_ROWS, which, arrays, shapes)
-    mine = own[0] == 1
-    big = jnp.where(mine, big, big_far)
-    small = jnp.where(mine, small, swap(small))
-    keep, give, stat = member_grad(which, own, core, recv, big, small, log_std, swap(log_std))
+    other = swap(log_std)
+    weights = jnp.where(own[0] == 1, weights, far)
+    keep, give, stat = member_grad(which, own, core, recv, weights, log_std, other)
     both = (keep.astype(f32) + swap(give).astype(f32)).astype(bf16)
     parts = lax.all_to_all(both, ("z", "x"), split_axis=0, concat_axis=0, tiled=True)
     mine, theirs, cast = reduce_parts(core, parts, stat)
-    near = lax.all_to_all(cast, ("z", "x"), split_axis=0, concat_axis=0, tiled=True)
-    theirs, near = lax.optimization_barrier((theirs, near))
-    return finish(core, mine, swap(theirs), near, swap(near))
+    lines = lax.all_to_all(cast, ("core", "z", "x"), split_axis=0, concat_axis=0, tiled=True)
+    return finish(core, mine, swap(theirs), lines)
 
 
 def solution(mesh):

time: 81.7 us -> 75.9 us (0.929)
  Pallas kernels: 25.3 us -> 21.4 us
  waiting for transfers between devices: 12.6 us -> 11.2 us
  starting transfers between devices: 8.67 us -> 7.71 us
    pallas_call x3 -> x1, Pallas kernels: 7.83 us -> 3.98 us  [pack(): pl.pallas_call(pack_kernel, out_shape=(jax.ShapeDtypeStruct((MEMBERS * SL...]
    ppermute x6 -> x4, waiting for transfers between devices: 3.42 us -> 2.37 us  [swap(): return lax.ppermute(value, 'core', [(0, 1), (1, 0)])]
    select_n x2 -> x1, other arithmetic: 1.25 us -> 1.64 us  [local(): weights = jnp.where(own[0] == 1, weights, far)]
  transfers between devices with their start and end apart: 7 -> 5, of which waited for: 3 -> 2; matrix products, arithmetic and copies ran while one was open for 2% -> 2% of each run, Pallas kernels for 6% -> 0%
where the time goes in v7:
time: 75.9 us; the launch traced here: 74.7 us
  blocking collectives  31.9 us (42%)
  Pallas kernels  21.4 us (28%)
  waiting for transfers between devices  11.2 us (15%)
  starting transfers between devices  7.71 us (10%)
  other arithmetic  1.91 us (3%)
    all_to_all x1, blocking collectives, local(): lax.all_to_all(both, ('z', 'x'), split_axis=0, concat_axis=0, tiled=True)  20.8 us
    pallas_call x1, Pallas kernels, member_grad(): pl.pallas_call(grad_kernel, out_shape=(jax.ShapeDtypeStruct((SHARDS, HALF...  16.1 us
    all_to_all x1, blocking collectives, local(): lax.all_to_all(cast, ('core', 'z', 'x'), split_axis=0, concat_axis=0, til...  11 us
    all_to_all x1, waiting for transfers between devices, local(): lax.all_to_all(packed, ('y', 'x'), split_axis=0, concat_axis=0, tiled=True)  8.78 us
    all_to_all x1, starting transfers between devices, local(): lax.all_to_all(packed, ('y', 'x'), split_axis=0, concat_axis=0, tiled=True)  7.17 us
    pallas_call x1, Pallas kernels, pack(): pl.pallas_call(pack_kernel, out_shape=(jax.ShapeDtypeStruct((MEMBERS * SL...  3.98 us
    ppermute x4, waiting for transfers between devices, swap(): return lax.ppermute(value, 'core', [(0, 1), (1, 0)])  2.37 us
    select_n x1, other arithmetic, local(): weights = jnp.where(own[0] == 1, weights, far)  1.64 us
  transfers between devices with their start and end apart: 5, of which 2 were waited for; matrix products, arithmetic and copies ran while one was open for 2% of the time, Pallas kernels for 0%

profile of v7, /device:TPU:0, one launch (start us, length us, event | category | flops | bytes accessed | tf_op | source)
XLA Modules:
  0.0 74.7 jit_solution(11217639439429228313)
XLA Ops:
  0.6 0.0 copy-start
  0.7 4.0 %pack.1 = (bf16[128,1536]{1,0:T(8,128)(2,1)}, bf16[3360,256]{1,0:T(8,128)(2,1)}) custom-call(s32[1]{0:T(128)} %bitcast.1.which_ref, bf16[32,1152]{1,0:T(8,128)(2,1)} %obs_hbm.1, bf16[32,384]{1,0:T(8,128)(2,1)} %roll_hbm.1, s32[24,32]{1,0:T(8,128)} %bitcast.17, s32[1,32]{1,0:T(1,128)} %bitcast.18, f32[2,48,256]{2,1,0:T(8,128)} %embed_hbm.1, ...), custom_call_target="tpu_custom_call" | custom-call | tf_op jit(solution)/shard_map/pack/pallas_call | solution.py:149
  4.7 0.1 collective-permute-start
  4.7 7.2 %all-to-all-start = ((bf16[16,8,1536]{2,1,0:T(8,128)(2,1)}), bf16[16,8,1536]{2,1,0:T(8,128)(2,1)S(1)}, u32[]{:S(2)}, u32[]{:S(2)}) async-start(bf16[16,8,1536]{2,1,0:T(8,128)(2,1)} %bitcast.15), calls=%async_computation | async-start | bytes 786432 | tf_op jit(solution)/shard_map/all_to_all | solution.py:498
  11.9 0.0 copy-done
  11.9 0.3 collective-permute-start.1
  12.2 0.0 collective-permute-done
  12.2 1.6 %broadcast_select_fusion.w_ref = bf16[3360,256]{1,0:T(8,128)(2,1)S(1)} fusion(bf16[3360,256]{1,0:T(8,128)(2,1)} %get-tuple-element.21, bf16[3360,256]{1,0:T(8,128)(2,1)} %collective-permute-done, pred[]{:T(512)S(6)} %eq.9), kind=kLoop, calls=%fused_computation | loop fusion | flops 860160 | bytes 5160961 | tf_op jit(solution)/shard_map/jit(_where)/select_n | solution.py:500
  13.9 0.0 collective-permute-done.1.other_ref
  13.9 8.8 %all-to-all-done = bf16[16,8,1536]{2,1,0:T(8,128)(2,1)S(1)} async-done(((bf16[16,8,1536]{2,1,0:T(8,128)(2,1)}), bf16[16,8,1536]{2,1,0:T(8,128)(2,1)S(1)}, u32[]{:S(2)}, u32[]{:S(2)}) %all-to-all-start) | async-done | bytes 393248 | tf_op jit(solution)/shard_map/all_to_all | solution.py:498
  22.7 16.1 %grad.1 = (bf16[16,104,256]{2,1,0:T(8,128)(2,1)S(1)}, bf16[16,104,256]{2,1,0:T(8,128)(2,1)S(1)}, f32[8,128]{1,0:T(8,128)S(1)}) custom-call(s32[1]{0:T(128)} %bitcast.1.which_ref, s32[1]{0:T(128)} %bitcast.2.own_ref, s32[1]{0:T(128)} %bitcast.core_ref, bf16[128,1536]{1,0:T(8,128)(2,1)S(1)} %bitcast.13, bf16[3360,256]{1,0:T(8,128)(2,1)S(1)} %broadcast_select_fusion.w_ref, ...), custom_call_target="tpu_custom_call" | custom-call | flops 11200000000 | bytes 4000000 | tf_op jit(solution)/shard_map/grad/pallas_call | solution.py:384
  38.7 0.1 collective-permute-start.2
  38.8 2.4 %collective-permute-done.2 = bf16[16,104,256]{2,1,0:T(8,128)(2,1)S(1)} collective-permute-done((bf16[16,104,256]{2,1,0:T(8,128)(2,1)S(1)}, bf16[16,104,256]{2,1,0:T(8,128)(2,1)S(1)}, u32[]{:S(2)}, u32[]{:S(2)}) %collective-permute-start.2) | collective-permute-done | bytes 852000 | tf_op jit(solution)/shard_map/ppermute | solution.py:487
  41.2 0.3 add_convert_fusion
  41.5 20.8 %all_to_all.27.recv_ref = bf16[16,104,256]{2,1,0:T(8,128)(2,1)S(1)} all-to-all(bf16[16,104,256]{2,1,0:T(8,128)(2,1)S(1)} %add_convert_fusion), channel_id=1, replica_groups=mesh['y'=4,'core'=2,'z'=4,'x'=4] {'z','x'}, dimensions={0} | all-to-all | bytes 1703936 | tf_op jit(solution)/shard_map/all_to_all | solution.py:503
  62.3 0.3 reduce.1
  62.6 0.1 collective-permute-start.3
  62.7 11.0 %all_to_all.28 = f32[32,8,128]{2,1,0:T(8,128)S(1)} all-to-all(f32[32,8,128]{2,1,0:T(8,128)S(1)} %bitcast.14), channel_id=1, replica_groups=mesh['y'=4,'core'=2,'z'=4,'x'=4] {'core','z','x'}, dimensions={0} | all-to-all | bytes 262144 | tf_op jit(solution)/shard_map/all_to_all | solution.py:505
  73.7 0.0 collective-permute-done.3.theirs_ref
  73.7 1.0 %finish.1 = (f32[3,2,256]{2,1,0:T(2,128)}, f32[2,3,2,16,256]{4,3,2,1,0:T(8,128)}, f32[2,16,512]{2,1,0:T(8,128)}, f32[2,32,512]{2,1,0:T(8,128)}, f32[13,2,32]{2,1,0:T(2,128)}, /*index=5*/f32[2,12]{1,0:T(2,128)}) custom-call(s32[1]{0:T(128)} %bitcast.core_ref, f32[2,104,256]{2,1,0:T(8,128)S(1)} %get-tuple-element.25.mine_ref, ...), custom_call_target="tpu_custom_call" | custom-call | tf_op jit(solution)/shard_map/finish/pallas_call | solution.py:476
Async XLA Ops:
  0.6 11.3 %copy-start = (f32[2,12]{1,0:T(2,128)S(1)}, f32[2,12]{1,0:T(2,128)}, u32[]{:S(2)}) copy-start(f32[2,12]{1,0:T(2,128)} %scale_ref.1) | copy-start | bytes 292
  4.7 7.6 %collective-permute-start = (bf16[3360,256]{1,0:T(8,128)(2,1)}, bf16[3360,256]{1,0:T(8,128)(2,1)}, u32[]{:S(2)}, u32[]{:S(2)}) collective-permute-start(bf16[3360,256]{1,0:T(8,128)(2,1)} %get-tuple-element.21), channel_id=1, source_target_pairs={{0,16},{16,0},{1,17},{17,1},{2,18},{18,2},{3,19},{19,3},{4,20},{20... | collective-permute-start | bytes 5160968 | tf_op jit(solution)/shard_map/ppermute | solution.py:487
  4.7 17.9 %all-to-all-start = ((bf16[16,8,1536]{2,1,0:T(8,128)(2,1)}), bf16[16,8,1536]{2,1,0:T(8,128)(2,1)S(1)}, u32[]{:S(2)}, u32[]{:S(2)}) async-start(bf16[16,8,1536]{2,1,0:T(8,128)(2,1)} %bitcast.15), calls=%async_computation | async-start | bytes 786432 | tf_op jit(solution)/shard_map/all_to_all | solution.py:498
  11.9 1.9 %collective-permute-start.1 = (f32[2,12]{1,0:T(2,128)S(1)}, f32[2,12]{1,0:T(2,128)S(1)}, u32[]{:S(2)}, u32[]{:S(2)}) collective-permute-start(f32[2,12]{1,0:T(2,128)S(1)} %copy-done), channel_id=1, source_target_pairs={{0,16},{16,0},{1,17},{17,1},{2,18},{18,2},{3,19},{19,3},{4,20},{20... | collective-permute-start | bytes 296 | tf_op jit(solution)/shard_map/ppermute | solution.py:487
  38.7 2.5 %collective-permute-start.2 = (bf16[16,104,256]{2,1,0:T(8,128)(2,1)S(1)}, bf16[16,104,256]{2,1,0:T(8,128)(2,1)S(1)}, u32[]{:S(2)}, u32[]{:S(2)}) collective-permute-start(bf16[16,104,256]{2,1,0:T(8,128)(2,1)S(1)} %get-tuple-element.23), channel_id=1, source_target_pairs={{0,16},{16,0},{1,17},{17,1},{2,18},{18,2},{3,19},{19,3},{4,20},{20... | collective-permute-start | bytes 2555912 | tf_op jit(solution)/shard_map/ppermute | solution.py:487
  62.6 11.1 %collective-permute-start.3 = (f32[2,104,256]{2,1,0:T(8,128)S(1)}, f32[2,104,256]{2,1,0:T(8,128)S(1)}, u32[]{:S(2)}, u32[]{:S(2)}) collective-permute-start(f32[2,104,256]{2,1,0:T(8,128)S(1)} %get-tuple-element.26), channel_id=1, source_target_pairs={{0,16},{16,0},{1,17},{17,1},{2,18},{18,2},{3,19},{19,3},{4,20},{20... | collective-permute-start | bytes 638984 | tf_op jit(solution)/shard_map/ppermute | solution.py:487
